TPU v7x, 128 devices: a whole 4x4x4 slice. The times are simulated.
128 devices in a mesh: zone: 4 (over y), blk: 32 (over z, x, core).
Axes of the slice: x: 4, y: 4, z: 4, core: 2. Of those that a mesh axis runs over, the one named last changes fastest.
Arguments:
- flow_state: float32 [4, 8192, 7, 256], P('zone', 'blk'), may hold values from -6 to 6
- right_side: float32 [4, 8192, 7, 256], P('zone', 'blk'), may hold values from -6 to 6
- inv_diag: float32 [4, 8192, 7, 7, 256], P('zone', 'blk'), may hold values from -0.2 to 1, as said below
- face_coef: float32 [4, 8192, 4, 256], P('zone', 'blk'), may hold values from 0.05 to 0.25
- face_jacobian: float32 [4, 7, 7], replicated, may hold values from -2 to 2
- hole_owner: int32 [16384, 1], P(('zone', 'blk')), may hold values from 0 to 127; in each aligned block of 128 rows (0 to 127, 128 to 255, ...) at most 2 rows name the same one
- source_row: int32 [16384], P(('zone', 'blk')), may hold values from 0 to 255
- target_row: int32 [16384], P(('zone', 'blk')), may hold values from 0 to 255
- block_device: int32 [128], replicated, may hold values from 0 to 127, each once
Outputs:
- relaxed: float32 [4, 8192, 7, 256], P('zone', 'blk')
Inputs may be any that keep to these rules, and one draw needn't show every extreme that they name: `hole_owner`: among the 128 holes of one device, no block is named more than 2 times, and some block exactly 2 times. `block_device`: each device index appears once. `inv_diag`: diagonal entries lie in 0.5 to 1.0, others in -0.2 to 0.2.
All inputs are finite; a program needn't handle non-finite values.
Results may differ from a plain program's by a relative error of at most 0.0001.
Values sent between devices are 32-bit elements; how exact they have to be, the bound alone decides.
No kernel may reach another device: no remote copies, remote signals or barrier semaphores. Data moves between devices by JAX's collectives and lax.ppermute only.
A program may use at most 128 MiB of HBM per device.

v0:
```python
import jax
import jax.numpy as jnp
from jax import lax
from jax.experimental import pallas as pl
from jax.experimental.pallas import tpu as pltpu
from jax.sharding import PartitionSpec as P

NV = 7
LANES = 128
COLS = 2 * LANES
AXES = ("zone", "blk")
F32 = jnp.float32
BF16 = jnp.bfloat16
I32 = jnp.int32
VMEM = pltpu.VMEM
SMEM = pl.BlockSpec(memory_space=pltpu.SMEM)
MIB = 1 << 20
RING = 4


def params(mib):
    return pltpu.CompilerParams(vmem_limit_bytes=mib * MIB)


def cost(flops, bytes_accessed):
    return pl.CostEstimate(flops=flops, bytes_accessed=bytes_accessed, transcendentals=0)


def whole(space=VMEM):
    return pl.BlockSpec(memory_space=space)


def tables_kernel(owner_in, device_in, source_in, target_in, sent, asking, rows, sems):
    n = owner_in.shape[1]
    copies = [
        pltpu.make_async_copy(ref, rows.at[i], sems.at[i])
        for i, ref in enumerate((owner_in, device_in, source_in, target_in))
    ]
    for copy in copies:
        copy.start()
    for copy in copies:
        copy.wait()
    owner, block_device, source_row, target_row = (rows[i].astype(F32) for i in range(4))
    lane = lax.broadcasted_iota(I32, (n, n), 1)
    sub = lax.broadcasted_iota(I32, (n, n), 0)
    eye = lane == sub

    def column(row):
        return jnp.sum(jnp.where(eye, row, 0.0), axis=1, keepdims=True)

    number = lane.astype(F32)
    owner_col = column(owner)
    target = jnp.sum(jnp.where(owner_col == number, block_device, 0.0), axis=1, keepdims=True)
    hot = target == number
    earlier = jnp.where(lane < sub, 1.0, 0.0).astype(BF16)
    prior = jnp.dot(earlier, jnp.where(hot, 1.0, 0.0).astype(BF16), preferred_element_type=F32)
    source_col = column(source_row + 1.0)
    target_col = column(target_row + 1.0)
    picked = jnp.zeros((n, n), F32)
    for k in range(2):
        mine = hot & ((prior > 0.5) if k else (prior < 0.5))
        sent[k : k + 1, :] = jnp.sum(jnp.where(mine, source_col, 0.0), axis=0, keepdims=True).astype(I32)
        asked = column(jnp.sum(jnp.where(mine, target_col, 0.0), axis=0, keepdims=True))
        picked = jnp.where(lane == k, asked, picked)
    asking[...] = picked.astype(I32).reshape(asking.shape)


def slot_tables(owner, block_device, source_row, target_row):
    n = owner.shape[1]
    return pl.pallas_call(
        tables_kernel,
        in_specs=[whole(pltpu.HBM)] * 4,
        out_specs=[whole()] * 2,
        out_shape=[jax.ShapeDtypeStruct((2, n), I32), jax.ShapeDtypeStruct((n, 1, LANES), I32)],
        scratch_shapes=[VMEM((4, 1, n), I32), pltpu.SemaphoreType.DMA((4,))],
        compiler_params=params(60),
        cost_estimate=cost(4_000_000, 100_000),
        name="slot_tables",
    )(owner, block_device, source_row, target_row)


def table_copies(sent_in, asked_in, sent, asked, sems):
    return [
        pltpu.make_async_copy(sent_in, sent, sems.at[0]),
        pltpu.make_async_copy(asked_in, asked, sems.at[1]),
    ]


def table_scratch(devices):
    return [
        pltpu.SMEM((2, devices), I32),
        pltpu.SMEM((devices, 1, LANES), I32),
        pltpu.SemaphoreType.DMA((2,)),
    ]


def gather_kernel(sent_in, asked_in, flow_in, message, asked_out, sent, asked, sems, flow, more):
    count = message.shape[0]
    base = pl.program_id(0) * count

    @pl.when(pl.program_id(0) == 0)
    def _():
        copies = table_copies(sent_in, asked_in, sent, asked, sems) + [
            pltpu.make_async_copy(flow_in, flow, more.at[0]),
            pltpu.make_async_copy(asked_in, asked_out, more.at[1]),
        ]
        for copy in copies:
            copy.start()
        for copy in copies:
            copy.wait()

    def step(d, carry):
        for part in range(2):
            for k in range(2):
                slot = asked[base + d, 0, k] if part else sent[k, base + d]
                row = jnp.maximum(slot - 1, 0)
                for h in range(2):
                    start = 28 * part + 14 * k + NV * h
                    message[d, start : start + NV, :] = flow[row, :, LANES * h : LANES * (h + 1)]
        return carry

    lax.fori_loop(0, count, step, 0, unroll=2)


def gather(sent, asked, flow):
    devices = asked.shape[0]
    return pl.pallas_call(
        gather_kernel,
        grid=(8,),
        in_specs=[whole(pltpu.HBM), whole(), whole(pltpu.HBM)],
        out_specs=[pl.BlockSpec((devices // 8, 8 * NV, LANES), lambda g: (g, 0, 0)), whole(pltpu.HBM)],
        out_shape=[
            jax.ShapeDtypeStruct((devices, 8 * NV, LANES), F32),
            jax.ShapeDtypeStruct(asked.shape, I32),
        ],
        scratch_shapes=table_scratch(devices) + [VMEM(flow.shape, F32), pltpu.SemaphoreType.DMA((2,))],
        compiler_params=params(58),
        cost_estimate=cost(1_000_000, 6_000_000),
        name="gather",
    )(sent, asked, flow)


def coupled(state, row, coef, mix):
    lane = lax.broadcasted_iota(I32, (8, LANES), 1)
    parts = []
    for direction in range(4):
        factor = coef(direction)
        for v in range(NV):
            if direction < 2:
                first = row + 2 * direction - 1
                pair = [state[2 * v + h, pl.ds(first, 8), :] for h in range(2)]
            else:
                mid = [state[2 * v + h, pl.ds(row, 8), :] for h in range(2)]
                if direction == 2:
                    left, right = (pltpu.roll(m, 1, 1) for m in mid)
                    pair = [jnp.where(lane == 0, 0.0, left), jnp.where(lane == 0, left, right)]
                else:
                    left, right = (pltpu.roll(m, LANES - 1, 1) for m in mid)
                    pair = [jnp.where(lane == LANES - 1, right, left), jnp.where(lane == LANES - 1, 0.0, right)]
            parts.append(factor * jnp.concatenate(pair, axis=1))
    cells = jnp.concatenate(parts, axis=0)
    high = cells.astype(BF16)
    low = (cells - high.astype(F32)).astype(BF16)
    dot = lambda a, b: jnp.dot(a, b, preferred_element_type=F32)
    return dot(mix[0], high) + dot(mix[1], high) + dot(mix[0], low)


def apply_inv(inv, cells):
    out = []
    for i in range(NV):
        total = None
        for j in range(NV):
            term = inv(i, j) * cells[j]
            total = term if j == 0 else total + term
        out.append(total)
    return out


def first_kernel(parity, flow, right, coef, mix, halo_a, halo_b, inv, start, start_edges, inv_edges, state, sems):
    tiles = right.shape[1] // 8
    copies = [
        pltpu.make_async_copy(inv.at[:, :, 8 * t : 8 * t + 8, :], inv_edges.at[g], sems.at[g])
        for g, t in enumerate((0, tiles - 1))
    ]
    for copy in copies:
        copy.start()
    even = parity[0] == 0
    for n in range(2 * NV):
        v, h = divmod(n, 2)
        a, b = halo_a[n : n + 1, :], halo_b[n : n + 1, :]
        state[n, 7:8, :] = jnp.where(even, b, a)
        state[n, 8 + 8 * tiles : 9 + 8 * tiles, :] = jnp.where(even, a, b)
        state[n, 8 : 8 + 8 * tiles, :] = flow[v, :, LANES * h : LANES * (h + 1)]

    def step(t, carry):
        row = pl.multiple_of(8 * t, 8)
        sums = coupled(state, row + 8, lambda d: coef[d, pl.ds(row, 8), :], mix)
        for v in range(NV):
            start[v, pl.ds(row, 8), :] = right[v, pl.ds(row, 8), :] - sums[8 * v : 8 * v + 8, :]
        return carry

    lax.fori_loop(0, tiles, step, 0)
    start_edges[0] = start[:, 0:8, :]
    start_edges[1] = start[:, 8 * tiles - 8 : 8 * tiles, :]
    for copy in copies:
        copy.wait()


def first_sum(parity, flow, right, coef, mix, halo_a, halo_b, inv):
    rows = flow.shape[1]
    shapes = (flow.shape, (2, NV, 8, COLS), (2, NV, NV, 8, COLS))
    return pl.pallas_call(
        first_kernel,
        in_specs=[SMEM] + [whole()] * 6 + [whole(pltpu.HBM)],
        out_specs=[whole()] * 3,
        out_shape=[jax.ShapeDtypeStruct(s, F32) for s in shapes],
        scratch_shapes=[VMEM((2 * NV, rows + 16, LANES), F32), pltpu.SemaphoreType.DMA((2,))],
        compiler_params=params(52),
        cost_estimate=cost(30_000_000, 8_000_000),
        name="first_sum",
    )(parity, flow, right, coef, mix, halo_a, halo_b, inv)


def scatter_kernel(
    parity, sent_in, asked_in, message, start_edges, inv_edges, source, edge_a, edge_b, sent, asked, sems
):
    groups = source.shape[1] // 8
    count = message.shape[0]
    base = pl.program_id(0) * count

    @pl.when(pl.program_id(0) == 0)
    def _():
        copies = table_copies(sent_in, asked_in, sent, asked, sems)
        for copy in copies:
            copy.start()

        def clear(g, carry):
            for h in range(2):
                source[h, pl.ds(pl.multiple_of(64 * g, 64), 64), :] = jnp.zeros((64, LANES), F32)
            return carry

        lax.fori_loop(0, groups // 8, clear, 0)
        for copy in copies:
            copy.wait()

    def step(d, carry):
        for part in range(2):
            for k in range(2):
                slot = sent[k, base + d] if part else asked[base + d, 0, k]
                row = pl.multiple_of(8 * slot, 8)
                for h in range(2):
                    start = 28 * part + 14 * k + NV * h
                    value = message[d, start : start + NV, :]
                    old = source[h, pl.ds(row, NV), :]
                    source[h, pl.ds(row, NV), :] = old - value if part else old + value
        return carry

    lax.fori_loop(0, count, step, 0, unroll=2)

    @pl.when(pl.program_id(0) == pl.num_programs(0) - 1)
    def _():
        even = parity[0] == 0
        edges = []
        for g, (tile, sub) in enumerate(((0, 0), (groups // 8 - 2, 7))):
            cells = [start_edges[g, v] + added(source, tile, v) for v in range(NV)]
            relaxed = apply_inv(lambda i, j, g=g: inv_edges[g, i, j], cells)
            edges.append([r[sub : sub + 1, :] for r in relaxed])
        for v in range(NV):
            top, bottom = edges[0][v], edges[1][v]
            out_a, out_b = jnp.where(even, bottom, top), jnp.where(even, top, bottom)
            for h in range(2):
                n = 2 * v + h
                edge_a[n : n + 1, :] = out_a[:, LANES * h : LANES * (h + 1)]
                edge_b[n : n + 1, :] = out_b[:, LANES * h : LANES * (h + 1)]


def added(source, tile, v):
    return jnp.concatenate([source[h, pl.ds(64 * tile + 8 + v, 8, stride=8), :] for h in range(2)], axis=1)


def scatter(parity, sent, asked, message, start_edges, inv_edges, rows):
    devices = message.shape[0]
    steps = 8
    sources = (2, 8 * (rows + 8), LANES)
    edge = (2 * NV, LANES)
    return pl.pallas_call(
        scatter_kernel,
        grid=(steps,),
        in_specs=[
            SMEM,
            whole(pltpu.HBM),
            whole(pltpu.HBM),
            pl.BlockSpec((devices // steps,) + message.shape[1:], lambda g: (g, 0, 0)),
            whole(),
            whole(),
        ],
        out_specs=[whole()] * 3,
        out_shape=[jax.ShapeDtypeStruct(s, F32) for s in (sources, edge, edge)],
        scratch_shapes=table_scratch(devices),
        compiler_params=params(16),
        cost_estimate=cost(2_000_000, 7_000_000),
        name="scatter",
    )(parity, sent, asked, message, start_edges, inv_edges)


def sweeps_kernel(
    source, mix, start_in, right_in, coef_in, inv_in, out, state, done, start, right, coef, inv, sems, out_sems
):
    tiles = start_in.shape[1] // 8
    chunk = 4

    def fetch(t):
        slot = lax.rem(t, RING)
        rows = pl.ds(pl.multiple_of(8 * t, 8), 8)
        streams = ((start_in, start), (right_in, right), (coef_in, coef))
        copies = [
            pltpu.make_async_copy(ref.at[:, rows, :], part.at[slot], sems.at[n, slot])
            for n, (ref, part) in enumerate(streams)
        ]
        return copies + [pltpu.make_async_copy(inv_in.at[:, :, rows, :], inv.at[slot], sems.at[3, slot])]

    def begin(copies):
        for copy in copies:
            copy.start()

    def finish(copies):
        for copy in copies:
            copy.wait()

    def store(c):
        rows = pl.ds(pl.multiple_of(8 * chunk * c, 8), 8 * chunk)
        return pltpu.make_async_copy(done.at[:, rows, :], out.at[:, rows, :], out_sems.at[c])

    for t in range(RING):
        begin(fetch(t))
    for n in range(2 * NV):
        state[n, 0:8, :] = jnp.zeros((8, LANES), F32)
        state[n, 8 + 8 * tiles : 16 + 8 * tiles, :] = jnp.zeros((8, LANES), F32)

    def sweep_one(t):
        slot = lax.rem(t, RING)
        row = pl.multiple_of(8 * t, 8)
        cells = [start[slot, v] + added(source, t, v) for v in range(NV)]
        relaxed = apply_inv(lambda i, j: inv[slot, i, j], cells)
        for v in range(NV):
            for h in range(2):
                state[2 * v + h, pl.ds(row + 8, 8), :] = relaxed[v][:, LANES * h : LANES * (h + 1)]

    def sweep_two(t):
        slot = lax.rem(t, RING)
        row = pl.multiple_of(8 * t, 8)
        sums = coupled(state, row + 8, lambda d: coef[slot, d], mix)
        cells = [right[slot, v] + added(source, t, v) - sums[8 * v : 8 * v + 8, :] for v in range(NV)]
        relaxed = apply_inv(lambda i, j: inv[slot, i, j], cells)
        for v in range(NV):
            done[v, pl.ds(row, 8), :] = relaxed[v]

    finish(fetch(0))
    sweep_one(0)

    def step(t, carry):
        finish(fetch(t))
        sweep_one(t)
        sweep_two(t - 1)

        @pl.when(t + RING - 1 < tiles)
        def _():
            begin(fetch(t + RING - 1))

        @pl.when(lax.rem(t, chunk) == 0)
        def _():
            store(t // chunk - 1).start()

        return carry

    lax.fori_loop(1, tiles, step, 0)
    sweep_two(tiles - 1)
    store(tiles // chunk - 1).start()
    for c in range(tiles // chunk):
        store(c).wait()


def sweeps(source, mix, start, right, coef, inv):
    rows = start.shape[1]
    return pl.pallas_call(
        sweeps_kernel,
        in_specs=[whole()] * 2 + [whole(pltpu.HBM)] * 4,
        out_specs=whole(pltpu.HBM),
        out_shape=jax.ShapeDtypeStruct(start.shape, F32),
        scratch_shapes=[
            VMEM((2 * NV, rows + 16, LANES), F32),
            VMEM(start.shape, F32),
            VMEM((RING, NV, 8, COLS), F32),
            VMEM((RING, NV, 8, COLS), F32),
            VMEM((RING, 4, 8, COLS), F32),
            VMEM((RING, NV, NV, 8, COLS), F32),
            pltpu.SemaphoreType.DMA((4, RING)),
            pltpu.SemaphoreType.DMA((rows // 32,)),
        ],
        compiler_params=params(40),
        cost_estimate=cost(45_000_000, 24_000_000),
        name="sweeps",
    )(source, mix, start, right, coef, inv)


def edge_kernel(parity, relaxed, coef, mix, inv, halo_a, halo_b, out):
    low = pl.program_id(0) == 0
    use_a = (parity[0] == 0) != low
    place = lax.broadcasted_iota(I32, (8, COLS), 0) == jnp.where(low, 0, 7)
    factor = jnp.where(low, coef[0], coef[1])
    parts = []
    for v in range(NV):
        rows = [jnp.where(use_a, halo_a[n : n + 1, :], halo_b[n : n + 1, :]) for n in (2 * v, 2 * v + 1)]
        row = jnp.broadcast_to(jnp.concatenate(rows, axis=1), (8, COLS))
        parts.append(jnp.where(place, factor * row, 0.0))
    cells = jnp.concatenate(parts, axis=0)
    zero = jnp.zeros_like(cells)
    cells = jnp.concatenate([jnp.where(low, cells, zero), jnp.where(low, zero, cells), zero, zero], axis=0)
    high = cells.astype(BF16)
    rest = (cells - high.astype(F32)).astype(BF16)
    dot = lambda a, b: jnp.dot(a, b, preferred_element_type=F32)
    sums = dot(mix[0], high) + dot(mix[1], high) + dot(mix[0], rest)
    change = apply_inv(lambda i, j: inv[i, j], [sums[8 * v : 8 * v + 8, :] for v in range(NV)])
    for v in range(NV):
        out[v] = relaxed[v] - change[v]


def edge_rows(parity, relaxed, coef, mix, inv, halo_a, halo_b):
    last = relaxed.shape[1] // 8 - 1
    slab = pl.BlockSpec((NV, 8, COLS), lambda g: (0, g * last, 0))
    return pl.pallas_call(
        edge_kernel,
        grid=(2,),
        in_specs=[
            SMEM,
            slab,
            pl.BlockSpec((4, 8, COLS), lambda g: (0, g * last, 0)),
            pl.BlockSpec(mix.shape, lambda g: (0, 0, 0)),
            pl.BlockSpec((None, NV, NV, 8, COLS), lambda g: (g, 0, 0, 0, 0)),
            pl.BlockSpec((2 * NV, LANES), lambda g: (0, 0)),
            pl.BlockSpec((2 * NV, LANES), lambda g: (0, 0)),
        ],
        out_specs=slab,
        out_shape=jax.ShapeDtypeStruct(relaxed.shape, F32),
        input_output_aliases={1: 0},
        compiler_params=params(40),
        cost_estimate=cost(100_000, 900_000),
        name="edge_rows",
    )(parity, relaxed, coef, mix, inv, halo_a, halo_b)


def exchange(edge_a, edge_b):
    size = lax.axis_size("blk")
    pairs_a = [(i, i ^ 1) for i in range(size)]
    pairs_b = [(i, i - 1 if i % 2 == 0 else i + 1) for i in range(1, size - 1)]
    return lax.ppermute(edge_a, "blk", pairs_a), lax.ppermute(edge_b, "blk", pairs_b)


def mixing(face_jacobian):
    wide = jnp.transpose(face_jacobian, (1, 0, 2)).reshape(NV, 4 * NV)
    full = (wide[:, None, :, None] * jnp.eye(8, dtype=F32)[None, :, None, :]).reshape(8 * NV, 32 * NV)
    high = lax.reduce_precision(full, exponent_bits=8, mantissa_bits=7)
    return jnp.stack([high.astype(BF16), (full - high).astype(BF16)])


def body(flow_state, right_side, inv_diag, face_coef, face_jacobian, hole_owner, source_row, target_row, block_device):
    flow = jnp.transpose(flow_state[0], (1, 0, 2))
    right = jnp.transpose(right_side[0], (1, 0, 2))
    inv = jnp.transpose(inv_diag[0], (1, 2, 0, 3))
    rows = flow.shape[1]
    parity = (lax.axis_index("blk") % 2).astype(I32).reshape(1)
    as_row = lambda a: a.reshape(1, -1)
    sent, asking = slot_tables(as_row(hole_owner), as_row(block_device), as_row(source_row), as_row(target_row))
    asked = lax.all_to_all(asking, AXES, split_axis=0, concat_axis=0, tiled=True)
    message, asked = gather(sent, asked, flow_state[0])
    message = lax.all_to_all(message, AXES, split_axis=0, concat_axis=0, tiled=True)

    coef = jnp.transpose(face_coef[0], (1, 0, 2))
    mix = mixing(face_jacobian)
    top, bottom = flow[:, 0].reshape(2 * NV, LANES), flow[:, rows - 1].reshape(2 * NV, LANES)
    even = parity[0] == 0
    halo_a, halo_b = exchange(jnp.where(even, bottom, top), jnp.where(even, top, bottom))
    start, start_edges, inv_edges = first_sum(parity, flow, right, coef, mix, halo_a, halo_b, inv)

    source, edge_a, edge_b = scatter(parity, sent, asked, message, start_edges, inv_edges, rows)
    halo_a, halo_b = exchange(edge_a, edge_b)
    relaxed = sweeps(source, mix, start, right, coef, inv)
    relaxed = edge_rows(parity, relaxed, coef, mix, inv_edges, halo_a, halo_b)
    return jnp.transpose(relaxed, (1, 0, 2))[None]


def solution(mesh):
    placed = (
        P("zone", "blk", None, None),
        P("zone", "blk", None, None),
        P("zone", "blk", None, None, None),
        P("zone", "blk", None, None),
        P(),
        P(("zone", "blk"), None),
        P(("zone", "blk")),
        P(("zone", "blk")),
        P(),
    )
    return jax.shard_map(
        body, mesh=mesh, in_specs=placed, out_specs=P("zone", "blk", None, None), check_vma=False
    )
```

profile of v0, /device:TPU:1, one launch (start us, length us, event | category | flops | bytes accessed | tf_op | source)
XLA Modules:
  0.0 119.3 jit_solution(8243612316641785407)
XLA Ops:
  0.0 1.8 %slot_tables.1 = (s32[2,128]{1,0:T(2,128)}, s32[128,1,128]{2,1,0:T(1,128)}) custom-call(s32[1,128]{1,0:T(1,128)} %bitcast.34, s32[1,128]{1,0:T(1,128)} %bitcast.35, s32[1,128]{1,0:T(1,128)} %bitcast.36, s32[1,128]{1,0:T(1,128)} %bitcast.37), custom_call_target="tpu_custom_call" | custom-call | flops 4000000 | bytes 100000 | tf_op jit(solution)/shard_map/slot_tables/pallas_call | solution.py:70
  1.8 11.5 %all-to-all-start = ((s32[128,1,128]{2,1,0:T(1,128)}), s32[128,1,128]{2,1,0:T(1,128)S(1)}, u32[]{:S(2)}, u32[]{:S(2)}) async-start(s32[128,1,128]{2,1,0:T(1,128)} %get-tuple-element.16), calls=%async_computation | async-start | bytes 131072 | tf_op jit(solution)/shard_map/all_to_all | solution.py:474
  13.3 3.9 %copy.13.flow_in = f32[256,7,256]{2,1,0:T(8,128)} copy(f32[256,7,256]{2,0,1:T(8,128)} %bitcast.30) | data formatting | bytes 3670016 | tf_op jit(solution)/shard_map/squeeze | solution.py:475
  17.2 5.5 %all-to-all-done.asked_in = s32[128,1,128]{2,1,0:T(1,128)S(1)} async-done(((s32[128,1,128]{2,1,0:T(1,128)}), s32[128,1,128]{2,1,0:T(1,128)S(1)}, u32[]{:S(2)}, u32[]{:S(2)}) %all-to-all-start) | async-done | bytes 65568 | tf_op jit(solution)/shard_map/all_to_all | solution.py:474
  22.8 0.6 copy-done.6
  23.4 6.5 %gather.1 = (f32[128,56,128]{2,1,0:T(8,128)}, s32[128,1,128]{2,1,0:T(1,128)}) custom-call(s32[2,128]{1,0:T(2,128)} %get-tuple-element.15.sent_in, s32[128,1,128]{2,1,0:T(1,128)} %copy-done.6, f32[256,7,256]{2,1,0:T(8,128)} %copy.13.flow_in), custom_call_target="tpu_custom_call" | custom-call | flops 1000000 | bytes 6000000 | tf_op jit(solution)/shard_map/gather/pallas_call | solution.py:127
  29.9 5.4 %all-to-all-start.1 = ((f32[128,56,128]{2,1,0:T(8,128)}), f32[128,56,128]{2,1,0:T(8,128)}, u32[]{:S(2)}, u32[]{:S(2)}) async-start(f32[128,56,128]{2,1,0:T(8,128)} %get-tuple-element.18), calls=%async_computation.1 | async-start | bytes 7340032 | tf_op jit(solution)/shard_map/all_to_all | solution.py:476
  35.3 1.0 fusion.2
  36.3 1.4 %collective-permute-start = (f32[14,128]{1,0:T(8,128)S(1)}, f32[14,128]{1,0:T(8,128)S(1)}, u32[]{:S(2)}, u32[]{:S(2)}) collective-permute-start(f32[14,128]{1,0:T(8,128)S(1)} %select_n.28), channel_id=1, source_target_pairs={{0,1},{1,0},{2,3},{3,2},{4,5},{5,4},{6,7},{7,6},{8,9},{9,8},{10,11... | collective-permute-start | bytes 21512 | tf_op jit(solution)/shard_map/ppermute | solution.py:456
  37.7 2.4 %collective-permute-start.1 = (f32[14,128]{1,0:T(8,128)S(1)}, f32[14,128]{1,0:T(8,128)S(1)}, u32[]{:S(2)}, u32[]{:S(2)}) collective-permute-start(f32[14,128]{1,0:T(8,128)S(1)} %select_n.30), channel_id=1, source_target_pairs={{1,2},{2,1},{3,4},{4,3},{5,6},{6,5},{7,8},{8,7},{9,10},{10,9},{11,... | collective-permute-start | bytes 21512 | tf_op jit(solution)/shard_map/ppermute | solution.py:456
  40.1 0.1 mul.30
  40.2 0.2 broadcast_multiply_fusion
  40.4 0.4 mul.34
  40.8 1.2 %copy.16 = f32[1,256,4,256]{3,1,2,0:T(8,128)} copy(f32[1,256,4,256]{3,2,1,0:T(4,128)S(1)} %copy-done.5) | data formatting | bytes 2097152 | tf_op args[3]
  42.1 34.3 %collective-permute-done.1.halo_b = f32[14,128]{1,0:T(8,128)S(1)} collective-permute-done((f32[14,128]{1,0:T(8,128)S(1)}, f32[14,128]{1,0:T(8,128)S(1)}, u32[]{:S(2)}, u32[]{:S(2)}) %collective-permute-start.1) | collective-permute-done | bytes 7200 | tf_op jit(solution)/shard_map/ppermute | solution.py:456
  76.4 12.2 %first_sum.1 = (f32[7,256,256]{2,1,0:T(8,128)}, f32[2,7,8,256]{3,2,1,0:T(8,128)S(1)}, f32[2,7,7,8,256]{4,3,2,1,0:T(8,128)S(1)}) custom-call(s32[1]{0:T(128)} %bitcast.parity, f32[7,256,256]{2,1,0:T(8,128)} %bitcast.32, f32[7,256,256]{2,1,0:T(8,128)} %bitcast.26, f32[4,256,256]{2,1,0:T(8,128)} %bitcast.23, bf16[2,56,224]{2,1,0:T(8,128)(2,1)S(1)} %pad_maximum_fusion.mix, ...), custom_call_target="tpu_custom_call" | custom-call | flops 30000000 | bytes 8000000 | tf_op jit(solution)/shard_map/first_sum/pallas_call | solution.py:212
  88.6 0.0 copy-start.1
  88.6 7.6 %scatter.1 = (f32[2,2112,128]{2,1,0:T(8,128)S(1)}, f32[14,128]{1,0:T(8,128)S(1)}, f32[14,128]{1,0:T(8,128)S(1)}) custom-call(s32[1]{0:T(128)} %bitcast.parity, s32[2,128]{1,0:T(2,128)S(1)} %copy-done.4, s32[128,1,128]{2,1,0:T(1,128)S(1)} %copy-done.3, f32[128,56,128]{2,1,0:T(8,128)} %all-to-all-done.1.message, ...), custom_call_target="tpu_custom_call" | custom-call | flops 2000000 | bytes 7000000 | tf_op jit(solution)/shard_map/scatter/pallas_call | solution.py:286
  96.3 0.1 collective-permute-start.2
  96.3 2.6 %collective-permute-start.3 = (f32[14,128]{1,0:T(8,128)S(1)}, f32[14,128]{1,0:T(8,128)S(1)}, u32[]{:S(2)}, u32[]{:S(2)}) collective-permute-start(f32[14,128]{1,0:T(8,128)S(1)} %get-tuple-element.24), channel_id=1, source_target_pairs={{1,2},{2,1},{3,4},{4,3},{5,6},{6,5},{7,8},{8,7},{9,10},{10,9},{11,... | collective-permute-start | bytes 21512 | tf_op jit(solution)/shard_map/ppermute | solution.py:456
  98.9 0.0 copy-start.2
  98.9 1.5 %copy-done.2 = f32[7,256,256]{2,1,0:T(8,128)S(1)} copy-done((f32[7,256,256]{2,1,0:T(8,128)S(1)}, f32[7,256,256]{2,1,0:T(8,128)}, u32[]{:S(2)}) %copy-start.2) | copy-done | bytes 1835032
  100.4 16.9 %sweeps.1.relaxed = f32[7,256,256]{2,1,0:T(8,128)} custom-call(f32[2,2112,128]{2,1,0:T(8,128)S(1)} %get-tuple-element.21.source, bf16[2,56,224]{2,1,0:T(8,128)(2,1)S(1)} %pad_maximum_fusion.mix, f32[7,256,256]{2,1,0:T(8,128)S(1)} %copy-done.2, f32[7,256,256]{2,1,0:T(8,128)S(1)} %bitcast.27, f32[4,256,256]{2,1,0:T(8,128)S(1)} %bitcast.24, ...), custom_call_target="tpu_custom_call" | custom-call | flops 45000000 | bytes 24000000 | tf_op jit(solution)/shard_map/sweeps/pallas_call | solution.py:385
  117.4 1.9 %edge_rows.1 = f32[7,256,256]{2,1,0:T(8,128)} custom-call(s32[1]{0:T(128)} %bitcast.parity, f32[7,256,256]{2,1,0:T(8,128)} %sweeps.1.relaxed, f32[4,256,256]{2,1,0:T(8,128)S(1)} %bitcast.25, bf16[2,56,224]{2,1,0:T(8,128)(2,1)S(1)} %pad_maximum_fusion.mix, f32[2,7,7,8,256]{4,3,2,1,0:T(8,128)S(1)} %get-tuple-element.20.inv_edges.inv, ...), custom_call_target="tpu_custom_call", output_to_operand_aliasing={{}: (1, {})} | custom-call | flops 100000 | bytes 900000 | tf_op jit(solution)/shard_map/edge_rows/pallas_call | solution.py:431
  (21 shorter events, 0.1 us)
Async XLA Ops:
  1.8 20.9 %all-to-all-start = ((s32[128,1,128]{2,1,0:T(1,128)}), s32[128,1,128]{2,1,0:T(1,128)S(1)}, u32[]{:S(2)}, u32[]{:S(2)}) async-start(s32[128,1,128]{2,1,0:T(1,128)} %get-tuple-element.16), calls=%async_computation | async-start | bytes 131072 | tf_op jit(solution)/shard_map/all_to_all | solution.py:474
  22.8 0.6 copy-start.6
  29.9 10.2 %copy-start.7 = (f32[4,7,7]{2,0,1:T(4,128)S(1)}, f32[4,7,7]{2,0,1:T(4,128)}, u32[]{:S(2)}) copy-start(f32[4,7,7]{2,0,1:T(4,128)} %param.13) | copy-start | bytes 2356
  29.9 58.6 %all-to-all-start.1 = ((f32[128,56,128]{2,1,0:T(8,128)}), f32[128,56,128]{2,1,0:T(8,128)}, u32[]{:S(2)}, u32[]{:S(2)}) async-start(f32[128,56,128]{2,1,0:T(8,128)} %get-tuple-element.18), calls=%async_computation.1 | async-start | bytes 7340032 | tf_op jit(solution)/shard_map/all_to_all | solution.py:476
  35.3 5.5 %copy-start.5 = (f32[1,256,4,256]{3,2,1,0:T(4,128)S(1)}, f32[1,256,4,256]{3,2,1,0:T(4,128)}, u32[]{:S(2)}) copy-start(f32[1,256,4,256]{3,2,1,0:T(4,128)} %param.12) | copy-start | bytes 3145732
  36.3 5.7 %collective-permute-start = (f32[14,128]{1,0:T(8,128)S(1)}, f32[14,128]{1,0:T(8,128)S(1)}, u32[]{:S(2)}, u32[]{:S(2)}) collective-permute-start(f32[14,128]{1,0:T(8,128)S(1)} %select_n.28), channel_id=1, source_target_pairs={{0,1},{1,0},{2,3},{3,2},{4,5},{5,4},{6,7},{7,6},{8,9},{9,8},{10,11... | collective-permute-start | bytes 21512 | tf_op jit(solution)/shard_map/ppermute | solution.py:456
  37.7 38.7 %collective-permute-start.1 = (f32[14,128]{1,0:T(8,128)S(1)}, f32[14,128]{1,0:T(8,128)S(1)}, u32[]{:S(2)}, u32[]{:S(2)}) collective-permute-start(f32[14,128]{1,0:T(8,128)S(1)} %select_n.30), channel_id=1, source_target_pairs={{1,2},{2,1},{3,4},{4,3},{5,6},{6,5},{7,8},{8,7},{9,10},{10,9},{11,... | collective-permute-start | bytes 21512 | tf_op jit(solution)/shard_map/ppermute | solution.py:456
  76.4 12.2 %copy-start.3 = (s32[128,1,128]{2,1,0:T(1,128)S(1)}, s32[128,1,128]{2,1,0:T(1,128)}, u32[]{:S(2)}) copy-start(s32[128,1,128]{2,1,0:T(1,128)} %get-tuple-element.17.asked_in) | copy-start | bytes 196612
  76.4 12.2 %copy-start.4 = (s32[2,128]{1,0:T(2,128)S(1)}, s32[2,128]{1,0:T(2,128)}, u32[]{:S(2)}) copy-start(s32[2,128]{1,0:T(2,128)} %get-tuple-element.15.sent_in) | copy-start | bytes 3076
  88.6 10.3 %copy-start = (f32[1,256,4,256]{3,1,2,0:T(8,128)S(1)}, f32[1,256,4,256]{3,1,2,0:T(8,128)}, u32[]{:S(2)}) copy-start(f32[1,256,4,256]{3,1,2,0:T(8,128)} %copy.16) | copy-start | bytes 3145732
  88.6 10.3 %copy-start.1 = (f32[1,256,7,256]{3,1,2,0:T(8,128)S(1)}, f32[1,256,7,256]{3,1,2,0:T(8,128)}, u32[]{:S(2)}) copy-start(f32[1,256,7,256]{3,1,2,0:T(8,128)} %param.10) | copy-start | bytes 5505028
  96.3 21.1 %collective-permute-start.2 = (f32[14,128]{1,0:T(8,128)S(1)}, f32[14,128]{1,0:T(8,128)S(1)}, u32[]{:S(2)}, u32[]{:S(2)}) collective-permute-start(f32[14,128]{1,0:T(8,128)S(1)} %get-tuple-element.23), channel_id=1, source_target_pairs={{0,1},{1,0},{2,3},{3,2},{4,5},{5,4},{6,7},{7,6},{8,9},{9,8},{10,11... | collective-permute-start | bytes 21512 | tf_op jit(solution)/shard_map/ppermute | solution.py:456
  96.3 21.0 %collective-permute-start.3 = (f32[14,128]{1,0:T(8,128)S(1)}, f32[14,128]{1,0:T(8,128)S(1)}, u32[]{:S(2)}, u32[]{:S(2)}) collective-permute-start(f32[14,128]{1,0:T(8,128)S(1)} %get-tuple-element.24), channel_id=1, source_target_pairs={{1,2},{2,1},{3,4},{4,3},{5,6},{6,5},{7,8},{8,7},{9,10},{10,9},{11,... | collective-permute-start | bytes 21512 | tf_op jit(solution)/shard_map/ppermute | solution.py:456
  98.9 1.5 %copy-start.2 = (f32[7,256,256]{2,1,0:T(8,128)S(1)}, f32[7,256,256]{2,1,0:T(8,128)}, u32[]{:S(2)}) copy-start(f32[7,256,256]{2,1,0:T(8,128)} %get-tuple-element.22.start_in) | copy-start | bytes 5505028
where the time goes:
time: 121 us; the launch traced here: 119 us
  Pallas kernels  47 us (39%)
  waiting for transfers between devices  39.9 us (33%)
  starting transfers between devices  23.2 us (19%)
  local copies, waits for them, and re-layouts  7.81 us (6%)
    ppermute x2, waiting for transfers between devices, exchange(): lax.ppermute(edge_b, 'blk', pairs_b)  34.3 us
    pallas_call x1, Pallas kernels, sweeps(): pl.pallas_call(sweeps_kernel, in_specs=[whole()] * 2 + [whole(pltpu.HBM)]...  16.9 us
    pallas_call x1, Pallas kernels, first_sum(): pl.pallas_call(first_kernel, in_specs=[SMEM] + [whole()] * 6 + [whole(plt...  12.2 us
    all_to_all x1, starting transfers between devices, body(): lax.all_to_all(asking, AXES, split_axis=0, concat_axis=0, tiled=True)  11.5 us
    pallas_call x1, Pallas kernels, scatter(): pl.pallas_call(scatter_kernel, grid=(steps,), in_specs=[SMEM, whole(pltpu...  7.61 us
    pallas_call x1, Pallas kernels, gather(): pl.pallas_call(gather_kernel, grid=(8,), in_specs=[whole(pltpu.HBM), whol...  6.52 us
    all_to_all x1, waiting for transfers between devices, body(): lax.all_to_all(asking, AXES, split_axis=0, concat_axis=0, tiled=True)  5.54 us
    all_to_all x1, starting transfers between devices, body(): lax.all_to_all(message, AXES, split_axis=0, concat_axis=0, tiled=True)  5.37 us
  transfers between devices with their start and end apart: 6, of which 2 were waited for; matrix products, arithmetic and copies ran while one was open for 6% of the time, Pallas kernels for 24%

commit v1 on v0

--- a/solution.py
+++ b/solution.py
@@ -15,7 +15,7 @@
 VMEM = pltpu.VMEM
 SMEM = pl.BlockSpec(memory_space=pltpu.SMEM)
 MIB = 1 << 20
-RING = 4
+CHUNKS = 8
 
 
 def params(mib):
@@ -73,67 +73,70 @@
         out_specs=[whole()] * 2,
         out_shape=[jax.ShapeDtypeStruct((2, n), I32), jax.ShapeDtypeStruct((n, 1, LANES), I32)],
         scratch_shapes=[VMEM((4, 1, n), I32), pltpu.SemaphoreType.DMA((4,))],
-        compiler_params=params(60),
+        compiler_params=params(61),
         cost_estimate=cost(4_000_000, 100_000),
         name="slot_tables",
     )(owner, block_device, source_row, target_row)
 
 
-def table_copies(sent_in, asked_in, sent, asked, sems):
-    return [
-        pltpu.make_async_copy(sent_in, sent, sems.at[0]),
-        pltpu.make_async_copy(asked_in, asked, sems.at[1]),
-    ]
-
-
-def table_scratch(devices):
-    return [
-        pltpu.SMEM((2, devices), I32),
-        pltpu.SMEM((devices, 1, LANES), I32),
-        pltpu.SemaphoreType.DMA((2,)),
-    ]
-
-
-def gather_kernel(sent_in, asked_in, flow_in, message, asked_out, sent, asked, sems, flow, more):
-    count = message.shape[0]
-    base = pl.program_id(0) * count
-
-    @pl.when(pl.program_id(0) == 0)
-    def _():
-        copies = table_copies(sent_in, asked_in, sent, asked, sems) + [
-            pltpu.make_async_copy(flow_in, flow, more.at[0]),
-            pltpu.make_async_copy(asked_in, asked_out, more.at[1]),
-        ]
-        for copy in copies:
-            copy.start()
-        for copy in copies:
-            copy.wait()
+def begin(copies):
+    for copy in copies:
+        copy.start()
+
+
+def finish(copies):
+    for copy in copies:
+        copy.wait()
+
+
+def gather_kernel(sent_in, asked_in, flow_in, message_out, asked_out, sent, asked, flow, packed, message, sems, out_sems):
+    n = message.shape[0]
+    copies = [pltpu.make_async_copy(sent_in, sent, sems.at[0]), pltpu.make_async_copy(flow_in, flow, sems.at[1])]
+    begin(copies)
+    eye = lax.broadcasted_iota(I32, (n, n), 0) == lax.broadcasted_iota(I32, (n, n), 1)
+    table = asked_in[...].reshape(n, LANES).astype(F32)
+    for k in range(2):
+        packed[k : k + 1, :] = jnp.sum(jnp.where(eye, table[:, k : k + 1], 0.0), axis=0, keepdims=True).astype(I32)
+    tables = [pltpu.make_async_copy(packed, asked, sems.at[2]), pltpu.make_async_copy(packed, asked_out, sems.at[3])]
+    begin(tables)
+    finish(copies + tables)
 
     def step(d, carry):
-        for part in range(2):
+        for part, rows in enumerate((sent, asked)):
             for k in range(2):
-                slot = asked[base + d, 0, k] if part else sent[k, base + d]
-                row = jnp.maximum(slot - 1, 0)
+                row = jnp.maximum(rows[k, d] - 1, 0)
                 for h in range(2):
                     start = 28 * part + 14 * k + NV * h
                     message[d, start : start + NV, :] = flow[row, :, LANES * h : LANES * (h + 1)]
         return carry
 
-    lax.fori_loop(0, count, step, 0, unroll=2)
+    size = n // CHUNKS
+    stores = []
+    for c in range(CHUNKS):
+        lax.fori_loop(c * size, (c + 1) * size, step, 0, unroll=4)
+        part = pl.ds(c * size, size)
+        stores.append(pltpu.make_async_copy(message.at[part], message_out.at[part], out_sems.at[c]))
+        stores[-1].start()
+    finish(stores)
 
 
 def gather(sent, asked, flow):
     devices = asked.shape[0]
+    message = (devices, 8 * NV, LANES)
     return pl.pallas_call(
         gather_kernel,
-        grid=(8,),
         in_specs=[whole(pltpu.HBM), whole(), whole(pltpu.HBM)],
-        out_specs=[pl.BlockSpec((devices // 8, 8 * NV, LANES), lambda g: (g, 0, 0)), whole(pltpu.HBM)],
-        out_shape=[
-            jax.ShapeDtypeStruct((devices, 8 * NV, LANES), F32),
-            jax.ShapeDtypeStruct(asked.shape, I32),
+        out_specs=[whole(pltpu.HBM)] * 2,
+        out_shape=[jax.ShapeDtypeStruct(message, F32), jax.ShapeDtypeStruct((2, devices), I32)],
+        scratch_shapes=[
+            pltpu.SMEM((2, devices), I32),
+            pltpu.SMEM((2, devices), I32),
+            VMEM(flow.shape, F32),
+            VMEM((2, devices), I32),
+            VMEM(message, F32),
+            pltpu.SemaphoreType.DMA((4,)),
+            pltpu.SemaphoreType.DMA((CHUNKS,)),
         ],
-        scratch_shapes=table_scratch(devices) + [VMEM(flow.shape, F32), pltpu.SemaphoreType.DMA((2,))],
         compiler_params=params(58),
         cost_estimate=cost(1_000_000, 6_000_000),
         name="gather",
@@ -215,192 +218,185 @@
         out_specs=[whole()] * 3,
         out_shape=[jax.ShapeDtypeStruct(s, F32) for s in shapes],
         scratch_shapes=[VMEM((2 * NV, rows + 16, LANES), F32), pltpu.SemaphoreType.DMA((2,))],
-        compiler_params=params(52),
+        compiler_params=params(61),
         cost_estimate=cost(30_000_000, 8_000_000),
         name="first_sum",
     )(parity, flow, right, coef, mix, halo_a, halo_b, inv)
 
 
+def added(sources, tile, v):
+    return jnp.concatenate([ref[pl.ds(64 * tile + 8 + v, 8, stride=8), :] for ref in sources], axis=1)
+
+
 def scatter_kernel(
-    parity, sent_in, asked_in, message, start_edges, inv_edges, source, edge_a, edge_b, sent, asked, sems
+    parity, sent, asked, message_in, start_edges, inv_edges, left, right, edge_a, edge_b, message, sems
 ):
-    groups = source.shape[1] // 8
-    count = message.shape[0]
-    base = pl.program_id(0) * count
-
-    @pl.when(pl.program_id(0) == 0)
-    def _():
-        copies = table_copies(sent_in, asked_in, sent, asked, sems)
-        for copy in copies:
-            copy.start()
-
-        def clear(g, carry):
-            for h in range(2):
-                source[h, pl.ds(pl.multiple_of(64 * g, 64), 64), :] = jnp.zeros((64, LANES), F32)
-            return carry
-
-        lax.fori_loop(0, groups // 8, clear, 0)
-        for copy in copies:
-            copy.wait()
+    sources = (left, right)
+    groups = left.shape[0] // 8
+    size = message.shape[0] // CHUNKS
+    loads = []
+    for c in range(CHUNKS):
+        part = pl.ds(c * size, size)
+        loads.append(pltpu.make_async_copy(message_in.at[part], message.at[part], sems.at[c]))
+    begin(loads)
+
+    def clear(g, carry):
+        for ref in sources:
+            ref[pl.ds(pl.multiple_of(64 * g, 64), 64), :] = jnp.zeros((64, LANES), F32)
+        return carry
+
+    lax.fori_loop(0, groups // 8, clear, 0)
 
     def step(d, carry):
-        for part in range(2):
+        for part, rows in enumerate((asked, sent)):
             for k in range(2):
-                slot = sent[k, base + d] if part else asked[base + d, 0, k]
-                row = pl.multiple_of(8 * slot, 8)
-                for h in range(2):
+                row = pl.multiple_of(8 * rows[k, d], 8)
+                for h, ref in enumerate(sources):
                     start = 28 * part + 14 * k + NV * h
                     value = message[d, start : start + NV, :]
-                    old = source[h, pl.ds(row, NV), :]
-                    source[h, pl.ds(row, NV), :] = old - value if part else old + value
+                    old = ref[pl.ds(row, NV), :]
+                    ref[pl.ds(row, NV), :] = old - value if part else old + value
         return carry
 
-    lax.fori_loop(0, count, step, 0, unroll=2)
-
-    @pl.when(pl.program_id(0) == pl.num_programs(0) - 1)
-    def _():
-        even = parity[0] == 0
-        edges = []
-        for g, (tile, sub) in enumerate(((0, 0), (groups // 8 - 2, 7))):
-            cells = [start_edges[g, v] + added(source, tile, v) for v in range(NV)]
-            relaxed = apply_inv(lambda i, j, g=g: inv_edges[g, i, j], cells)
-            edges.append([r[sub : sub + 1, :] for r in relaxed])
-        for v in range(NV):
-            top, bottom = edges[0][v], edges[1][v]
-            out_a, out_b = jnp.where(even, bottom, top), jnp.where(even, top, bottom)
-            for h in range(2):
-                n = 2 * v + h
-                edge_a[n : n + 1, :] = out_a[:, LANES * h : LANES * (h + 1)]
-                edge_b[n : n + 1, :] = out_b[:, LANES * h : LANES * (h + 1)]
-
-
-def added(source, tile, v):
-    return jnp.concatenate([source[h, pl.ds(64 * tile + 8 + v, 8, stride=8), :] for h in range(2)], axis=1)
+    for c in range(CHUNKS):
+        loads[c].wait()
+        lax.fori_loop(c * size, (c + 1) * size, step, 0, unroll=4)
+    even = parity[0] == 0
+    edges = []
+    for g, (tile, sub) in enumerate(((0, 0), (groups // 8 - 2, 7))):
+        cells = [start_edges[g, v] + added(sources, tile, v) for v in range(NV)]
+        relaxed = apply_inv(lambda i, j, g=g: inv_edges[g, i, j], cells)
+        edges.append([r[sub : sub + 1, :] for r in relaxed])
+    for v in range(NV):
+        top, bottom = edges[0][v], edges[1][v]
+        out_a, out_b = jnp.where(even, bottom, top), jnp.where(even, top, bottom)
+        for h in range(2):
+            n = 2 * v + h
+            edge_a[n : n + 1, :] = out_a[:, LANES * h : LANES * (h + 1)]
+            edge_b[n : n + 1, :] = out_b[:, LANES * h : LANES * (h + 1)]
 
 
 def scatter(parity, sent, asked, message, start_edges, inv_edges, rows):
-    devices = message.shape[0]
-    steps = 8
-    sources = (2, 8 * (rows + 8), LANES)
-    edge = (2 * NV, LANES)
+    shapes = [(8 * (rows + 8), LANES)] * 2 + [(2 * NV, LANES)] * 2
     return pl.pallas_call(
         scatter_kernel,
-        grid=(steps,),
-        in_specs=[
-            SMEM,
-            whole(pltpu.HBM),
-            whole(pltpu.HBM),
-            pl.BlockSpec((devices // steps,) + message.shape[1:], lambda g: (g, 0, 0)),
-            whole(),
-            whole(),
-        ],
-        out_specs=[whole()] * 3,
-        out_shape=[jax.ShapeDtypeStruct(s, F32) for s in (sources, edge, edge)],
-        scratch_shapes=table_scratch(devices),
-        compiler_params=params(16),
+        in_specs=[SMEM] * 3 + [whole(pltpu.HBM)] + [whole()] * 2,
+        out_specs=[whole()] * 4,
+        out_shape=[jax.ShapeDtypeStruct(s, F32) for s in shapes],
+        scratch_shapes=[VMEM(message.shape, F32), pltpu.SemaphoreType.DMA((CHUNKS,))],
+        compiler_params=params(61),
         cost_estimate=cost(2_000_000, 7_000_000),
         name="scatter",
     )(parity, sent, asked, message, start_edges, inv_edges)
 
 
 def sweeps_kernel(
-    source, mix, start_in, right_in, coef_in, inv_in, out, state, done, start, right, coef, inv, sems, out_sems
+    mix,
+    left_in,
+    other_in,
+    start_in,
+    right_in,
+    coef_in,
+    inv_in,
+    out,
+    state,
+    done,
+    left,
+    other,
+    start,
+    right,
+    coef,
+    inv,
+    sems,
+    out_sems,
 ):
-    tiles = start_in.shape[1] // 8
-    chunk = 4
-
-    def fetch(t):
-        slot = lax.rem(t, RING)
-        rows = pl.ds(pl.multiple_of(8 * t, 8), 8)
+    sources = (left, other)
+    tiles = start.shape[1] // 8
+    size = tiles // CHUNKS
+
+    def fetch(c):
+        rows = pl.ds(pl.multiple_of(8 * size * c, 8), 8 * size)
         streams = ((start_in, start), (right_in, right), (coef_in, coef))
         copies = [
-            pltpu.make_async_copy(ref.at[:, rows, :], part.at[slot], sems.at[n, slot])
+            pltpu.make_async_copy(ref.at[:, rows, :], part.at[:, rows, :], sems.at[n, c])
             for n, (ref, part) in enumerate(streams)
         ]
-        return copies + [pltpu.make_async_copy(inv_in.at[:, :, rows, :], inv.at[slot], sems.at[3, slot])]
-
-    def begin(copies):
-        for copy in copies:
-            copy.start()
-
-    def finish(copies):
-        for copy in copies:
-            copy.wait()
+        groups = pl.ds(pl.multiple_of(64 * size * c + 8, 8), 64 * size)
+        copies += [
+            pltpu.make_async_copy(ref.at[groups, :], part.at[groups, :], sems.at[n, c])
+            for n, (ref, part) in enumerate(((left_in, left), (other_in, other)), 3)
+        ]
+        return copies + [pltpu.make_async_copy(inv_in.at[:, :, rows, :], inv.at[:, :, rows, :], sems.at[5, c])]
 
     def store(c):
-        rows = pl.ds(pl.multiple_of(8 * chunk * c, 8), 8 * chunk)
+        rows = pl.ds(pl.multiple_of(8 * size * c, 8), 8 * size)
         return pltpu.make_async_copy(done.at[:, rows, :], out.at[:, rows, :], out_sems.at[c])
 
-    for t in range(RING):
-        begin(fetch(t))
+    for c in range(CHUNKS):
+        begin(fetch(c))
     for n in range(2 * NV):
         state[n, 0:8, :] = jnp.zeros((8, LANES), F32)
         state[n, 8 + 8 * tiles : 16 + 8 * tiles, :] = jnp.zeros((8, LANES), F32)
 
     def sweep_one(t):
-        slot = lax.rem(t, RING)
-        row = pl.multiple_of(8 * t, 8)
-        cells = [start[slot, v] + added(source, t, v) for v in range(NV)]
-        relaxed = apply_inv(lambda i, j: inv[slot, i, j], cells)
+        rows = pl.ds(pl.multiple_of(8 * t, 8), 8)
+        cells = [start[v, rows, :] + added(sources, t, v) for v in range(NV)]
+        relaxed = apply_inv(lambda i, j: inv[i, j, rows, :], cells)
         for v in range(NV):
             for h in range(2):
-                state[2 * v + h, pl.ds(row + 8, 8), :] = relaxed[v][:, LANES * h : LANES * (h + 1)]
+                state[2 * v + h, pl.ds(8 * t + 8, 8), :] = relaxed[v][:, LANES * h : LANES * (h + 1)]
 
     def sweep_two(t):
-        slot = lax.rem(t, RING)
-        row = pl.multiple_of(8 * t, 8)
-        sums = coupled(state, row + 8, lambda d: coef[slot, d], mix)
-        cells = [right[slot, v] + added(source, t, v) - sums[8 * v : 8 * v + 8, :] for v in range(NV)]
-        relaxed = apply_inv(lambda i, j: inv[slot, i, j], cells)
+        rows = pl.ds(pl.multiple_of(8 * t, 8), 8)
+        sums = coupled(state, pl.multiple_of(8 * t + 8, 8), lambda d: coef[d, rows, :], mix)
+        cells = [right[v, rows, :] + added(sources, t, v) - sums[8 * v : 8 * v + 8, :] for v in range(NV)]
+        relaxed = apply_inv(lambda i, j: inv[i, j, rows, :], cells)
         for v in range(NV):
-            done[v, pl.ds(row, 8), :] = relaxed[v]
-
-    finish(fetch(0))
-    sweep_one(0)
-
-    def step(t, carry):
-        finish(fetch(t))
-        sweep_one(t)
-        sweep_two(t - 1)
-
-        @pl.when(t + RING - 1 < tiles)
+            done[v, rows, :] = relaxed[v]
+
+    def step(c, carry):
+        finish(fetch(c))
+        for k in range(size):
+            t = c * size + k
+            sweep_one(t)
+            sweep_two(jnp.maximum(t - 1, 0))
+
+        @pl.when(c > 0)
         def _():
-            begin(fetch(t + RING - 1))
-
-        @pl.when(lax.rem(t, chunk) == 0)
-        def _():
-            store(t // chunk - 1).start()
+            store(c - 1).start()
 
         return carry
 
-    lax.fori_loop(1, tiles, step, 0)
+    lax.fori_loop(0, CHUNKS, step, 0)
     sweep_two(tiles - 1)
-    store(tiles // chunk - 1).start()
-    for c in range(tiles // chunk):
+    store(CHUNKS - 1).start()
+    for c in range(CHUNKS):
         store(c).wait()
 
 
-def sweeps(source, mix, start, right, coef, inv):
+def sweeps(left, other, mix, start, right, coef, inv):
     rows = start.shape[1]
     return pl.pallas_call(
         sweeps_kernel,
-        in_specs=[whole()] * 2 + [whole(pltpu.HBM)] * 4,
+        in_specs=[whole()] + [whole(pltpu.HBM)] * 6,
         out_specs=whole(pltpu.HBM),
         out_shape=jax.ShapeDtypeStruct(start.shape, F32),
         scratch_shapes=[
             VMEM((2 * NV, rows + 16, LANES), F32),
             VMEM(start.shape, F32),
-            VMEM((RING, NV, 8, COLS), F32),
-            VMEM((RING, NV, 8, COLS), F32),
-            VMEM((RING, 4, 8, COLS), F32),
-            VMEM((RING, NV, NV, 8, COLS), F32),
-            pltpu.SemaphoreType.DMA((4, RING)),
-            pltpu.SemaphoreType.DMA((rows // 32,)),
+            VMEM(left.shape, F32),
+            VMEM(left.shape, F32),
+            VMEM(start.shape, F32),
+            VMEM(start.shape, F32),
+            VMEM(coef.shape, F32),
+            VMEM(inv.shape, F32),
+            pltpu.SemaphoreType.DMA((6, CHUNKS)),
+            pltpu.SemaphoreType.DMA((CHUNKS,)),
         ],
-        compiler_params=params(40),
+        compiler_params=params(61),
         cost_estimate=cost(45_000_000, 24_000_000),
         name="sweeps",
-    )(source, mix, start, right, coef, inv)
+    )(mix, left, other, start, right, coef, inv)
 
 
 def edge_kernel(parity, relaxed, coef, mix, inv, halo_a, halo_b, out):
@@ -443,7 +439,7 @@
         out_specs=slab,
         out_shape=jax.ShapeDtypeStruct(relaxed.shape, F32),
         input_output_aliases={1: 0},
-        compiler_params=params(40),
+        compiler_params=params(24),
         cost_estimate=cost(100_000, 900_000),
         name="edge_rows",
     )(parity, relaxed, coef, mix, inv, halo_a, halo_b)
@@ -472,19 +468,20 @@
     as_row = lambda a: a.reshape(1, -1)
     sent, asking = slot_tables(as_row(hole_owner), as_row(block_device), as_row(source_row), as_row(target_row))
     asked = lax.all_to_all(asking, AXES, split_axis=0, concat_axis=0, tiled=True)
-    message, asked = gather(sent, asked, flow_state[0])
-    message = lax.all_to_all(message, AXES, split_axis=0, concat_axis=0, tiled=True)
-
-    coef = jnp.transpose(face_coef[0], (1, 0, 2))
-    mix = mixing(face_jacobian)
     top, bottom = flow[:, 0].reshape(2 * NV, LANES), flow[:, rows - 1].reshape(2 * NV, LANES)
     even = parity[0] == 0
     halo_a, halo_b = exchange(jnp.where(even, bottom, top), jnp.where(even, top, bottom))
+    asked, halo_a, halo_b = lax.optimization_barrier((asked, halo_a, halo_b))
+    message, asked = gather(sent, asked, flow_state[0])
+    message = lax.all_to_all(message, AXES, split_axis=0, concat_axis=0, tiled=True)
+
+    coef = jnp.transpose(face_coef[0], (1, 0, 2))
+    mix = mixing(face_jacobian)
     start, start_edges, inv_edges = first_sum(parity, flow, right, coef, mix, halo_a, halo_b, inv)
 
-    source, edge_a, edge_b = scatter(parity, sent, asked, message, start_edges, inv_edges, rows)
+    left, other, edge_a, edge_b = scatter(parity, sent, asked, message, start_edges, inv_edges, rows)
     halo_a, halo_b = exchange(edge_a, edge_b)
-    relaxed = sweeps(source, mix, start, right, coef, inv)
+    relaxed = sweeps(left, other, mix, start, right, coef, inv)
     relaxed = edge_rows(parity, relaxed, coef, mix, inv_edges, halo_a, halo_b)
     return jnp.transpose(relaxed, (1, 0, 2))[None]
 

time: 121 us -> 106 us (0.88)
  Pallas kernels: 47 us -> 36.9 us
  waiting for transfers between devices: 39.9 us -> 32.4 us
  starting transfers between devices: 23.2 us -> 27 us
    ppermute x2, waiting for transfers between devices: 34.3 us -> 0.01 us  [exchange(): lax.ppermute(edge_b, 'blk', pairs_b)]
    all_to_all x1, waiting for transfers between devices: 0.01 us -> 31.5 us  [body(): lax.all_to_all(message, AXES, split_axis=0, concat_axis=0, tiled=True)]
    pallas_call x3, Pallas kernels: 31.1 us -> 20.7 us  [the longest x1 10.2 us: sweeps(): pl.pallas_call(sweeps_kernel, in_specs=[whole()] + [whole(pltpu.HBM)] * 6...]
    all_to_all x1, waiting for transfers between devices: 5.54 us -> 0.86 us  [body(): lax.all_to_all(asking, AXES, split_axis=0, concat_axis=0, tiled=True)]
    all_to_all x1, starting transfers between devices: 5.37 us -> 8.63 us  [body(): lax.all_to_all(message, AXES, split_axis=0, concat_axis=0, tiled=True)]
  transfers between devices with their start and end apart: 6 -> 6, of which waited for: 2 -> 2; matrix products, arithmetic and copies ran while one was open for 6% -> 7% of each run, Pallas kernels for 24% -> 22%
where the time goes in v1:
time: 106 us; the launch traced here: 105 us
  Pallas kernels  36.9 us (35%)
  waiting for transfers between devices  32.4 us (31%)
  starting transfers between devices  27 us (25%)
  local copies, waits for them, and re-layouts  6.75 us (6%)
  other arithmetic  1.7 us (2%)
    all_to_all x1, waiting for transfers between devices, body(): lax.all_to_all(message, AXES, split_axis=0, concat_axis=0, tiled=True)  31.5 us
    pallas_call x1, Pallas kernels, first_sum(): pl.pallas_call(first_kernel, in_specs=[SMEM] + [whole()] * 6 + [whole(plt...  12.5 us
    all_to_all x1, starting transfers between devices, body(): lax.all_to_all(asking, AXES, split_axis=0, concat_axis=0, tiled=True)  11.5 us
    pallas_call x1, Pallas kernels, sweeps(): pl.pallas_call(sweeps_kernel, in_specs=[whole()] + [whole(pltpu.HBM)] * 6...  10.2 us
    all_to_all x1, starting transfers between devices, body(): lax.all_to_all(message, AXES, split_axis=0, concat_axis=0, tiled=True)  8.63 us
    pallas_call x1, Pallas kernels, scatter(): pl.pallas_call(scatter_kernel, in_specs=[SMEM] * 3 + [whole(pltpu.HBM)] +...  5.89 us
    ppermute x2, starting transfers between devices, exchange(): lax.ppermute(edge_b, 'blk', pairs_b)  4.68 us
    pallas_call x1, Pallas kernels, gather(): pl.pallas_call(gather_kernel, in_specs=[whole(pltpu.HBM), whole(), whole(...  4.59 us
  transfers between devices with their start and end apart: 6, of which 2 were waited for; matrix products, arithmetic and copies ran while one was open for 7% of the time, Pallas kernels for 22%

profile of v1, /device:TPU:1, one launch (start us, length us, event | category | flops | bytes accessed | tf_op | source)
XLA Modules:
  0.0 105.0 jit_solution(9651901212218226691)
XLA Ops:
  0.0 1.8 %slot_tables.1 = (s32[2,128]{1,0:T(2,128)}, s32[128,1,128]{2,1,0:T(1,128)}) custom-call(s32[1,128]{1,0:T(1,128)} %bitcast.34, s32[1,128]{1,0:T(1,128)} %bitcast.35, s32[1,128]{1,0:T(1,128)} %bitcast.36, s32[1,128]{1,0:T(1,128)} %bitcast.37), custom_call_target="tpu_custom_call" | custom-call | flops 4000000 | bytes 100000 | tf_op jit(solution)/shard_map/slot_tables/pallas_call | solution.py:70
  1.8 11.5 %all-to-all-start = ((s32[128,1,128]{2,1,0:T(1,128)}), s32[128,1,128]{2,1,0:T(1,128)S(1)}, u32[]{:S(2)}, u32[]{:S(2)}) async-start(s32[128,1,128]{2,1,0:T(1,128)} %get-tuple-element.20), calls=%async_computation | async-start | bytes 131072 | tf_op jit(solution)/shard_map/all_to_all | solution.py:470
  13.3 0.9 fusion.2
  14.2 1.1 %collective-permute-start = (f32[14,128]{1,0:T(8,128)S(1)}, f32[14,128]{1,0:T(8,128)S(1)}, u32[]{:S(2)}, u32[]{:S(2)}) collective-permute-start(f32[14,128]{1,0:T(8,128)S(1)} %select_n.28), channel_id=1, source_target_pairs={{0,1},{1,0},{2,3},{3,2},{4,5},{5,4},{6,7},{7,6},{8,9},{9,8},{10,11... | collective-permute-start | bytes 21512 | tf_op jit(solution)/shard_map/ppermute | solution.py:452
  15.4 2.6 %collective-permute-start.1 = (f32[14,128]{1,0:T(8,128)S(1)}, f32[14,128]{1,0:T(8,128)S(1)}, u32[]{:S(2)}, u32[]{:S(2)}) collective-permute-start(f32[14,128]{1,0:T(8,128)S(1)} %select_n.30), channel_id=1, source_target_pairs={{1,2},{2,1},{3,4},{4,3},{5,6},{6,5},{7,8},{8,7},{9,10},{10,9},{11,... | collective-permute-start | bytes 21512 | tf_op jit(solution)/shard_map/ppermute | solution.py:452
  18.0 3.9 %copy.13.flow_in = f32[256,7,256]{2,1,0:T(8,128)} copy(f32[256,7,256]{2,0,1:T(8,128)} %bitcast.29) | data formatting | bytes 3670016 | tf_op jit(solution)/shard_map/squeeze | solution.py:463
  21.9 0.9 all-to-all-done.asked_in
  22.8 0.6 copy-done.4
  23.4 4.6 %gather.1 = (f32[128,56,128]{2,1,0:T(8,128)}, s32[2,128]{1,0:T(2,128)}) custom-call(s32[2,128]{1,0:T(2,128)} %get-tuple-element.19.sent_in.sent, s32[128,1,128]{2,1,0:T(1,128)} %copy-done.4, f32[256,7,256]{2,1,0:T(8,128)} %copy.13.flow_in), custom_call_target="tpu_custom_call" | custom-call | flops 1000000 | bytes 6000000 | tf_op jit(solution)/shard_map/gather/pallas_call | solution.py:126
  28.0 0.0 copy-start.5
  28.0 8.6 %all-to-all-start.1 = ((f32[128,56,128]{2,1,0:T(8,128)}), f32[128,56,128]{2,1,0:T(8,128)}, u32[]{:S(2)}, u32[]{:S(2)}) async-start(f32[128,56,128]{2,1,0:T(8,128)} %get-tuple-element.23), calls=%async_computation.1 | async-start | bytes 7340032 | tf_op jit(solution)/shard_map/all_to_all | solution.py:476
  36.7 0.1 mul.30
  36.8 0.2 broadcast_multiply_fusion
  36.9 0.4 mul.34
  37.4 0.5 copy-done.3
  37.9 1.2 %copy.16 = f32[1,256,4,256]{3,1,2,0:T(8,128)} copy(f32[1,256,4,256]{3,2,1,0:T(4,128)S(1)} %copy-done.3) | data formatting | bytes 2097152 | tf_op args[3]
  39.1 0.6 pad_maximum_fusion.mix
  39.7 12.5 %first_sum.1 = (f32[7,256,256]{2,1,0:T(8,128)}, f32[2,7,8,256]{3,2,1,0:T(8,128)}, f32[2,7,7,8,256]{4,3,2,1,0:T(8,128)}) custom-call(s32[1]{0:T(128)} %bitcast.parity, f32[7,256,256]{2,1,0:T(8,128)} %bitcast.30, f32[7,256,256]{2,1,0:T(8,128)} %bitcast.31, f32[4,256,256]{2,1,0:T(8,128)} %bitcast.23, bf16[2,56,224]{2,1,0:T(8,128)(2,1)} %pad_maximum_fusion.mix, ...), custom_call_target="tpu_custom_call" | custom-call | flops 30000000 | bytes 8000000 | tf_op jit(solution)/shard_map/first_sum/pallas_call | solution.py:215
  52.2 31.5 %all-to-all-done.1.message_in = f32[128,56,128]{2,1,0:T(8,128)} async-done(((f32[128,56,128]{2,1,0:T(8,128)}), f32[128,56,128]{2,1,0:T(8,128)}, u32[]{:S(2)}, u32[]{:S(2)}) %all-to-all-start.1) | async-done | bytes 3670048 | tf_op jit(solution)/shard_map/all_to_all | solution.py:476
  83.7 5.9 %scatter.1 = (f32[2112,128]{1,0:T(8,128)}, f32[2112,128]{1,0:T(8,128)}, f32[14,128]{1,0:T(8,128)}, f32[14,128]{1,0:T(8,128)}) custom-call(s32[1]{0:T(128)} %bitcast.parity, s32[2,128]{1,0:T(2,128)} %get-tuple-element.19.sent_in.sent, s32[2,128]{1,0:T(2,128)} %get-tuple-element.22.asked, f32[128,56,128]{2,1,0:T(8,128)} %all-to-all-done.1.message_in, ...), custom_call_target="tpu_custom_call" | custom-call | flops 2000000 | bytes 7000000 | tf_op jit(solution)/shard_map/scatter/pallas_call | solution.py:281
  89.6 1.1 %collective-permute-start.2 = (f32[14,128]{1,0:T(8,128)}, f32[14,128]{1,0:T(8,128)S(1)}, u32[]{:S(2)}, u32[]{:S(2)}) collective-permute-start(f32[14,128]{1,0:T(8,128)} %get-tuple-element.31), channel_id=1, source_target_pairs={{0,1},{1,0},{2,3},{3,2},{4,5},{5,4},{6,7},{7,6},{8,9},{9,8},{10,11... | collective-permute-start | bytes 21512 | tf_op jit(solution)/shard_map/ppermute | solution.py:452
  90.7 2.1 %collective-permute-start.3 = (f32[14,128]{1,0:T(8,128)}, f32[14,128]{1,0:T(8,128)S(1)}, u32[]{:S(2)}, u32[]{:S(2)}) collective-permute-start(f32[14,128]{1,0:T(8,128)} %get-tuple-element.32), channel_id=1, source_target_pairs={{1,2},{2,1},{3,4},{4,3},{5,6},{6,5},{7,8},{8,7},{9,10},{10,9},{11,... | collective-permute-start | bytes 21512 | tf_op jit(solution)/shard_map/ppermute | solution.py:452
  92.8 10.2 %sweeps.1.relaxed = f32[7,256,256]{2,1,0:T(8,128)} custom-call(bf16[2,56,224]{2,1,0:T(8,128)(2,1)} %pad_maximum_fusion.mix, f32[2112,128]{1,0:T(8,128)} %get-tuple-element.28.left_in, f32[2112,128]{1,0:T(8,128)} %get-tuple-element.29.other_in, f32[7,256,256]{2,1,0:T(8,128)} %get-tuple-element.30.start_in, f32[7,256,256]{2,1,0:T(8,128)} %bitcast.32, ...), custom_call_target="tpu_custom_call" | custom-call | flops 45000000 | bytes 24000000 | tf_op jit(solution)/shard_map/sweeps/pallas_call | solution.py:379
  103.1 1.9 %edge_rows.1 = f32[7,256,256]{2,1,0:T(8,128)} custom-call(s32[1]{0:T(128)} %bitcast.parity, f32[7,256,256]{2,1,0:T(8,128)} %sweeps.1.relaxed, f32[4,256,256]{2,1,0:T(8,128)S(1)} %bitcast.25, bf16[2,56,224]{2,1,0:T(8,128)(2,1)S(1)} %copy-done.2, f32[2,7,7,8,256]{4,3,2,1,0:T(8,128)S(1)} %copy-done.1, ...), custom_call_target="tpu_custom_call", output_to_operand_aliasing={{}: (1, {})} | custom-call | flops 100000 | bytes 900000 | tf_op jit(solution)/shard_map/edge_rows/pallas_call | solution.py:427
  (21 shorter events, 0.1 us)
Async XLA Ops:
  1.8 20.9 %all-to-all-start = ((s32[128,1,128]{2,1,0:T(1,128)}), s32[128,1,128]{2,1,0:T(1,128)S(1)}, u32[]{:S(2)}, u32[]{:S(2)}) async-start(s32[128,1,128]{2,1,0:T(1,128)} %get-tuple-element.20), calls=%async_computation | async-start | bytes 131072 | tf_op jit(solution)/shard_map/all_to_all | solution.py:470
  14.2 7.6 %collective-permute-start = (f32[14,128]{1,0:T(8,128)S(1)}, f32[14,128]{1,0:T(8,128)S(1)}, u32[]{:S(2)}, u32[]{:S(2)}) collective-permute-start(f32[14,128]{1,0:T(8,128)S(1)} %select_n.28), channel_id=1, source_target_pairs={{0,1},{1,0},{2,3},{3,2},{4,5},{5,4},{6,7},{7,6},{8,9},{9,8},{10,11... | collective-permute-start | bytes 21512 | tf_op jit(solution)/shard_map/ppermute | solution.py:452
  15.4 6.5 %collective-permute-start.1 = (f32[14,128]{1,0:T(8,128)S(1)}, f32[14,128]{1,0:T(8,128)S(1)}, u32[]{:S(2)}, u32[]{:S(2)}) collective-permute-start(f32[14,128]{1,0:T(8,128)S(1)} %select_n.30), channel_id=1, source_target_pairs={{1,2},{2,1},{3,4},{4,3},{5,6},{6,5},{7,8},{8,7},{9,10},{10,9},{11,... | collective-permute-start | bytes 21512 | tf_op jit(solution)/shard_map/ppermute | solution.py:452
  21.9 15.5 %copy-start.6 = (f32[14,128]{1,0:T(8,128)}, f32[14,128]{1,0:T(8,128)S(1)}, u32[]{:S(2)}) copy-start(f32[14,128]{1,0:T(8,128)S(1)} %collective-permute-done.halo_a) | copy-start | bytes 21508
  21.9 15.5 %copy-start.7 = (f32[14,128]{1,0:T(8,128)}, f32[14,128]{1,0:T(8,128)S(1)}, u32[]{:S(2)}) copy-start(f32[14,128]{1,0:T(8,128)S(1)} %collective-permute-done.1.halo_b) | copy-start | bytes 21508
  22.8 0.6 copy-start.4
  28.0 8.7 %copy-start.5 = (f32[4,7,7]{2,0,1:T(4,128)S(1)}, f32[4,7,7]{2,0,1:T(4,128)}, u32[]{:S(2)}) copy-start(f32[4,7,7]{2,0,1:T(4,128)} %param.13) | copy-start | bytes 2356
  28.0 55.7 %all-to-all-start.1 = ((f32[128,56,128]{2,1,0:T(8,128)}), f32[128,56,128]{2,1,0:T(8,128)}, u32[]{:S(2)}, u32[]{:S(2)}) async-start(f32[128,56,128]{2,1,0:T(8,128)} %get-tuple-element.23), calls=%async_computation.1 | async-start | bytes 7340032 | tf_op jit(solution)/shard_map/all_to_all | solution.py:476
  36.7 1.2 %copy-start.3 = (f32[1,256,4,256]{3,2,1,0:T(4,128)S(1)}, f32[1,256,4,256]{3,2,1,0:T(4,128)}, u32[]{:S(2)}) copy-start(f32[1,256,4,256]{3,2,1,0:T(4,128)} %param.12) | copy-start | bytes 3145732
  89.6 13.4 %collective-permute-start.2 = (f32[14,128]{1,0:T(8,128)}, f32[14,128]{1,0:T(8,128)S(1)}, u32[]{:S(2)}, u32[]{:S(2)}) collective-permute-start(f32[14,128]{1,0:T(8,128)} %get-tuple-element.31), channel_id=1, source_target_pairs={{0,1},{1,0},{2,3},{3,2},{4,5},{5,4},{6,7},{7,6},{8,9},{9,8},{10,11... | collective-permute-start | bytes 21512 | tf_op jit(solution)/shard_map/ppermute | solution.py:452
  90.7 12.4 %collective-permute-start.3 = (f32[14,128]{1,0:T(8,128)}, f32[14,128]{1,0:T(8,128)S(1)}, u32[]{:S(2)}, u32[]{:S(2)}) collective-permute-start(f32[14,128]{1,0:T(8,128)} %get-tuple-element.32), channel_id=1, source_target_pairs={{1,2},{2,1},{3,4},{4,3},{5,6},{6,5},{7,8},{8,7},{9,10},{10,9},{11,... | collective-permute-start | bytes 21512 | tf_op jit(solution)/shard_map/ppermute | solution.py:452
  92.8 10.3 %copy-start = (f32[1,256,4,256]{3,1,2,0:T(8,128)S(1)}, f32[1,256,4,256]{3,1,2,0:T(8,128)}, u32[]{:S(2)}) copy-start(f32[1,256,4,256]{3,1,2,0:T(8,128)} %copy.16) | copy-start | bytes 3145732
  92.8 10.3 %copy-start.1 = (f32[2,7,7,8,256]{4,3,2,1,0:T(8,128)S(1)}, f32[2,7,7,8,256]{4,3,2,1,0:T(8,128)}, u32[]{:S(2)}) copy-start(f32[2,7,7,8,256]{4,3,2,1,0:T(8,128)} %get-tuple-element.27.inv_edges.inv) | copy-start | bytes 2408452
  92.8 10.3 %copy-start.2 = (bf16[2,56,224]{2,1,0:T(8,128)(2,1)S(1)}, bf16[2,56,224]{2,1,0:T(8,128)(2,1)}, u32[]{:S(2)}) copy-start(bf16[2,56,224]{2,1,0:T(8,128)(2,1)} %pad_maximum_fusion.mix) | copy-start | bytes 150532

commit v2 on v1

--- a/solution.py
+++ b/solution.py
@@ -179,7 +179,7 @@
     return out
 
 
-def first_kernel(parity, flow, right, coef, mix, halo_a, halo_b, inv, start, start_edges, inv_edges, state, sems):
+def first_kernel(parity, flow, right, coef, mix, halo_a, halo_b, inv, start, inv_edges, state, sems):
     tiles = right.shape[1] // 8
     copies = [
         pltpu.make_async_copy(inv.at[:, :, 8 * t : 8 * t + 8, :], inv_edges.at[g], sems.at[g])
@@ -203,19 +203,17 @@
         return carry
 
     lax.fori_loop(0, tiles, step, 0)
-    start_edges[0] = start[:, 0:8, :]
-    start_edges[1] = start[:, 8 * tiles - 8 : 8 * tiles, :]
     for copy in copies:
         copy.wait()
 
 
 def first_sum(parity, flow, right, coef, mix, halo_a, halo_b, inv):
     rows = flow.shape[1]
-    shapes = (flow.shape, (2, NV, 8, COLS), (2, NV, NV, 8, COLS))
+    shapes = (flow.shape, (2, NV, NV, 8, COLS))
     return pl.pallas_call(
         first_kernel,
         in_specs=[SMEM] + [whole()] * 6 + [whole(pltpu.HBM)],
-        out_specs=[whole()] * 3,
+        out_specs=[whole()] * 2,
         out_shape=[jax.ShapeDtypeStruct(s, F32) for s in shapes],
         scratch_shapes=[VMEM((2 * NV, rows + 16, LANES), F32), pltpu.SemaphoreType.DMA((2,))],
         compiler_params=params(61),
@@ -224,95 +222,44 @@
     )(parity, flow, right, coef, mix, halo_a, halo_b, inv)
 
 
-def added(sources, tile, v):
-    return jnp.concatenate([ref[pl.ds(64 * tile + 8 + v, 8, stride=8), :] for ref in sources], axis=1)
-
-
-def scatter_kernel(
-    parity, sent, asked, message_in, start_edges, inv_edges, left, right, edge_a, edge_b, message, sems
-):
-    sources = (left, right)
-    groups = left.shape[0] // 8
-    size = message.shape[0] // CHUNKS
-    loads = []
-    for c in range(CHUNKS):
-        part = pl.ds(c * size, size)
-        loads.append(pltpu.make_async_copy(message_in.at[part], message.at[part], sems.at[c]))
-    begin(loads)
-
-    def clear(g, carry):
-        for ref in sources:
-            ref[pl.ds(pl.multiple_of(64 * g, 64), 64), :] = jnp.zeros((64, LANES), F32)
-        return carry
-
-    lax.fori_loop(0, groups // 8, clear, 0)
-
-    def step(d, carry):
-        for part, rows in enumerate((asked, sent)):
-            for k in range(2):
-                row = pl.multiple_of(8 * rows[k, d], 8)
-                for h, ref in enumerate(sources):
-                    start = 28 * part + 14 * k + NV * h
-                    value = message[d, start : start + NV, :]
-                    old = ref[pl.ds(row, NV), :]
-                    ref[pl.ds(row, NV), :] = old - value if part else old + value
-        return carry
-
-    for c in range(CHUNKS):
-        loads[c].wait()
-        lax.fori_loop(c * size, (c + 1) * size, step, 0, unroll=4)
-    even = parity[0] == 0
-    edges = []
-    for g, (tile, sub) in enumerate(((0, 0), (groups // 8 - 2, 7))):
-        cells = [start_edges[g, v] + added(sources, tile, v) for v in range(NV)]
-        relaxed = apply_inv(lambda i, j, g=g: inv_edges[g, i, j], cells)
-        edges.append([r[sub : sub + 1, :] for r in relaxed])
-    for v in range(NV):
-        top, bottom = edges[0][v], edges[1][v]
-        out_a, out_b = jnp.where(even, bottom, top), jnp.where(even, top, bottom)
-        for h in range(2):
-            n = 2 * v + h
-            edge_a[n : n + 1, :] = out_a[:, LANES * h : LANES * (h + 1)]
-            edge_b[n : n + 1, :] = out_b[:, LANES * h : LANES * (h + 1)]
-
-
-def scatter(parity, sent, asked, message, start_edges, inv_edges, rows):
-    shapes = [(8 * (rows + 8), LANES)] * 2 + [(2 * NV, LANES)] * 2
-    return pl.pallas_call(
-        scatter_kernel,
-        in_specs=[SMEM] * 3 + [whole(pltpu.HBM)] + [whole()] * 2,
-        out_specs=[whole()] * 4,
-        out_shape=[jax.ShapeDtypeStruct(s, F32) for s in shapes],
-        scratch_shapes=[VMEM(message.shape, F32), pltpu.SemaphoreType.DMA((CHUNKS,))],
-        compiler_params=params(61),
-        cost_estimate=cost(2_000_000, 7_000_000),
-        name="scatter",
-    )(parity, sent, asked, message, start_edges, inv_edges)
-
-
-def sweeps_kernel(
-    mix,
-    left_in,
-    other_in,
+def finish_kernel(
+    parity,
+    sent,
+    asked,
+    turn,
+    message_in,
     start_in,
     right_in,
     coef_in,
     inv_in,
     out,
-    state,
-    done,
-    left,
-    other,
+    edge_a,
+    edge_b,
+    message,
+    add_left,
+    add_right,
+    sub_left,
+    sub_right,
     start,
     right,
     coef,
     inv,
+    above,
+    below,
+    ends,
+    done,
+    message_sems,
     sems,
     out_sems,
 ):
-    sources = (left, other)
     tiles = start.shape[1] // 8
     size = tiles // CHUNKS
+    count = message.shape[0] // CHUNKS
+    plus, minus = (add_left, add_right), (sub_left, sub_right)
+
+    def load(c):
+        part = pl.ds(c * count, count)
+        return pltpu.make_async_copy(message_in.at[part], message.at[part], message_sems.at[c])
 
     def fetch(c):
         rows = pl.ds(pl.multiple_of(8 * size * c, 8), 8 * size)
@@ -321,35 +268,73 @@
             pltpu.make_async_copy(ref.at[:, rows, :], part.at[:, rows, :], sems.at[n, c])
             for n, (ref, part) in enumerate(streams)
         ]
-        groups = pl.ds(pl.multiple_of(64 * size * c + 8, 8), 64 * size)
-        copies += [
-            pltpu.make_async_copy(ref.at[groups, :], part.at[groups, :], sems.at[n, c])
-            for n, (ref, part) in enumerate(((left_in, left), (other_in, other)), 3)
-        ]
-        return copies + [pltpu.make_async_copy(inv_in.at[:, :, rows, :], inv.at[:, :, rows, :], sems.at[5, c])]
+        return copies + [pltpu.make_async_copy(inv_in.at[:, :, rows, :], inv.at[:, :, rows, :], sems.at[3, c])]
 
     def store(c):
         rows = pl.ds(pl.multiple_of(8 * size * c, 8), 8 * size)
         return pltpu.make_async_copy(done.at[:, rows, :], out.at[:, rows, :], out_sems.at[c])
 
+    begin([load(c) for c in range(CHUNKS)])
     for c in range(CHUNKS):
         begin(fetch(c))
+
+    def clear(g, carry):
+        for ref in plus + minus:
+            ref[pl.ds(pl.multiple_of(64 * g, 64), 64), :] = jnp.zeros((64, LANES), F32)
+        return carry
+
+    lax.fori_loop(0, add_left.shape[0] // 64, clear, 0)
     for n in range(2 * NV):
-        state[n, 0:8, :] = jnp.zeros((8, LANES), F32)
-        state[n, 8 + 8 * tiles : 16 + 8 * tiles, :] = jnp.zeros((8, LANES), F32)
+        above[n, 0:8, :] = jnp.zeros((8, LANES), F32)
+        below[n, 8 + 8 * tiles : 16 + 8 * tiles, :] = jnp.zeros((8, LANES), F32)
+
+    def scatter(d, carry):
+        for k in range(2):
+            for part, (rows, refs) in enumerate(((asked, plus), (sent, minus))):
+                row = pl.multiple_of(8 * rows[k, d], 8)
+                for h, ref in enumerate(refs):
+                    first = 28 * part + 14 * k + NV * h
+                    ref[pl.ds(row, NV), :] += message[d, first : first + NV, :]
+        return carry
+
+    for c in range(CHUNKS):
+        load(c).wait()
+        lax.fori_loop(c * count, (c + 1) * count, scatter, 0, unroll=4)
+
+    lane = lax.broadcasted_iota(I32, (8, COLS), 1)
 
     def sweep_one(t):
         rows = pl.ds(pl.multiple_of(8 * t, 8), 8)
-        cells = [start[v, rows, :] + added(sources, t, v) for v in range(NV)]
+        groups = [pl.ds(64 * t + 8 + v, 8, stride=8) for v in range(NV)]
+        source = [jnp.concatenate([p[g, :] - m[g, :] for p, m in zip(plus, minus)], axis=1) for g in groups]
+        cells = [start[v, rows, :] + source[v] for v in range(NV)]
         relaxed = apply_inv(lambda i, j: inv[i, j, rows, :], cells)
+        end = jnp.minimum(t, 1)
+        for v in range(NV):
+            ends[end, v] = relaxed[v]
+        wide = jnp.concatenate(relaxed + [jnp.zeros((8, COLS), F32)], axis=0)
+        high = wide.astype(BF16)
+        low = (wide - high.astype(F32)).astype(BF16)
+        mixed = jnp.dot(turn[...], jnp.concatenate([high, high, low], axis=0), preferred_element_type=F32)
+        piece = lambda d, v: mixed[8 * (NV * d + v) : 8 * (NV * d + v) + 8, :]
         for v in range(NV):
             for h in range(2):
-                state[2 * v + h, pl.ds(8 * t + 8, 8), :] = relaxed[v][:, LANES * h : LANES * (h + 1)]
+                half = slice(LANES * h, LANES * (h + 1))
+                above[2 * v + h, pl.ds(8 * t + 8, 8), :] = piece(0, v)[:, half]
+                below[2 * v + h, pl.ds(8 * t + 8, 8), :] = piece(1, v)[:, half]
+            west = jnp.where(lane == 0, 0.0, pltpu.roll(piece(2, v), 1, 1))
+            east = jnp.where(lane == COLS - 1, 0.0, pltpu.roll(piece(3, v), COLS - 1, 1))
+            right[v, rows, :] = right[v, rows, :] + source[v] - coef[2, rows, :] * west - coef[3, rows, :] * east
 
     def sweep_two(t):
         rows = pl.ds(pl.multiple_of(8 * t, 8), 8)
-        sums = coupled(state, pl.multiple_of(8 * t + 8, 8), lambda d: coef[d, rows, :], mix)
-        cells = [right[v, rows, :] + added(sources, t, v) - sums[8 * v : 8 * v + 8, :] for v in range(NV)]
+        cells = []
+        for v in range(NV):
+            north, south = (
+                jnp.concatenate([ref[2 * v + h, pl.ds(8 * t + 8 + shift, 8), :] for h in range(2)], axis=1)
+                for ref, shift in ((above, -1), (below, 1))
+            )
+            cells.append(right[v, rows, :] - coef[0, rows, :] * north - coef[1, rows, :] * south)
         relaxed = apply_inv(lambda i, j: inv[i, j, rows, :], cells)
         for v in range(NV):
             done[v, rows, :] = relaxed[v]
@@ -370,33 +355,38 @@
     lax.fori_loop(0, CHUNKS, step, 0)
     sweep_two(tiles - 1)
     store(CHUNKS - 1).start()
+    even = parity[0] == 0
+    for v in range(NV):
+        top, bottom = ends[0, v][0:1, :], ends[1, v][7:8, :]
+        out_a, out_b = jnp.where(even, bottom, top), jnp.where(even, top, bottom)
+        for h in range(2):
+            n = 2 * v + h
+            edge_a[n : n + 1, :] = out_a[:, LANES * h : LANES * (h + 1)]
+            edge_b[n : n + 1, :] = out_b[:, LANES * h : LANES * (h + 1)]
     for c in range(CHUNKS):
         store(c).wait()
 
 
-def sweeps(left, other, mix, start, right, coef, inv):
+def finish_sweeps(parity, sent, asked, turn, message, start, right, coef, inv):
     rows = start.shape[1]
+    sums = VMEM((8 * (rows + 8), LANES), F32)
+    padded = VMEM((2 * NV, rows + 16, LANES), F32)
+    like = lambda a: VMEM(a.shape, F32)
     return pl.pallas_call(
-        sweeps_kernel,
-        in_specs=[whole()] + [whole(pltpu.HBM)] * 6,
-        out_specs=whole(pltpu.HBM),
-        out_shape=jax.ShapeDtypeStruct(start.shape, F32),
-        scratch_shapes=[
-            VMEM((2 * NV, rows + 16, LANES), F32),
-            VMEM(start.shape, F32),
-            VMEM(left.shape, F32),
-            VMEM(left.shape, F32),
-            VMEM(start.shape, F32),
-            VMEM(start.shape, F32),
-            VMEM(coef.shape, F32),
-            VMEM(inv.shape, F32),
-            pltpu.SemaphoreType.DMA((6, CHUNKS)),
-            pltpu.SemaphoreType.DMA((CHUNKS,)),
-        ],
+        finish_kernel,
+        in_specs=[SMEM] * 3 + [whole()] + [whole(pltpu.HBM)] * 5,
+        out_specs=[whole(pltpu.HBM), whole(), whole()],
+        out_shape=[jax.ShapeDtypeStruct(s, F32) for s in (start.shape, (2 * NV, LANES), (2 * NV, LANES))],
+        scratch_shapes=[like(message)]
+        + [sums] * 4
+        + [like(a) for a in (start, right, coef, inv)]
+        + [padded] * 2
+        + [VMEM((2, NV, 8, COLS), F32), like(start)]
+        + [pltpu.SemaphoreType.DMA(s) for s in ((CHUNKS,), (4, CHUNKS), (CHUNKS,))],
         compiler_params=params(61),
         cost_estimate=cost(45_000_000, 24_000_000),
-        name="sweeps",
-    )(mix, left, other, start, right, coef, inv)
+        name="finish_sweeps",
+    )(parity, sent, asked, turn, message, start, right, coef, inv)
 
 
 def edge_kernel(parity, relaxed, coef, mix, inv, halo_a, halo_b, out):
@@ -452,11 +442,20 @@
     return lax.ppermute(edge_a, "blk", pairs_a), lax.ppermute(edge_b, "blk", pairs_b)
 
 
+def split(full):
+    high = lax.reduce_precision(full, exponent_bits=8, mantissa_bits=7)
+    return high.astype(BF16), (full - high).astype(BF16)
+
+
 def mixing(face_jacobian):
     wide = jnp.transpose(face_jacobian, (1, 0, 2)).reshape(NV, 4 * NV)
-    full = (wide[:, None, :, None] * jnp.eye(8, dtype=F32)[None, :, None, :]).reshape(8 * NV, 32 * NV)
-    high = lax.reduce_precision(full, exponent_bits=8, mantissa_bits=7)
-    return jnp.stack([high.astype(BF16), (full - high).astype(BF16)])
+    return jnp.stack(split((wide[:, None, :, None] * jnp.eye(8, dtype=F32)[None, :, None, :]).reshape(8 * NV, 32 * NV)))
+
+
+def turning(face_jacobian):
+    tall = jnp.pad(face_jacobian.reshape(4 * NV, NV), ((0, 0), (0, 1)))
+    high, low = split((tall[:, None, :, None] * jnp.eye(8, dtype=F32)[None, :, None, :]).reshape(32 * NV, 64))
+    return jnp.concatenate([high, low, high], axis=1)
 
 
 def body(flow_state, right_side, inv_diag, face_coef, face_jacobian, hole_owner, source_row, target_row, block_device):
@@ -477,11 +476,11 @@
 
     coef = jnp.transpose(face_coef[0], (1, 0, 2))
     mix = mixing(face_jacobian)
-    start, start_edges, inv_edges = first_sum(parity, flow, right, coef, mix, halo_a, halo_b, inv)
-
-    left, other, edge_a, edge_b = scatter(parity, sent, asked, message, start_edges, inv_edges, rows)
+    start, inv_edges = first_sum(parity, flow, right, coef, mix, halo_a, halo_b, inv)
+    relaxed, edge_a, edge_b = finish_sweeps(
+        parity, sent, asked, turning(face_jacobian), message, start, right, coef, inv
+    )
     halo_a, halo_b = exchange(edge_a, edge_b)
-    relaxed = sweeps(left, other, mix, start, right, coef, inv)
     relaxed = edge_rows(parity, relaxed, coef, mix, inv_edges, halo_a, halo_b)
     return jnp.transpose(relaxed, (1, 0, 2))[None]
 

time: 106 us -> 108 us (1.019)
  waiting for transfers between devices: 32.4 us -> 34.5 us
    ppermute x2, waiting for transfers between devices: 0.01 us -> 3.05 us  [exchange(): lax.ppermute(edge_b, 'blk', pairs_b)]
    pallas_call x2 -> x1, Pallas kernels: 16.1 us -> 15.8 us  [finish_sweeps(): pl.pallas_call(finish_kernel, in_specs=[SMEM] * 3 + [whole()] + [whole(pl...]
    unnamed x17 -> x19, local copies, waits for them, and re-layouts: 2.33 us -> 2 us
  transfers between devices with their start and end apart: 6 -> 6, of which waited for: 2 -> 3; matrix products, arithmetic and copies ran while one was open for 7% -> 8% of each run, Pallas kernels for 22% -> 12%
where the time goes in v2:
time: 108 us
  Pallas kernels  36.6 us (34%)
  waiting for transfers between devices  34.5 us (32%)
  starting transfers between devices  27 us (25%)
  local copies, waits for them, and re-layouts  6.72 us (6%)
  other arithmetic  2.59 us (2%)
    all_to_all x1, waiting for transfers between devices, body(): lax.all_to_all(message, AXES, split_axis=0, concat_axis=0, tiled=True)  30.6 us
    pallas_call x1, Pallas kernels, finish_sweeps(): pl.pallas_call(finish_kernel, in_specs=[SMEM] * 3 + [whole()] + [whole(pl...  15.8 us
    pallas_call x1, Pallas kernels, first_sum(): pl.pallas_call(first_kernel, in_specs=[SMEM] + [whole()] * 6 + [whole(plt...  12.5 us
    all_to_all x1, starting transfers between devices, body(): lax.all_to_all(asking, AXES, split_axis=0, concat_axis=0, tiled=True)  11.5 us
    all_to_all x1, starting transfers between devices, body(): lax.all_to_all(message, AXES, split_axis=0, concat_axis=0, tiled=True)  8.63 us
    ppermute x2, starting transfers between devices, exchange(): lax.ppermute(edge_b, 'blk', pairs_b)  4.68 us
    pallas_call x1, Pallas kernels, gather(): pl.pallas_call(gather_kernel, in_specs=[whole(pltpu.HBM), whole(), whole(...  4.6 us
    squeeze x1, local copies, waits for them, and re-layouts, body(): flow = jnp.transpose(flow_state[0], (1, 0, 2))  3.93 us
  transfers between devices with their start and end apart: 6, of which 3 were waited for; matrix products, arithmetic and copies ran while one was open for 8% of the time, Pallas kernels for 12%

profile of v2, /device:TPU:1, one launch (start us, length us, event | category | flops | bytes accessed | tf_op | source)
XLA Modules:
  0.0 107.6 jit_solution(16899225133979609319)
XLA Ops:
  0.0 1.8 %slot_tables.1 = (s32[2,128]{1,0:T(2,128)}, s32[128,1,128]{2,1,0:T(1,128)}) custom-call(s32[1,128]{1,0:T(1,128)} %bitcast.36, s32[1,128]{1,0:T(1,128)} %bitcast.37, s32[1,128]{1,0:T(1,128)} %bitcast.38, s32[1,128]{1,0:T(1,128)} %bitcast.39), custom_call_target="tpu_custom_call" | custom-call | flops 4000000 | bytes 100000 | tf_op jit(solution)/shard_map/slot_tables/pallas_call | solution.py:70
  1.8 11.5 %all-to-all-start = ((s32[128,1,128]{2,1,0:T(1,128)}), s32[128,1,128]{2,1,0:T(1,128)S(1)}, u32[]{:S(2)}, u32[]{:S(2)}) async-start(s32[128,1,128]{2,1,0:T(1,128)} %get-tuple-element.18), calls=%async_computation | async-start | bytes 131072 | tf_op jit(solution)/shard_map/all_to_all | solution.py:469
  13.3 0.9 fusion.3
  14.2 1.1 %collective-permute-start = (f32[14,128]{1,0:T(8,128)S(1)}, f32[14,128]{1,0:T(8,128)S(1)}, u32[]{:S(2)}, u32[]{:S(2)}) collective-permute-start(f32[14,128]{1,0:T(8,128)S(1)} %select_n.28), channel_id=1, source_target_pairs={{0,1},{1,0},{2,3},{3,2},{4,5},{5,4},{6,7},{7,6},{8,9},{9,8},{10,11... | collective-permute-start | bytes 21512 | tf_op jit(solution)/shard_map/ppermute | solution.py:442
  15.4 2.6 %collective-permute-start.1 = (f32[14,128]{1,0:T(8,128)S(1)}, f32[14,128]{1,0:T(8,128)S(1)}, u32[]{:S(2)}, u32[]{:S(2)}) collective-permute-start(f32[14,128]{1,0:T(8,128)S(1)} %select_n.30), channel_id=1, source_target_pairs={{1,2},{2,1},{3,4},{4,3},{5,6},{6,5},{7,8},{8,7},{9,10},{10,9},{11,... | collective-permute-start | bytes 21512 | tf_op jit(solution)/shard_map/ppermute | solution.py:442
  18.0 3.9 %copy.13.flow_in = f32[256,7,256]{2,1,0:T(8,128)} copy(f32[256,7,256]{2,0,1:T(8,128)} %bitcast.31) | data formatting | bytes 3670016 | tf_op jit(solution)/shard_map/squeeze | solution.py:462
  21.9 0.8 all-to-all-done.asked_in
  22.8 0.6 copy-done.4
  23.4 4.6 %gather.1 = (f32[128,56,128]{2,1,0:T(8,128)}, s32[2,128]{1,0:T(2,128)}) custom-call(s32[2,128]{1,0:T(2,128)} %get-tuple-element.17.sent_in.sent, s32[128,1,128]{2,1,0:T(1,128)} %copy-done.4, f32[256,7,256]{2,1,0:T(8,128)} %copy.13.flow_in), custom_call_target="tpu_custom_call" | custom-call | flops 1000000 | bytes 6000000 | tf_op jit(solution)/shard_map/gather/pallas_call | solution.py:126
  28.0 8.6 %all-to-all-start.1 = ((f32[128,56,128]{2,1,0:T(8,128)}), f32[128,56,128]{2,1,0:T(8,128)}, u32[]{:S(2)}, u32[]{:S(2)}) async-start(f32[128,56,128]{2,1,0:T(8,128)} %get-tuple-element.21), calls=%async_computation.1 | async-start | bytes 7340032 | tf_op jit(solution)/shard_map/all_to_all | solution.py:475
  36.9 0.3 mul.50
  37.2 0.2 broadcast_multiply_fusion
  37.4 0.4 mul.55
  37.8 0.2 copy-done.3
  38.0 1.2 %copy.21 = f32[1,256,4,256]{3,1,2,0:T(8,128)} copy(f32[1,256,4,256]{3,2,1,0:T(4,128)S(1)} %copy-done.3) | data formatting | bytes 2097152 | tf_op args[3]
  39.2 0.6 pad_maximum_fusion.1.mix
  39.8 0.7 pad_maximum_fusion.turn
  40.6 12.5 %first_sum.1 = (f32[7,256,256]{2,1,0:T(8,128)}, f32[2,7,7,8,256]{4,3,2,1,0:T(8,128)}) custom-call(s32[1]{0:T(128)} %bitcast.parity, f32[7,256,256]{2,1,0:T(8,128)} %bitcast.32, f32[7,256,256]{2,1,0:T(8,128)} %bitcast.33, f32[4,256,256]{2,1,0:T(8,128)} %bitcast.25, bf16[2,56,224]{2,1,0:T(8,128)(2,1)} %pad_maximum_fusion.1.mix, f32[14,128]{1,0:T(8,128)} %copy-done.6, ...), custom_call_target="tpu_custom_call" | custom-call | flops 30000000 | bytes 8000000 | tf_op jit(solution)/shard_map/first_sum/pallas_call | solution.py:213
  53.1 30.6 %all-to-all-done.1.message_in = f32[128,56,128]{2,1,0:T(8,128)} async-done(((f32[128,56,128]{2,1,0:T(8,128)}), f32[128,56,128]{2,1,0:T(8,128)}, u32[]{:S(2)}, u32[]{:S(2)}) %all-to-all-start.1) | async-done | bytes 3670048 | tf_op jit(solution)/shard_map/all_to_all | solution.py:475
  83.7 15.8 %finish_sweeps.1 = (f32[7,256,256]{2,1,0:T(8,128)}, f32[14,128]{1,0:T(8,128)}, f32[14,128]{1,0:T(8,128)}) custom-call(s32[1]{0:T(128)} %bitcast.parity, s32[2,128]{1,0:T(2,128)} %get-tuple-element.17.sent_in.sent, s32[2,128]{1,0:T(2,128)} %get-tuple-element.20.asked, bf16[224,192]{1,0:T(8,128)(2,1)} %pad_maximum_fusion.turn, ...), custom_call_target="tpu_custom_call" | custom-call | flops 45000000 | bytes 24000000 | tf_op jit(solution)/shard_map/finish_sweeps/pallas_call | solution.py:375
  99.5 1.0 collective-permute-start.2
  100.5 2.1 %collective-permute-start.3 = (f32[14,128]{1,0:T(8,128)}, f32[14,128]{1,0:T(8,128)S(1)}, u32[]{:S(2)}, u32[]{:S(2)}) collective-permute-start(f32[14,128]{1,0:T(8,128)} %get-tuple-element.28), channel_id=1, source_target_pairs={{1,2},{2,1},{3,4},{4,3},{5,6},{6,5},{7,8},{8,7},{9,10},{10,9},{11,... | collective-permute-start | bytes 21512 | tf_op jit(solution)/shard_map/ppermute | solution.py:442
  102.6 3.0 %collective-permute-done.3.halo_b = f32[14,128]{1,0:T(8,128)S(1)} collective-permute-done((f32[14,128]{1,0:T(8,128)}, f32[14,128]{1,0:T(8,128)S(1)}, u32[]{:S(2)}, u32[]{:S(2)}) %collective-permute-start.3) | collective-permute-done | bytes 7200 | tf_op jit(solution)/shard_map/ppermute | solution.py:442
  105.7 1.9 %edge_rows.1 = f32[7,256,256]{2,1,0:T(8,128)} custom-call(s32[1]{0:T(128)} %bitcast.parity, f32[7,256,256]{2,1,0:T(8,128)} %get-tuple-element.25.relaxed, f32[4,256,256]{2,1,0:T(8,128)S(1)} %bitcast.27, bf16[2,56,224]{2,1,0:T(8,128)(2,1)S(1)} %copy-done.2, f32[2,7,7,8,256]{4,3,2,1,0:T(8,128)S(1)} %copy-done.1, ...), custom_call_target="tpu_custom_call", output_to_operand_aliasing={{}: (1, {})} | custom-call | flops 100000 | bytes 900000 | tf_op jit(solution)/shard_map/edge_rows/pallas_call | solution.py:417
  (27 shorter events, 0.3 us)
Async XLA Ops:
  1.8 20.9 %all-to-all-start = ((s32[128,1,128]{2,1,0:T(1,128)}), s32[128,1,128]{2,1,0:T(1,128)S(1)}, u32[]{:S(2)}, u32[]{:S(2)}) async-start(s32[128,1,128]{2,1,0:T(1,128)} %get-tuple-element.18), calls=%async_computation | async-start | bytes 131072 | tf_op jit(solution)/shard_map/all_to_all | solution.py:469
  14.2 7.7 %collective-permute-start = (f32[14,128]{1,0:T(8,128)S(1)}, f32[14,128]{1,0:T(8,128)S(1)}, u32[]{:S(2)}, u32[]{:S(2)}) collective-permute-start(f32[14,128]{1,0:T(8,128)S(1)} %select_n.28), channel_id=1, source_target_pairs={{0,1},{1,0},{2,3},{3,2},{4,5},{5,4},{6,7},{7,6},{8,9},{9,8},{10,11... | collective-permute-start | bytes 21512 | tf_op jit(solution)/shard_map/ppermute | solution.py:442
  15.4 6.5 %collective-permute-start.1 = (f32[14,128]{1,0:T(8,128)S(1)}, f32[14,128]{1,0:T(8,128)S(1)}, u32[]{:S(2)}, u32[]{:S(2)}) collective-permute-start(f32[14,128]{1,0:T(8,128)S(1)} %select_n.30), channel_id=1, source_target_pairs={{1,2},{2,1},{3,4},{4,3},{5,6},{6,5},{7,8},{8,7},{9,10},{10,9},{11,... | collective-permute-start | bytes 21512 | tf_op jit(solution)/shard_map/ppermute | solution.py:442
  21.9 15.3 %copy-start.6 = (f32[14,128]{1,0:T(8,128)}, f32[14,128]{1,0:T(8,128)S(1)}, u32[]{:S(2)}) copy-start(f32[14,128]{1,0:T(8,128)S(1)} %collective-permute-done.halo_a) | copy-start | bytes 21508
  21.9 15.3 %copy-start.7 = (f32[14,128]{1,0:T(8,128)}, f32[14,128]{1,0:T(8,128)S(1)}, u32[]{:S(2)}) copy-start(f32[14,128]{1,0:T(8,128)S(1)} %collective-permute-done.1.halo_b) | copy-start | bytes 21508
  22.8 0.6 copy-start.4
  28.0 8.7 %copy-start.5 = (f32[4,7,7]{2,0,1:T(4,128)S(1)}, f32[4,7,7]{2,0,1:T(4,128)}, u32[]{:S(2)}) copy-start(f32[4,7,7]{2,0,1:T(4,128)} %param.13) | copy-start | bytes 2356
  28.0 55.7 %all-to-all-start.1 = ((f32[128,56,128]{2,1,0:T(8,128)}), f32[128,56,128]{2,1,0:T(8,128)}, u32[]{:S(2)}, u32[]{:S(2)}) async-start(f32[128,56,128]{2,1,0:T(8,128)} %get-tuple-element.21), calls=%async_computation.1 | async-start | bytes 7340032 | tf_op jit(solution)/shard_map/all_to_all | solution.py:475
  36.8 1.2 %copy-start.3 = (f32[1,256,4,256]{3,2,1,0:T(4,128)S(1)}, f32[1,256,4,256]{3,2,1,0:T(4,128)}, u32[]{:S(2)}) copy-start(f32[1,256,4,256]{3,2,1,0:T(4,128)} %param.12) | copy-start | bytes 3145732
  83.7 22.0 %copy-start = (f32[1,256,4,256]{3,1,2,0:T(8,128)S(1)}, f32[1,256,4,256]{3,1,2,0:T(8,128)}, u32[]{:S(2)}) copy-start(f32[1,256,4,256]{3,1,2,0:T(8,128)} %copy.21) | copy-start | bytes 3145732
  83.7 22.0 %copy-start.1 = (f32[2,7,7,8,256]{4,3,2,1,0:T(8,128)S(1)}, f32[2,7,7,8,256]{4,3,2,1,0:T(8,128)}, u32[]{:S(2)}) copy-start(f32[2,7,7,8,256]{4,3,2,1,0:T(8,128)} %get-tuple-element.26.inv) | copy-start | bytes 2408452
  83.7 22.0 %copy-start.2 = (bf16[2,56,224]{2,1,0:T(8,128)(2,1)S(1)}, bf16[2,56,224]{2,1,0:T(8,128)(2,1)}, u32[]{:S(2)}) copy-start(bf16[2,56,224]{2,1,0:T(8,128)(2,1)} %pad_maximum_fusion.1.mix) | copy-start | bytes 150532
  99.5 3.2 %collective-permute-start.2 = (f32[14,128]{1,0:T(8,128)}, f32[14,128]{1,0:T(8,128)S(1)}, u32[]{:S(2)}, u32[]{:S(2)}) collective-permute-start(f32[14,128]{1,0:T(8,128)} %get-tuple-element.27), channel_id=1, source_target_pairs={{0,1},{1,0},{2,3},{3,2},{4,5},{5,4},{6,7},{7,6},{8,9},{9,8},{10,11... | collective-permute-start | bytes 21512 | tf_op jit(solution)/shard_map/ppermute | solution.py:442
  100.5 5.2 %collective-permute-start.3 = (f32[14,128]{1,0:T(8,128)}, f32[14,128]{1,0:T(8,128)S(1)}, u32[]{:S(2)}, u32[]{:S(2)}) collective-permute-start(f32[14,128]{1,0:T(8,128)} %get-tuple-element.28), channel_id=1, source_target_pairs={{1,2},{2,1},{3,4},{4,3},{5,6},{6,5},{7,8},{8,7},{9,10},{10,9},{11,... | collective-permute-start | bytes 21512 | tf_op jit(solution)/shard_map/ppermute | solution.py:442

commit v3 on v2

--- a/solution.py
+++ b/solution.py
@@ -16,6 +16,8 @@
 SMEM = pl.BlockSpec(memory_space=pltpu.SMEM)
 MIB = 1 << 20
 CHUNKS = 8
+TILES = 4
+PACKED = 2 * NV + 4
 
 
 def params(mib):
@@ -89,22 +91,27 @@
         copy.wait()
 
 
-def gather_kernel(sent_in, asked_in, flow_in, message_out, asked_out, sent, asked, flow, packed, message, sems, out_sems):
+def gather_kernel(
+    parity, sent_in, asked_in, flow_in, message_out, tables_out, flow, sent, tables, table, message, sems, out_sems
+):
     n = message.shape[0]
     copies = [pltpu.make_async_copy(sent_in, sent, sems.at[0]), pltpu.make_async_copy(flow_in, flow, sems.at[1])]
     begin(copies)
     eye = lax.broadcasted_iota(I32, (n, n), 0) == lax.broadcasted_iota(I32, (n, n), 1)
-    table = asked_in[...].reshape(n, LANES).astype(F32)
+    columns = asked_in[...].reshape(n, LANES).astype(F32)
     for k in range(2):
-        packed[k : k + 1, :] = jnp.sum(jnp.where(eye, table[:, k : k + 1], 0.0), axis=0, keepdims=True).astype(I32)
-    tables = [pltpu.make_async_copy(packed, asked, sems.at[2]), pltpu.make_async_copy(packed, asked_out, sems.at[3])]
-    begin(tables)
-    finish(copies + tables)
+        tables[k : k + 1, :] = jnp.sum(jnp.where(eye, columns[:, k : k + 1], 0.0), axis=0, keepdims=True).astype(I32)
+    tables[4:8, :] = jnp.full((4, n), parity[0], I32)
+    copies[0].wait()
+    tables[2:4, :] = sent[...]
+    shared = [pltpu.make_async_copy(tables, table, sems.at[2]), pltpu.make_async_copy(tables, tables_out, sems.at[3])]
+    begin(shared)
+    finish(shared + copies[1:])
 
     def step(d, carry):
-        for part, rows in enumerate((sent, asked)):
+        for part in range(2):
             for k in range(2):
-                row = jnp.maximum(rows[k, d] - 1, 0)
+                row = jnp.maximum(table[2 - 2 * part + k, d] - 1, 0)
                 for h in range(2):
                     start = 28 * part + 14 * k + NV * h
                     message[d, start : start + NV, :] = flow[row, :, LANES * h : LANES * (h + 1)]
@@ -120,19 +127,19 @@
     finish(stores)
 
 
-def gather(sent, asked, flow):
+def gather(parity, sent, asked, flow):
     devices = asked.shape[0]
     message = (devices, 8 * NV, LANES)
     return pl.pallas_call(
         gather_kernel,
-        in_specs=[whole(pltpu.HBM), whole(), whole(pltpu.HBM)],
+        in_specs=[SMEM, whole(pltpu.HBM), whole(), whole(pltpu.HBM)],
         out_specs=[whole(pltpu.HBM)] * 2,
-        out_shape=[jax.ShapeDtypeStruct(message, F32), jax.ShapeDtypeStruct((2, devices), I32)],
+        out_shape=[jax.ShapeDtypeStruct(message, F32), jax.ShapeDtypeStruct((8, devices), I32)],
         scratch_shapes=[
-            pltpu.SMEM((2, devices), I32),
-            pltpu.SMEM((2, devices), I32),
             VMEM(flow.shape, F32),
             VMEM((2, devices), I32),
+            VMEM((8, devices), I32),
+            pltpu.SMEM((8, devices), I32),
             VMEM(message, F32),
             pltpu.SemaphoreType.DMA((4,)),
             pltpu.SemaphoreType.DMA((CHUNKS,)),
@@ -140,7 +147,7 @@
         compiler_params=params(58),
         cost_estimate=cost(1_000_000, 6_000_000),
         name="gather",
-    )(sent, asked, flow)
+    )(parity, sent, asked, flow)
 
 
 def coupled(state, row, coef, mix):
@@ -179,81 +186,105 @@
     return out
 
 
-def first_kernel(parity, flow, right, coef, mix, halo_a, halo_b, inv, start, inv_edges, state, sems):
-    tiles = right.shape[1] // 8
-    copies = [
-        pltpu.make_async_copy(inv.at[:, :, 8 * t : 8 * t + 8, :], inv_edges.at[g], sems.at[g])
-        for g, t in enumerate((0, tiles - 1))
-    ]
-    for copy in copies:
-        copy.start()
+def first_kernel(
+    parity, flow, mix, halo_a, halo_b, right, coef, inv, packed_out, inv_out, inv_edges, state, packed, blocks, sems
+):
+    rows = 8 * TILES
+    steps = flow.shape[1] // rows
     even = parity[0] == 0
+    reads, writes = [], []
+    for c in range(steps):
+        part = pl.ds(rows * c, rows)
+        reads.append(
+            [
+                pltpu.make_async_copy(right.at[:, part, :], packed.at[c, NV : 2 * NV], sems.at[0, c]),
+                pltpu.make_async_copy(coef.at[:, part, :], packed.at[c, 2 * NV : PACKED], sems.at[1, c]),
+                pltpu.make_async_copy(inv.at[:, :, part, :], blocks.at[c], sems.at[2, c]),
+            ]
+        )
+        begin(reads[c])
     for n in range(2 * NV):
         v, h = divmod(n, 2)
         a, b = halo_a[n : n + 1, :], halo_b[n : n + 1, :]
         state[n, 7:8, :] = jnp.where(even, b, a)
-        state[n, 8 + 8 * tiles : 9 + 8 * tiles, :] = jnp.where(even, a, b)
-        state[n, 8 : 8 + 8 * tiles, :] = flow[v, :, LANES * h : LANES * (h + 1)]
-
-    def step(t, carry):
-        row = pl.multiple_of(8 * t, 8)
-        sums = coupled(state, row + 8, lambda d: coef[d, pl.ds(row, 8), :], mix)
-        for v in range(NV):
-            start[v, pl.ds(row, 8), :] = right[v, pl.ds(row, 8), :] - sums[8 * v : 8 * v + 8, :]
-        return carry
-
-    lax.fori_loop(0, tiles, step, 0)
-    for copy in copies:
-        copy.wait()
+        state[n, 8 + rows * steps : 9 + rows * steps, :] = jnp.where(even, a, b)
+        state[n, 8 : 8 + rows * steps, :] = flow[v, :, LANES * h : LANES * (h + 1)]
+
+    for c in range(steps):
+        finish(reads[c])
+
+        def step(k, carry, c=c):
+            here = pl.ds(pl.multiple_of(8 * k, 8), 8)
+            row = pl.multiple_of(rows * c + 8 + 8 * k, 8)
+            sums = coupled(state, row, lambda d: packed[c, 2 * NV + d, here, :], mix)
+            for v in range(NV):
+                packed[c, v, here, :] = packed[c, NV + v, here, :] - sums[8 * v : 8 * v + 8, :]
+            return carry
+
+        lax.fori_loop(0, TILES, step, 0)
+        writes += [
+            pltpu.make_async_copy(packed.at[c], packed_out.at[c], sems.at[3, c]),
+            pltpu.make_async_copy(blocks.at[c], inv_out.at[c], sems.at[4, c]),
+        ]
+        begin(writes[-2:])
+    inv_edges[0] = blocks[0, :, :, 0:8, :]
+    inv_edges[1] = blocks[steps - 1, :, :, rows - 8 : rows, :]
+    finish(writes)
 
 
 def first_sum(parity, flow, right, coef, mix, halo_a, halo_b, inv):
     rows = flow.shape[1]
-    shapes = (flow.shape, (2, NV, NV, 8, COLS))
+    steps = rows // (8 * TILES)
+    packed = (steps, PACKED, 8 * TILES, COLS)
+    blocks = (steps, NV, NV, 8 * TILES, COLS)
     return pl.pallas_call(
         first_kernel,
-        in_specs=[SMEM] + [whole()] * 6 + [whole(pltpu.HBM)],
-        out_specs=[whole()] * 2,
-        out_shape=[jax.ShapeDtypeStruct(s, F32) for s in shapes],
-        scratch_shapes=[VMEM((2 * NV, rows + 16, LANES), F32), pltpu.SemaphoreType.DMA((2,))],
+        in_specs=[SMEM] + [whole()] * 4 + [whole(pltpu.HBM)] * 3,
+        out_specs=[whole(pltpu.HBM)] * 2 + [whole()],
+        out_shape=[jax.ShapeDtypeStruct(s, F32) for s in (packed, blocks, (2, NV, NV, 8, COLS))],
+        scratch_shapes=[
+            VMEM((2 * NV, rows + 16, LANES), F32),
+            VMEM(packed, F32),
+            VMEM(blocks, F32),
+            pltpu.SemaphoreType.DMA((5, steps)),
+        ],
         compiler_params=params(61),
-        cost_estimate=cost(30_000_000, 8_000_000),
+        cost_estimate=cost(30_000_000, 40_000_000),
         name="first_sum",
-    )(parity, flow, right, coef, mix, halo_a, halo_b, inv)
+    )(parity, flow, mix, halo_a, halo_b, right, coef, inv)
 
 
 def finish_kernel(
-    parity,
-    sent,
-    asked,
-    turn,
+    table_in,
+    turn_in,
     message_in,
-    start_in,
-    right_in,
-    coef_in,
+    packed_in,
     inv_in,
     out,
-    edge_a,
-    edge_b,
+    edge_a_out,
+    edge_b_out,
+    table,
+    turn,
     message,
     add_left,
     add_right,
     sub_left,
     sub_right,
-    start,
-    right,
-    coef,
+    packed,
     inv,
     above,
     below,
     ends,
     done,
+    edge_a,
+    edge_b,
     message_sems,
     sems,
     out_sems,
+    small_sems,
 ):
-    tiles = start.shape[1] // 8
-    size = tiles // CHUNKS
+    steps = packed_in.shape[0]
+    rows = 8 * TILES
     count = message.shape[0] // CHUNKS
     plus, minus = (add_left, add_right), (sub_left, sub_right)
 
@@ -262,21 +293,19 @@
         return pltpu.make_async_copy(message_in.at[part], message.at[part], message_sems.at[c])
 
     def fetch(c):
-        rows = pl.ds(pl.multiple_of(8 * size * c, 8), 8 * size)
-        streams = ((start_in, start), (right_in, right), (coef_in, coef))
-        copies = [
-            pltpu.make_async_copy(ref.at[:, rows, :], part.at[:, rows, :], sems.at[n, c])
-            for n, (ref, part) in enumerate(streams)
+        return [
+            pltpu.make_async_copy(packed_in.at[c], packed.at[c + 1], sems.at[0, c]),
+            pltpu.make_async_copy(inv_in.at[c], inv.at[c + 1], sems.at[1, c]),
         ]
-        return copies + [pltpu.make_async_copy(inv_in.at[:, :, rows, :], inv.at[:, :, rows, :], sems.at[3, c])]
 
     def store(c):
-        rows = pl.ds(pl.multiple_of(8 * size * c, 8), 8 * size)
-        return pltpu.make_async_copy(done.at[:, rows, :], out.at[:, rows, :], out_sems.at[c])
-
+        part = pl.ds(pl.multiple_of(rows * c, rows), rows)
+        return pltpu.make_async_copy(done.at[c + 1], out.at[:, part, :], out_sems.at[c])
+
+    small = [pltpu.make_async_copy(table_in, table, small_sems.at[0]), pltpu.make_async_copy(turn_in, turn, small_sems.at[1])]
+    begin(small)
     begin([load(c) for c in range(CHUNKS)])
-    for c in range(CHUNKS):
-        begin(fetch(c))
+    begin(fetch(0))
 
     def clear(g, carry):
         for ref in plus + minus:
@@ -285,66 +314,82 @@
 
     lax.fori_loop(0, add_left.shape[0] // 64, clear, 0)
     for n in range(2 * NV):
-        above[n, 0:8, :] = jnp.zeros((8, LANES), F32)
-        below[n, 8 + 8 * tiles : 16 + 8 * tiles, :] = jnp.zeros((8, LANES), F32)
+        above[n, rows : rows + 8, :] = jnp.zeros((8, LANES), F32)
+        below[n, 8 + rows * (steps + 1) : 16 + rows * (steps + 1), :] = jnp.zeros((8, LANES), F32)
 
     def scatter(d, carry):
         for k in range(2):
-            for part, (rows, refs) in enumerate(((asked, plus), (sent, minus))):
-                row = pl.multiple_of(8 * rows[k, d], 8)
+            for part, refs in enumerate((plus, minus)):
+                row = pl.multiple_of(8 * table[2 * part + k, d], 8)
                 for h, ref in enumerate(refs):
                     first = 28 * part + 14 * k + NV * h
                     ref[pl.ds(row, NV), :] += message[d, first : first + NV, :]
         return carry
 
+    finish(small)
     for c in range(CHUNKS):
         load(c).wait()
+        if c in (2, 6):
+            begin(fetch(1 if c == 2 else 2))
         lax.fori_loop(c * count, (c + 1) * count, scatter, 0, unroll=4)
 
     lane = lax.broadcasted_iota(I32, (8, COLS), 1)
 
-    def sweep_one(t):
-        rows = pl.ds(pl.multiple_of(8 * t, 8), 8)
-        groups = [pl.ds(64 * t + 8 + v, 8, stride=8) for v in range(NV)]
+    def sweep_one(c, k):
+        here = slice(8 * k, 8 * k + 8)
+        base = pl.multiple_of(64 * TILES * c, 64)
+        groups = [pl.ds(base + 64 * k + 8 + v, 8, stride=8) for v in range(NV)]
         source = [jnp.concatenate([p[g, :] - m[g, :] for p, m in zip(plus, minus)], axis=1) for g in groups]
-        cells = [start[v, rows, :] + source[v] for v in range(NV)]
-        relaxed = apply_inv(lambda i, j: inv[i, j, rows, :], cells)
-        end = jnp.minimum(t, 1)
-        for v in range(NV):
-            ends[end, v] = relaxed[v]
+        cells = [packed[c + 1, v, here, :] + source[v] for v in range(NV)]
+        relaxed = apply_inv(lambda i, j: inv[c + 1, i, j, here, :], cells)
+        if k in (0, TILES - 1):
+            end = jnp.minimum(c, 1) if k == 0 else 2
+            for v in range(NV):
+                ends[end, v] = relaxed[v]
         wide = jnp.concatenate(relaxed + [jnp.zeros((8, COLS), F32)], axis=0)
         high = wide.astype(BF16)
         low = (wide - high.astype(F32)).astype(BF16)
         mixed = jnp.dot(turn[...], jnp.concatenate([high, high, low], axis=0), preferred_element_type=F32)
         piece = lambda d, v: mixed[8 * (NV * d + v) : 8 * (NV * d + v) + 8, :]
+        first = pl.multiple_of(rows * (c + 1), rows)
         for v in range(NV):
             for h in range(2):
                 half = slice(LANES * h, LANES * (h + 1))
-                above[2 * v + h, pl.ds(8 * t + 8, 8), :] = piece(0, v)[:, half]
-                below[2 * v + h, pl.ds(8 * t + 8, 8), :] = piece(1, v)[:, half]
+                above[2 * v + h, pl.ds(first + 8 * k + 8, 8), :] = piece(0, v)[:, half]
+                below[2 * v + h, pl.ds(first + 8 * k + 8, 8), :] = piece(1, v)[:, half]
             west = jnp.where(lane == 0, 0.0, pltpu.roll(piece(2, v), 1, 1))
             east = jnp.where(lane == COLS - 1, 0.0, pltpu.roll(piece(3, v), COLS - 1, 1))
-            right[v, rows, :] = right[v, rows, :] + source[v] - coef[2, rows, :] * west - coef[3, rows, :] * east
-
-    def sweep_two(t):
-        rows = pl.ds(pl.multiple_of(8 * t, 8), 8)
+            share = packed[c + 1, 2 * NV + 2, here, :] * west + packed[c + 1, 2 * NV + 3, here, :] * east
+            packed[c + 1, NV + v, here, :] = packed[c + 1, NV + v, here, :] + source[v] - share
+
+    def sweep_two(c, k):
+        c, k = (c, k - 1) if k else (c - 1, TILES - 1)
+        here = slice(8 * k, 8 * k + 8)
+        first = rows * (c + 1)
         cells = []
         for v in range(NV):
             north, south = (
-                jnp.concatenate([ref[2 * v + h, pl.ds(8 * t + 8 + shift, 8), :] for h in range(2)], axis=1)
+                jnp.concatenate([ref[2 * v + h, pl.ds(first + 8 * k + 8 + shift, 8), :] for h in range(2)], axis=1)
                 for ref, shift in ((above, -1), (below, 1))
             )
-            cells.append(right[v, rows, :] - coef[0, rows, :] * north - coef[1, rows, :] * south)
-        relaxed = apply_inv(lambda i, j: inv[i, j, rows, :], cells)
+            share = packed[c + 1, 2 * NV, here, :] * north + packed[c + 1, 2 * NV + 1, here, :] * south
+            cells.append(packed[c + 1, NV + v, here, :] - share)
+        relaxed = apply_inv(lambda i, j: inv[c + 1, i, j, here, :], cells)
         for v in range(NV):
-            done[v, rows, :] = relaxed[v]
+            done[c + 1, v, here, :] = relaxed[v]
 
     def step(c, carry):
         finish(fetch(c))
-        for k in range(size):
-            t = c * size + k
-            sweep_one(t)
-            sweep_two(jnp.maximum(t - 1, 0))
+
+        @pl.when(c + 3 < steps)
+        def _():
+            begin(fetch(c + 3))
+
+        for k in range(0, TILES, 2):
+            sweep_one(c, k)
+            sweep_one(c, k + 1)
+            sweep_two(c, k)
+            sweep_two(c, k + 1)
 
         @pl.when(c > 0)
         def _():
@@ -352,41 +397,49 @@
 
         return carry
 
-    lax.fori_loop(0, CHUNKS, step, 0)
-    sweep_two(tiles - 1)
-    store(CHUNKS - 1).start()
-    even = parity[0] == 0
+    lax.fori_loop(0, steps, step, 0)
+    sweep_two(steps, 0)
+    store(steps - 1).start()
+    even = table[4, 0] == 0
     for v in range(NV):
-        top, bottom = ends[0, v][0:1, :], ends[1, v][7:8, :]
+        top, bottom = ends[0, v][0:1, :], ends[2, v][7:8, :]
         out_a, out_b = jnp.where(even, bottom, top), jnp.where(even, top, bottom)
         for h in range(2):
             n = 2 * v + h
             edge_a[n : n + 1, :] = out_a[:, LANES * h : LANES * (h + 1)]
             edge_b[n : n + 1, :] = out_b[:, LANES * h : LANES * (h + 1)]
-    for c in range(CHUNKS):
+    edges = [
+        pltpu.make_async_copy(edge_a, edge_a_out, small_sems.at[2]),
+        pltpu.make_async_copy(edge_b, edge_b_out, small_sems.at[3]),
+    ]
+    begin(edges)
+    for c in range(steps):
         store(c).wait()
-
-
-def finish_sweeps(parity, sent, asked, turn, message, start, right, coef, inv):
-    rows = start.shape[1]
+    finish(edges)
+
+
+def finish_sweeps(tables, turn, message, packed, inv):
+    steps = packed.shape[0]
+    rows = 8 * TILES * steps
     sums = VMEM((8 * (rows + 8), LANES), F32)
-    padded = VMEM((2 * NV, rows + 16, LANES), F32)
-    like = lambda a: VMEM(a.shape, F32)
+    padded = VMEM((2 * NV, rows + 8 * TILES + 16, LANES), F32)
+    slab = (NV, rows, COLS)
     return pl.pallas_call(
         finish_kernel,
-        in_specs=[SMEM] * 3 + [whole()] + [whole(pltpu.HBM)] * 5,
-        out_specs=[whole(pltpu.HBM), whole(), whole()],
-        out_shape=[jax.ShapeDtypeStruct(s, F32) for s in (start.shape, (2 * NV, LANES), (2 * NV, LANES))],
-        scratch_shapes=[like(message)]
+        in_specs=[whole(pltpu.HBM)] * 5,
+        out_specs=[whole(pltpu.HBM)] * 3,
+        out_shape=[jax.ShapeDtypeStruct(s, F32) for s in (slab, (2 * NV, LANES), (2 * NV, LANES))],
+        scratch_shapes=[pltpu.SMEM(tables.shape, I32), VMEM(turn.shape, BF16), VMEM(message.shape, F32)]
         + [sums] * 4
-        + [like(a) for a in (start, right, coef, inv)]
+        + [VMEM((steps + 1,) + a.shape[1:], F32) for a in (packed, inv)]
         + [padded] * 2
-        + [VMEM((2, NV, 8, COLS), F32), like(start)]
-        + [pltpu.SemaphoreType.DMA(s) for s in ((CHUNKS,), (4, CHUNKS), (CHUNKS,))],
+        + [VMEM((3, NV, 8, COLS), F32), VMEM((steps + 1, NV, 8 * TILES, COLS), F32)]
+        + [VMEM((2 * NV, LANES), F32)] * 2
+        + [pltpu.SemaphoreType.DMA(s) for s in ((CHUNKS,), (2, steps), (steps,), (4,))],
         compiler_params=params(61),
         cost_estimate=cost(45_000_000, 24_000_000),
         name="finish_sweeps",
-    )(parity, sent, asked, turn, message, start, right, coef, inv)
+    )(tables, turn, message, packed, inv)
 
 
 def edge_kernel(parity, relaxed, coef, mix, inv, halo_a, halo_b, out):
@@ -471,14 +524,14 @@
     even = parity[0] == 0
     halo_a, halo_b = exchange(jnp.where(even, bottom, top), jnp.where(even, top, bottom))
     asked, halo_a, halo_b = lax.optimization_barrier((asked, halo_a, halo_b))
-    message, asked = gather(sent, asked, flow_state[0])
+    message, tables = gather(parity, sent, asked, flow_state[0])
     message = lax.all_to_all(message, AXES, split_axis=0, concat_axis=0, tiled=True)
 
     coef = jnp.transpose(face_coef[0], (1, 0, 2))
     mix = mixing(face_jacobian)
-    start, inv_edges = first_sum(parity, flow, right, coef, mix, halo_a, halo_b, inv)
+    packed, blocks, inv_edges = first_sum(parity, flow, right, coef, mix, halo_a, halo_b, inv)
     relaxed, edge_a, edge_b = finish_sweeps(
-        parity, sent, asked, turning(face_jacobian), message, start, right, coef, inv
+        tables, turning(face_jacobian), message, packed, blocks
     )
     halo_a, halo_b = exchange(edge_a, edge_b)
     relaxed = edge_rows(parity, relaxed, coef, mix, inv_edges, halo_a, halo_b)

time: 108 us -> 103 us (0.954)
  waiting for transfers between devices: 34.5 us -> 31.6 us
  Pallas kernels: 36.6 us -> 34.1 us
    all_to_all x1, waiting for transfers between devices: 30.6 us -> 27.7 us  [body(): lax.all_to_all(message, AXES, split_axis=0, concat_axis=0, tiled=True)]
    pallas_call x3, Pallas kernels: 32.9 us -> 30.4 us  [the longest x1 15.4 us: first_sum(): pl.pallas_call(first_kernel, in_specs=[SMEM] + [whole()] * 4 + [whole(plt...]
  transfers between devices with their start and end apart: 6 -> 6, of which waited for: 3 -> 3; matrix products, arithmetic and copies ran while one was open for 8% -> 8% of each run, Pallas kernels for 12% -> 15%
where the time goes in v3:
time: 103 us; the launch traced here: 102 us
  Pallas kernels  34.1 us (33%)
  waiting for transfers between devices  31.6 us (31%)
  starting transfers between devices  27 us (26%)
  local copies, waits for them, and re-layouts  6.69 us (6%)
  other arithmetic  2.59 us (3%)
    all_to_all x1, waiting for transfers between devices, body(): lax.all_to_all(message, AXES, split_axis=0, concat_axis=0, tiled=True)  27.7 us
    pallas_call x1, Pallas kernels, first_sum(): pl.pallas_call(first_kernel, in_specs=[SMEM] + [whole()] * 4 + [whole(plt...  15.4 us
    all_to_all x1, starting transfers between devices, body(): lax.all_to_all(asking, AXES, split_axis=0, concat_axis=0, tiled=True)  11.5 us
    pallas_call x1, Pallas kernels, finish_sweeps(): pl.pallas_call(finish_kernel, in_specs=[whole(pltpu.HBM)] * 5, out_specs=...  10.3 us
    all_to_all x1, starting transfers between devices, body(): lax.all_to_all(message, AXES, split_axis=0, concat_axis=0, tiled=True)  8.64 us
    ppermute x2, starting transfers between devices, exchange(): lax.ppermute(edge_b, 'blk', pairs_b)  4.7 us
    pallas_call x1, Pallas kernels, gather(): pl.pallas_call(gather_kernel, in_specs=[SMEM, whole(pltpu.HBM), whole(),...  4.63 us
    squeeze x1, local copies, waits for them, and re-layouts, body(): flow = jnp.transpose(flow_state[0], (1, 0, 2))  3.93 us
  transfers between devices with their start and end apart: 6, of which 3 were waited for; matrix products, arithmetic and copies ran while one was open for 8% of the time, Pallas kernels for 15%

profile of v3, /device:TPU:1, one launch (start us, length us, event | category | flops | bytes accessed | tf_op | source)
XLA Modules:
  0.0 102.2 jit_solution(1638003881052743550)
XLA Ops:
  0.0 1.8 %slot_tables.1 = (s32[2,128]{1,0:T(2,128)}, s32[128,1,128]{2,1,0:T(1,128)}) custom-call(s32[1,128]{1,0:T(1,128)} %bitcast.33, s32[1,128]{1,0:T(1,128)} %bitcast.34, s32[1,128]{1,0:T(1,128)} %bitcast.35, s32[1,128]{1,0:T(1,128)} %bitcast.36), custom_call_target="tpu_custom_call" | custom-call | flops 4000000 | bytes 100000 | tf_op jit(solution)/shard_map/slot_tables/pallas_call | solution.py:72
  1.8 11.5 %all-to-all-start = ((s32[128,1,128]{2,1,0:T(1,128)}), s32[128,1,128]{2,1,0:T(1,128)S(1)}, u32[]{:S(2)}, u32[]{:S(2)}) async-start(s32[128,1,128]{2,1,0:T(1,128)} %get-tuple-element.19), calls=%async_computation | async-start | bytes 131072 | tf_op jit(solution)/shard_map/all_to_all | solution.py:522
  13.3 0.9 fusion.3
  14.2 1.1 %collective-permute-start = (f32[14,128]{1,0:T(8,128)S(1)}, f32[14,128]{1,0:T(8,128)S(1)}, u32[]{:S(2)}, u32[]{:S(2)}) collective-permute-start(f32[14,128]{1,0:T(8,128)S(1)} %select_n.28), channel_id=1, source_target_pairs={{0,1},{1,0},{2,3},{3,2},{4,5},{5,4},{6,7},{7,6},{8,9},{9,8},{10,11... | collective-permute-start | bytes 21512 | tf_op jit(solution)/shard_map/ppermute | solution.py:495
  15.4 2.6 %collective-permute-start.1 = (f32[14,128]{1,0:T(8,128)S(1)}, f32[14,128]{1,0:T(8,128)S(1)}, u32[]{:S(2)}, u32[]{:S(2)}) collective-permute-start(f32[14,128]{1,0:T(8,128)S(1)} %select_n.30), channel_id=1, source_target_pairs={{1,2},{2,1},{3,4},{4,3},{5,6},{6,5},{7,8},{8,7},{9,10},{10,9},{11,... | collective-permute-start | bytes 21512 | tf_op jit(solution)/shard_map/ppermute | solution.py:495
  18.0 3.9 %copy.13.flow_in = f32[256,7,256]{2,1,0:T(8,128)} copy(f32[256,7,256]{2,0,1:T(8,128)} %bitcast.29) | data formatting | bytes 3670016 | tf_op jit(solution)/shard_map/squeeze | solution.py:515
  21.9 0.8 all-to-all-done.asked_in
  22.8 0.6 copy-done.4
  23.4 4.6 %gather.1 = (f32[128,56,128]{2,1,0:T(8,128)}, s32[8,128]{1,0:T(8,128)}) custom-call(s32[1]{0:T(128)} %bitcast.parity, s32[2,128]{1,0:T(2,128)} %get-tuple-element.18.sent_in, s32[128,1,128]{2,1,0:T(1,128)} %copy-done.4, f32[256,7,256]{2,1,0:T(8,128)} %copy.13.flow_in), custom_call_target="tpu_custom_call" | custom-call | flops 1000000 | bytes 6000000 | tf_op jit(solution)/shard_map/gather/pallas_call | solution.py:133
  28.1 8.6 %all-to-all-start.1 = ((f32[128,56,128]{2,1,0:T(8,128)}), f32[128,56,128]{2,1,0:T(8,128)}, u32[]{:S(2)}, u32[]{:S(2)}) async-start(f32[128,56,128]{2,1,0:T(8,128)} %get-tuple-element.22), calls=%async_computation.1 | async-start | bytes 7340032 | tf_op jit(solution)/shard_map/all_to_all | solution.py:528
  36.8 0.1 broadcast_multiply_fusion.1
  37.0 0.3 mul.50
  37.3 0.2 broadcast_multiply_fusion
  37.4 0.4 mul.55
  37.9 1.2 %copy.21 = f32[1,256,4,256]{3,1,2,0:T(8,128)} copy(f32[1,256,4,256]{3,2,1,0:T(4,128)S(1)} %copy-done.3) | data formatting | bytes 2097152 | tf_op args[3]
  39.2 0.6 pad_maximum_fusion.1.mix
  39.8 0.8 pad_maximum_fusion.turn_in
  40.6 15.4 %first_sum.1 = (f32[8,18,32,256]{3,2,1,0:T(8,128)}, f32[8,7,7,32,256]{4,3,2,1,0:T(8,128)}, f32[2,7,7,8,256]{4,3,2,1,0:T(8,128)}) custom-call(s32[1]{0:T(128)} %bitcast.parity, f32[7,256,256]{2,1,0:T(8,128)} %bitcast.30, bf16[2,56,224]{2,1,0:T(8,128)(2,1)} %pad_maximum_fusion.1.mix, f32[14,128]{1,0:T(8,128)} %copy-done.6, f32[14,128]{1,0:T(8,128)} %copy-done.7, ...), custom_call_target="tpu_custom_call" | custom-call | flops 30000000 | bytes 40000000 | tf_op jit(solution)/shard_map/first_sum/pallas_call | solution.py:240
  56.0 27.7 %all-to-all-done.1.message_in = f32[128,56,128]{2,1,0:T(8,128)} async-done(((f32[128,56,128]{2,1,0:T(8,128)}), f32[128,56,128]{2,1,0:T(8,128)}, u32[]{:S(2)}, u32[]{:S(2)}) %all-to-all-start.1) | async-done | bytes 3670048 | tf_op jit(solution)/shard_map/all_to_all | solution.py:528
  83.7 10.3 %finish_sweeps.1 = (f32[7,256,256]{2,1,0:T(8,128)}, f32[14,128]{1,0:T(8,128)}, f32[14,128]{1,0:T(8,128)}) custom-call(s32[8,128]{1,0:T(8,128)} %get-tuple-element.21.table_in, bf16[224,192]{1,0:T(8,128)(2,1)} %pad_maximum_fusion.turn_in, f32[128,56,128]{2,1,0:T(8,128)} %all-to-all-done.1.message_in, f32[8,18,32,256]{3,2,1,0:T(8,128)} %get-tuple-element.25.packed_in, ...), custom_call_target="tpu_custom_call" | custom-call | flops 45000000 | bytes 24000000 | tf_op jit(solution)/shard_map/finish_sweeps/pallas_call | solution.py:427
  94.1 1.0 collective-permute-start.2
  95.1 2.1 %collective-permute-start.3 = (f32[14,128]{1,0:T(8,128)}, f32[14,128]{1,0:T(8,128)S(1)}, u32[]{:S(2)}, u32[]{:S(2)}) collective-permute-start(f32[14,128]{1,0:T(8,128)} %get-tuple-element.30), channel_id=1, source_target_pairs={{1,2},{2,1},{3,4},{4,3},{5,6},{6,5},{7,8},{8,7},{9,10},{10,9},{11,... | collective-permute-start | bytes 21512 | tf_op jit(solution)/shard_map/ppermute | solution.py:495
  97.3 3.0 %collective-permute-done.3.halo_b = f32[14,128]{1,0:T(8,128)S(1)} collective-permute-done((f32[14,128]{1,0:T(8,128)}, f32[14,128]{1,0:T(8,128)S(1)}, u32[]{:S(2)}, u32[]{:S(2)}) %collective-permute-start.3) | collective-permute-done | bytes 7200 | tf_op jit(solution)/shard_map/ppermute | solution.py:495
  100.3 1.9 %edge_rows.1 = f32[7,256,256]{2,1,0:T(8,128)} custom-call(s32[1]{0:T(128)} %bitcast.parity, f32[7,256,256]{2,1,0:T(8,128)} %get-tuple-element.27.relaxed, f32[4,256,256]{2,1,0:T(8,128)S(1)} %bitcast.26, bf16[2,56,224]{2,1,0:T(8,128)(2,1)S(1)} %copy-done.2, f32[2,7,7,8,256]{4,3,2,1,0:T(8,128)S(1)} %copy-done.1, ...), custom_call_target="tpu_custom_call", output_to_operand_aliasing={{}: (1, {})} | custom-call | flops 100000 | bytes 900000 | tf_op jit(solution)/shard_map/edge_rows/pallas_call | solution.py:470
  (27 shorter events, 0.2 us)
Async XLA Ops:
  1.8 20.9 %all-to-all-start = ((s32[128,1,128]{2,1,0:T(1,128)}), s32[128,1,128]{2,1,0:T(1,128)S(1)}, u32[]{:S(2)}, u32[]{:S(2)}) async-start(s32[128,1,128]{2,1,0:T(1,128)} %get-tuple-element.19), calls=%async_computation | async-start | bytes 131072 | tf_op jit(solution)/shard_map/all_to_all | solution.py:522
  14.2 7.7 %collective-permute-start = (f32[14,128]{1,0:T(8,128)S(1)}, f32[14,128]{1,0:T(8,128)S(1)}, u32[]{:S(2)}, u32[]{:S(2)}) collective-permute-start(f32[14,128]{1,0:T(8,128)S(1)} %select_n.28), channel_id=1, source_target_pairs={{0,1},{1,0},{2,3},{3,2},{4,5},{5,4},{6,7},{7,6},{8,9},{9,8},{10,11... | collective-permute-start | bytes 21512 | tf_op jit(solution)/shard_map/ppermute | solution.py:495
  15.4 6.5 %collective-permute-start.1 = (f32[14,128]{1,0:T(8,128)S(1)}, f32[14,128]{1,0:T(8,128)S(1)}, u32[]{:S(2)}, u32[]{:S(2)}) collective-permute-start(f32[14,128]{1,0:T(8,128)S(1)} %select_n.30), channel_id=1, source_target_pairs={{1,2},{2,1},{3,4},{4,3},{5,6},{6,5},{7,8},{8,7},{9,10},{10,9},{11,... | collective-permute-start | bytes 21512 | tf_op jit(solution)/shard_map/ppermute | solution.py:495
  21.9 16.0 %copy-start.6 = (f32[14,128]{1,0:T(8,128)}, f32[14,128]{1,0:T(8,128)S(1)}, u32[]{:S(2)}) copy-start(f32[14,128]{1,0:T(8,128)S(1)} %collective-permute-done.halo_a) | copy-start | bytes 21508
  21.9 15.9 %copy-start.7 = (f32[14,128]{1,0:T(8,128)}, f32[14,128]{1,0:T(8,128)S(1)}, u32[]{:S(2)}) copy-start(f32[14,128]{1,0:T(8,128)S(1)} %collective-permute-done.1.halo_b) | copy-start | bytes 21508
  22.8 0.6 copy-start.4
  28.1 8.7 %copy-start.5 = (f32[4,7,7]{2,0,1:T(4,128)S(1)}, f32[4,7,7]{2,0,1:T(4,128)}, u32[]{:S(2)}) copy-start(f32[4,7,7]{2,0,1:T(4,128)} %param.13) | copy-start | bytes 2356
  28.1 55.7 %all-to-all-start.1 = ((f32[128,56,128]{2,1,0:T(8,128)}), f32[128,56,128]{2,1,0:T(8,128)}, u32[]{:S(2)}, u32[]{:S(2)}) async-start(f32[128,56,128]{2,1,0:T(8,128)} %get-tuple-element.22), calls=%async_computation.1 | async-start | bytes 7340032 | tf_op jit(solution)/shard_map/all_to_all | solution.py:528
  36.7 1.2 %copy-start.3 = (f32[1,256,4,256]{3,2,1,0:T(4,128)S(1)}, f32[1,256,4,256]{3,2,1,0:T(4,128)}, u32[]{:S(2)}) copy-start(f32[1,256,4,256]{3,2,1,0:T(4,128)} %param.12) | copy-start | bytes 3145732
  83.7 16.6 %copy-start = (f32[1,256,4,256]{3,1,2,0:T(8,128)S(1)}, f32[1,256,4,256]{3,1,2,0:T(8,128)}, u32[]{:S(2)}) copy-start(f32[1,256,4,256]{3,1,2,0:T(8,128)} %copy.21) | copy-start | bytes 3145732
  83.7 16.6 %copy-start.1 = (f32[2,7,7,8,256]{4,3,2,1,0:T(8,128)S(1)}, f32[2,7,7,8,256]{4,3,2,1,0:T(8,128)}, u32[]{:S(2)}) copy-start(f32[2,7,7,8,256]{4,3,2,1,0:T(8,128)} %get-tuple-element.28.inv) | copy-start | bytes 2408452
  83.7 16.6 %copy-start.2 = (bf16[2,56,224]{2,1,0:T(8,128)(2,1)S(1)}, bf16[2,56,224]{2,1,0:T(8,128)(2,1)}, u32[]{:S(2)}) copy-start(bf16[2,56,224]{2,1,0:T(8,128)(2,1)} %pad_maximum_fusion.1.mix) | copy-start | bytes 150532
  94.1 3.2 %collective-permute-start.2 = (f32[14,128]{1,0:T(8,128)}, f32[14,128]{1,0:T(8,128)S(1)}, u32[]{:S(2)}, u32[]{:S(2)}) collective-permute-start(f32[14,128]{1,0:T(8,128)} %get-tuple-element.29), channel_id=1, source_target_pairs={{0,1},{1,0},{2,3},{3,2},{4,5},{5,4},{6,7},{7,6},{8,9},{9,8},{10,11... | collective-permute-start | bytes 21512 | tf_op jit(solution)/shard_map/ppermute | solution.py:495
  95.1 5.2 %collective-permute-start.3 = (f32[14,128]{1,0:T(8,128)}, f32[14,128]{1,0:T(8,128)S(1)}, u32[]{:S(2)}, u32[]{:S(2)}) collective-permute-start(f32[14,128]{1,0:T(8,128)} %get-tuple-element.30), channel_id=1, source_target_pairs={{1,2},{2,1},{3,4},{4,3},{5,6},{6,5},{7,8},{8,7},{9,10},{10,9},{11,... | collective-permute-start | bytes 21512 | tf_op jit(solution)/shard_map/ppermute | solution.py:495

commit v4 on v3

--- a/solution.py
+++ b/solution.py
@@ -92,21 +92,24 @@
 
 
 def gather_kernel(
-    parity, sent_in, asked_in, flow_in, message_out, tables_out, flow, sent, tables, table, message, sems, out_sems
+    sent_in, asked_in, flow_in, message_out, tables_out, flow, sent, asked, tables, table, message, sems, out_sems
 ):
     n = message.shape[0]
-    copies = [pltpu.make_async_copy(sent_in, sent, sems.at[0]), pltpu.make_async_copy(flow_in, flow, sems.at[1])]
+    copies = [
+        pltpu.make_async_copy(asked_in, asked, sems.at[4]),
+        pltpu.make_async_copy(sent_in, sent, sems.at[0]),
+        pltpu.make_async_copy(flow_in, flow, sems.at[1]),
+    ]
     begin(copies)
     eye = lax.broadcasted_iota(I32, (n, n), 0) == lax.broadcasted_iota(I32, (n, n), 1)
-    columns = asked_in[...].reshape(n, LANES).astype(F32)
+    finish(copies[:2])
+    columns = asked[...].reshape(n, LANES).astype(F32)
     for k in range(2):
         tables[k : k + 1, :] = jnp.sum(jnp.where(eye, columns[:, k : k + 1], 0.0), axis=0, keepdims=True).astype(I32)
-    tables[4:8, :] = jnp.full((4, n), parity[0], I32)
-    copies[0].wait()
     tables[2:4, :] = sent[...]
     shared = [pltpu.make_async_copy(tables, table, sems.at[2]), pltpu.make_async_copy(tables, tables_out, sems.at[3])]
     begin(shared)
-    finish(shared + copies[1:])
+    finish(shared + copies[2:])
 
     def step(d, carry):
         for part in range(2):
@@ -127,27 +130,28 @@
     finish(stores)
 
 
-def gather(parity, sent, asked, flow):
+def gather(sent, asked, flow):
     devices = asked.shape[0]
     message = (devices, 8 * NV, LANES)
     return pl.pallas_call(
         gather_kernel,
-        in_specs=[SMEM, whole(pltpu.HBM), whole(), whole(pltpu.HBM)],
+        in_specs=[whole(pltpu.HBM)] * 3,
         out_specs=[whole(pltpu.HBM)] * 2,
-        out_shape=[jax.ShapeDtypeStruct(message, F32), jax.ShapeDtypeStruct((8, devices), I32)],
+        out_shape=[jax.ShapeDtypeStruct(message, F32), jax.ShapeDtypeStruct((4, devices), I32)],
         scratch_shapes=[
             VMEM(flow.shape, F32),
             VMEM((2, devices), I32),
-            VMEM((8, devices), I32),
-            pltpu.SMEM((8, devices), I32),
+            VMEM(asked.shape, I32),
+            VMEM((4, devices), I32),
+            pltpu.SMEM((4, devices), I32),
             VMEM(message, F32),
-            pltpu.SemaphoreType.DMA((4,)),
+            pltpu.SemaphoreType.DMA((5,)),
             pltpu.SemaphoreType.DMA((CHUNKS,)),
         ],
         compiler_params=params(58),
         cost_estimate=cost(1_000_000, 6_000_000),
         name="gather",
-    )(parity, sent, asked, flow)
+    )(sent, asked, flow)
 
 
 def coupled(state, row, coef, mix):
@@ -187,11 +191,11 @@
 
 
 def first_kernel(
-    parity, flow, mix, halo_a, halo_b, right, coef, inv, packed_out, inv_out, inv_edges, state, packed, blocks, sems
+    place, flow, mix, halo_a, halo_b, right, coef, inv, packed_out, inv_out, inv_edges, state, packed, blocks, sems
 ):
     rows = 8 * TILES
     steps = flow.shape[1] // rows
-    even = parity[0] == 0
+    even, ahead, behind = (place[i] == 1 for i in range(3))
     reads, writes = [], []
     for c in range(steps):
         part = pl.ds(rows * c, rows)
@@ -206,8 +210,8 @@
     for n in range(2 * NV):
         v, h = divmod(n, 2)
         a, b = halo_a[n : n + 1, :], halo_b[n : n + 1, :]
-        state[n, 7:8, :] = jnp.where(even, b, a)
-        state[n, 8 + rows * steps : 9 + rows * steps, :] = jnp.where(even, a, b)
+        state[n, 7:8, :] = jnp.where(ahead, jnp.where(even, b, a), 0.0)
+        state[n, 8 + rows * steps : 9 + rows * steps, :] = jnp.where(behind, jnp.where(even, a, b), 0.0)
         state[n, 8 : 8 + rows * steps, :] = flow[v, :, LANES * h : LANES * (h + 1)]
 
     for c in range(steps):
@@ -232,7 +236,7 @@
     finish(writes)
 
 
-def first_sum(parity, flow, right, coef, mix, halo_a, halo_b, inv):
+def first_sum(place, flow, right, coef, mix, halo_a, halo_b, inv):
     rows = flow.shape[1]
     steps = rows // (8 * TILES)
     packed = (steps, PACKED, 8 * TILES, COLS)
@@ -251,7 +255,7 @@
         compiler_params=params(61),
         cost_estimate=cost(30_000_000, 40_000_000),
         name="first_sum",
-    )(parity, flow, mix, halo_a, halo_b, right, coef, inv)
+    )(place, flow, mix, halo_a, halo_b, right, coef, inv)
 
 
 def finish_kernel(
@@ -261,8 +265,8 @@
     packed_in,
     inv_in,
     out,
-    edge_a_out,
-    edge_b_out,
+    top_out,
+    bottom_out,
     table,
     turn,
     message,
@@ -276,8 +280,8 @@
     below,
     ends,
     done,
-    edge_a,
-    edge_b,
+    top,
+    bottom,
     message_sems,
     sems,
     out_sems,
@@ -400,17 +404,14 @@
     lax.fori_loop(0, steps, step, 0)
     sweep_two(steps, 0)
     store(steps - 1).start()
-    even = table[4, 0] == 0
     for v in range(NV):
-        top, bottom = ends[0, v][0:1, :], ends[2, v][7:8, :]
-        out_a, out_b = jnp.where(even, bottom, top), jnp.where(even, top, bottom)
         for h in range(2):
             n = 2 * v + h
-            edge_a[n : n + 1, :] = out_a[:, LANES * h : LANES * (h + 1)]
-            edge_b[n : n + 1, :] = out_b[:, LANES * h : LANES * (h + 1)]
+            top[n : n + 1, :] = ends[0, v, 0:1, LANES * h : LANES * (h + 1)]
+            bottom[n : n + 1, :] = ends[2, v, 7:8, LANES * h : LANES * (h + 1)]
     edges = [
-        pltpu.make_async_copy(edge_a, edge_a_out, small_sems.at[2]),
-        pltpu.make_async_copy(edge_b, edge_b_out, small_sems.at[3]),
+        pltpu.make_async_copy(top, top_out, small_sems.at[2]),
+        pltpu.make_async_copy(bottom, bottom_out, small_sems.at[3]),
     ]
     begin(edges)
     for c in range(steps):
@@ -442,57 +443,78 @@
     )(tables, turn, message, packed, inv)
 
 
-def edge_kernel(parity, relaxed, coef, mix, inv, halo_a, halo_b, out):
-    low = pl.program_id(0) == 0
-    use_a = (parity[0] == 0) != low
-    place = lax.broadcasted_iota(I32, (8, COLS), 0) == jnp.where(low, 0, 7)
-    factor = jnp.where(low, coef[0], coef[1])
-    parts = []
-    for v in range(NV):
-        rows = [jnp.where(use_a, halo_a[n : n + 1, :], halo_b[n : n + 1, :]) for n in (2 * v, 2 * v + 1)]
-        row = jnp.broadcast_to(jnp.concatenate(rows, axis=1), (8, COLS))
-        parts.append(jnp.where(place, factor * row, 0.0))
-    cells = jnp.concatenate(parts, axis=0)
-    zero = jnp.zeros_like(cells)
-    cells = jnp.concatenate([jnp.where(low, cells, zero), jnp.where(low, zero, cells), zero, zero], axis=0)
-    high = cells.astype(BF16)
-    rest = (cells - high.astype(F32)).astype(BF16)
+def edge_kernel(
+    place, relaxed_in, coef_in, mix_in, inv_in, halo_a_in, halo_b_in, out, ends, coef, mix, inv, halo_a, halo_b, sems
+):
+    even = place[0] == 1
+    tiles = (pl.ds(0, 8), pl.ds(out.shape[1] - 8, 8))
+    copies = [
+        pltpu.make_async_copy(src, dst, sems.at[i])
+        for i, (src, dst) in enumerate(
+            [(mix_in, mix), (inv_in, inv), (halo_a_in, halo_a), (halo_b_in, halo_b)]
+            + [(relaxed_in.at[:, tile, :], ends.at[g]) for g, tile in enumerate(tiles)]
+            + [(coef_in.at[:, tile, :], coef.at[g]) for g, tile in enumerate(tiles)]
+        )
+    ]
+    begin(copies)
+    finish(copies)
+    sub = lax.broadcasted_iota(I32, (8, COLS), 0)
+    zero = jnp.zeros((8 * NV, COLS), F32)
     dot = lambda a, b: jnp.dot(a, b, preferred_element_type=F32)
-    sums = dot(mix[0], high) + dot(mix[1], high) + dot(mix[0], rest)
-    change = apply_inv(lambda i, j: inv[i, j], [sums[8 * v : 8 * v + 8, :] for v in range(NV)])
-    for v in range(NV):
-        out[v] = relaxed[v] - change[v]
-
-
-def edge_rows(parity, relaxed, coef, mix, inv, halo_a, halo_b):
-    last = relaxed.shape[1] // 8 - 1
-    slab = pl.BlockSpec((NV, 8, COLS), lambda g: (0, g * last, 0))
+    for g in range(2):
+        use_a = even if g else jnp.logical_not(even)
+        mine = (sub == (7 if g else 0)) & (place[1 + g] == 1)
+        parts = []
+        for v in range(NV):
+            rows = [jnp.where(use_a, halo_a[n : n + 1, :], halo_b[n : n + 1, :]) for n in (2 * v, 2 * v + 1)]
+            row = jnp.broadcast_to(jnp.concatenate(rows, axis=1), (8, COLS))
+            parts.append(jnp.where(mine, coef[g, g] * row, 0.0))
+        cells = jnp.concatenate([zero] * g + parts + [zero] * (3 - g), axis=0)
+        high = cells.astype(BF16)
+        low = (cells - high.astype(F32)).astype(BF16)
+        sums = dot(mix[0], high) + dot(mix[1], high) + dot(mix[0], low)
+        change = apply_inv(lambda i, j, g=g: inv[g, i, j], [sums[8 * v : 8 * v + 8, :] for v in range(NV)])
+        for v in range(NV):
+            ends[g, v] = ends[g, v] - change[v]
+    writes = [pltpu.make_async_copy(ends.at[g], out.at[:, tile, :], sems.at[g]) for g, tile in enumerate(tiles)]
+    begin(writes)
+    finish(writes)
+
+
+def edge_rows(place, relaxed, coef, mix, inv, halo_a, halo_b):
     return pl.pallas_call(
         edge_kernel,
-        grid=(2,),
-        in_specs=[
-            SMEM,
-            slab,
-            pl.BlockSpec((4, 8, COLS), lambda g: (0, g * last, 0)),
-            pl.BlockSpec(mix.shape, lambda g: (0, 0, 0)),
-            pl.BlockSpec((None, NV, NV, 8, COLS), lambda g: (g, 0, 0, 0, 0)),
-            pl.BlockSpec((2 * NV, LANES), lambda g: (0, 0)),
-            pl.BlockSpec((2 * NV, LANES), lambda g: (0, 0)),
+        in_specs=[SMEM] + [whole(pltpu.HBM)] * 6,
+        out_specs=whole(pltpu.HBM),
+        out_shape=jax.ShapeDtypeStruct(relaxed.shape, F32),
+        scratch_shapes=[
+            VMEM((2, NV, 8, COLS), F32),
+            VMEM((2, 4, 8, COLS), F32),
+            VMEM(mix.shape, BF16),
+            VMEM(inv.shape, F32),
+            VMEM(halo_a.shape, F32),
+            VMEM(halo_b.shape, F32),
+            pltpu.SemaphoreType.DMA((8,)),
         ],
-        out_specs=slab,
-        out_shape=jax.ShapeDtypeStruct(relaxed.shape, F32),
         input_output_aliases={1: 0},
-        compiler_params=params(24),
+        compiler_params=params(40),
         cost_estimate=cost(100_000, 900_000),
         name="edge_rows",
-    )(parity, relaxed, coef, mix, inv, halo_a, halo_b)
-
-
-def exchange(edge_a, edge_b):
-    size = lax.axis_size("blk")
+    )(place, relaxed, coef, mix, inv, halo_a, halo_b)
+
+
+def exchange(top, bottom, even):
+    zones, size = lax.axis_size("zone"), lax.axis_size("blk")
     pairs_a = [(i, i ^ 1) for i in range(size)]
-    pairs_b = [(i, i - 1 if i % 2 == 0 else i + 1) for i in range(1, size - 1)]
-    return lax.ppermute(edge_a, "blk", pairs_a), lax.ppermute(edge_b, "blk", pairs_b)
+    pairs_b = []
+    for z in range(zones):
+        for i in range(size):
+            other, j = z, i - 1 if i % 2 == 0 else i + 1
+            if not 0 <= j < size:
+                other, j = z ^ 1, i
+            pairs_b.append((z * size + i, other * size + j))
+    edge_a, edge_b = jnp.where(even, bottom, top), jnp.where(even, top, bottom)
+    return lax.ppermute(edge_a, "blk", pairs_a), lax.ppermute(edge_b, AXES, pairs_b)
 
 
 def split(full):
@@ -516,25 +538,26 @@
     right = jnp.transpose(right_side[0], (1, 0, 2))
     inv = jnp.transpose(inv_diag[0], (1, 2, 0, 3))
     rows = flow.shape[1]
-    parity = (lax.axis_index("blk") % 2).astype(I32).reshape(1)
+    slab = lax.axis_index("blk")
+    even = slab % 2 == 0
+    place = jnp.stack([even, slab > 0, slab < lax.axis_size("blk") - 1]).astype(I32)
     as_row = lambda a: a.reshape(1, -1)
     sent, asking = slot_tables(as_row(hole_owner), as_row(block_device), as_row(source_row), as_row(target_row))
     asked = lax.all_to_all(asking, AXES, split_axis=0, concat_axis=0, tiled=True)
     top, bottom = flow[:, 0].reshape(2 * NV, LANES), flow[:, rows - 1].reshape(2 * NV, LANES)
-    even = parity[0] == 0
-    halo_a, halo_b = exchange(jnp.where(even, bottom, top), jnp.where(even, top, bottom))
+    halo_a, halo_b = exchange(top, bottom, even)
     asked, halo_a, halo_b = lax.optimization_barrier((asked, halo_a, halo_b))
-    message, tables = gather(parity, sent, asked, flow_state[0])
+    message, tables = gather(sent, asked, flow_state[0])
     message = lax.all_to_all(message, AXES, split_axis=0, concat_axis=0, tiled=True)
 
     coef = jnp.transpose(face_coef[0], (1, 0, 2))
     mix = mixing(face_jacobian)
-    packed, blocks, inv_edges = first_sum(parity, flow, right, coef, mix, halo_a, halo_b, inv)
-    relaxed, edge_a, edge_b = finish_sweeps(
+    packed, blocks, inv_edges = first_sum(place, flow, right, coef, mix, halo_a, halo_b, inv)
+    relaxed, top, bottom = finish_sweeps(
         tables, turning(face_jacobian), message, packed, blocks
     )
-    halo_a, halo_b = exchange(edge_a, edge_b)
-    relaxed = edge_rows(parity, relaxed, coef, mix, inv_edges, halo_a, halo_b)
+    halo_a, halo_b = exchange(top, bottom, even)
+    relaxed = edge_rows(place, relaxed, coef, mix, inv_edges, halo_a, halo_b)
     return jnp.transpose(relaxed, (1, 0, 2))[None]
 
 

time: 103 us -> 98.6 us (0.957)
  starting transfers between devices: 27 us -> 21.3 us
  other arithmetic: 2.59 us -> 3.9 us
    ppermute x2, starting transfers between devices: 4.7 us -> 1.83 us  [exchange(): lax.ppermute(edge_b, AXES, pairs_b)]
    all_to_all x1, waiting for transfers between devices: 0.85 us -> 2.75 us  [body(): lax.all_to_all(asking, AXES, split_axis=0, concat_axis=0, tiled=True)]
    all_to_all x1, starting transfers between devices: 8.64 us -> 6.75 us  [body(): lax.all_to_all(message, AXES, split_axis=0, concat_axis=0, tiled=True)]
    ppermute x2, waiting for transfers between devices: 3.03 us -> 1.84 us  [exchange(): lax.ppermute(edge_b, AXES, pairs_b)]
  transfers between devices with their start and end apart: 6 -> 6, of which waited for: 3 -> 3; matrix products, arithmetic and copies ran while one was open for 8% -> 9% of each run, Pallas kernels for 15% -> 16%
where the time goes in v4:
time: 98.6 us; the launch traced here: 97.9 us
  Pallas kernels  34.1 us (35%)
  waiting for transfers between devices  31.7 us (32%)
  starting transfers between devices  21.3 us (22%)
  local copies, waits for them, and re-layouts  6.68 us (7%)
  other arithmetic  3.9 us (4%)
    all_to_all x1, waiting for transfers between devices, body(): lax.all_to_all(message, AXES, split_axis=0, concat_axis=0, tiled=True)  27.1 us
    pallas_call x1, Pallas kernels, first_sum(): pl.pallas_call(first_kernel, in_specs=[SMEM] + [whole()] * 4 + [whole(plt...  15.4 us
    all_to_all x1, starting transfers between devices, body(): lax.all_to_all(asking, AXES, split_axis=0, concat_axis=0, tiled=True)  11.5 us
    pallas_call x1, Pallas kernels, finish_sweeps(): pl.pallas_call(finish_kernel, in_specs=[whole(pltpu.HBM)] * 5, out_specs=...  10.3 us
    all_to_all x1, starting transfers between devices, body(): lax.all_to_all(message, AXES, split_axis=0, concat_axis=0, tiled=True)  6.75 us
    pallas_call x1, Pallas kernels, gather(): pl.pallas_call(gather_kernel, in_specs=[whole(pltpu.HBM)] * 3, out_specs=...  4.01 us
    squeeze x1, local copies, waits for them, and re-layouts, body(): flow = jnp.transpose(flow_state[0], (1, 0, 2))  3.92 us
    all_to_all x1, waiting for transfers between devices, body(): lax.all_to_all(asking, AXES, split_axis=0, concat_axis=0, tiled=True)  2.75 us
  transfers between devices with their start and end apart: 6, of which 3 were waited for; matrix products, arithmetic and copies ran while one was open for 9% of the time, Pallas kernels for 16%

profile of v4, /device:TPU:1, one launch (start us, length us, event | category | flops | bytes accessed | tf_op | source)
XLA Modules:
  0.0 97.9 jit_solution(14919588737980891949)
XLA Ops:
  0.0 1.8 %slot_tables.1 = (s32[2,128]{1,0:T(2,128)}, s32[128,1,128]{2,1,0:T(1,128)}) custom-call(s32[1,128]{1,0:T(1,128)} %bitcast.35, s32[1,128]{1,0:T(1,128)} %bitcast.36, s32[1,128]{1,0:T(1,128)} %bitcast.37, s32[1,128]{1,0:T(1,128)} %bitcast.38), custom_call_target="tpu_custom_call" | custom-call | flops 4000000 | bytes 100000 | tf_op jit(solution)/shard_map/slot_tables/pallas_call | solution.py:72
  1.8 11.5 %all-to-all-start = ((s32[128,1,128]{2,1,0:T(1,128)}), s32[128,1,128]{2,1,0:T(1,128)S(1)}, u32[]{:S(2)}, u32[]{:S(2)}) async-start(s32[128,1,128]{2,1,0:T(1,128)} %get-tuple-element.19), calls=%async_computation | async-start | bytes 131072 | tf_op jit(solution)/shard_map/all_to_all | solution.py:546
  13.3 0.9 fusion.3
  14.2 1.1 %collective-permute-start = (f32[14,128]{1,0:T(8,128)S(1)}, f32[14,128]{1,0:T(8,128)S(1)}, u32[]{:S(2)}, u32[]{:S(2)}) collective-permute-start(f32[14,128]{1,0:T(8,128)S(1)} %select_n.38), channel_id=1, source_target_pairs={{0,1},{1,0},{2,3},{3,2},{4,5},{5,4},{6,7},{7,6},{8,9},{9,8},{10,11... | collective-permute-start | bytes 21512 | tf_op jit(solution)/shard_map/ppermute | solution.py:517
  15.4 0.7 collective-permute-start.1
  16.1 3.9 %copy.13.flow_in = f32[256,7,256]{2,1,0:T(8,128)} copy(f32[256,7,256]{2,0,1:T(8,128)} %bitcast.31) | data formatting | bytes 3670016 | tf_op jit(solution)/shard_map/squeeze | solution.py:537
  20.0 2.8 %all-to-all-done.asked_in = s32[128,1,128]{2,1,0:T(1,128)S(1)} async-done(((s32[128,1,128]{2,1,0:T(1,128)}), s32[128,1,128]{2,1,0:T(1,128)S(1)}, u32[]{:S(2)}, u32[]{:S(2)}) %all-to-all-start) | async-done | bytes 65568 | tf_op jit(solution)/shard_map/all_to_all | solution.py:546
  22.8 0.6 copy-done.5
  23.4 4.0 %gather.1 = (f32[128,56,128]{2,1,0:T(8,128)}, s32[4,128]{1,0:T(4,128)}) custom-call(s32[2,128]{1,0:T(2,128)} %get-tuple-element.18.sent_in, s32[128,1,128]{2,1,0:T(1,128)} %copy-done.5, f32[256,7,256]{2,1,0:T(8,128)} %copy.13.flow_in), custom_call_target="tpu_custom_call" | custom-call | flops 1000000 | bytes 6000000 | tf_op jit(solution)/shard_map/gather/pallas_call | solution.py:136
  27.4 6.8 %all-to-all-start.1 = ((f32[128,56,128]{2,1,0:T(8,128)}), f32[128,56,128]{2,1,0:T(8,128)}, u32[]{:S(2)}, u32[]{:S(2)}) async-start(f32[128,56,128]{2,1,0:T(8,128)} %get-tuple-element.22), calls=%async_computation.1 | async-start | bytes 7340032 | tf_op jit(solution)/shard_map/all_to_all | solution.py:551
  34.5 0.3 mul.50
  34.8 0.2 broadcast_multiply_fusion
  34.9 0.4 mul.55
  35.4 1.2 %copy.21 = f32[1,256,4,256]{3,1,2,0:T(8,128)} copy(f32[1,256,4,256]{3,2,1,0:T(4,128)S(1)} %copy-done.4) | data formatting | bytes 2097152 | tf_op args[3]
  36.7 0.6 add_convert_fusion.place
  37.3 0.6 pad_maximum_fusion.1.mix.mix_in
  37.9 0.8 pad_maximum_fusion.turn_in
  38.7 15.4 %first_sum.1 = (f32[8,18,32,256]{3,2,1,0:T(8,128)}, f32[8,7,7,32,256]{4,3,2,1,0:T(8,128)}, f32[2,7,7,8,256]{4,3,2,1,0:T(8,128)}) custom-call(s32[3]{0:T(128)} %add_convert_fusion.place, f32[7,256,256]{2,1,0:T(8,128)} %bitcast.32, bf16[2,56,224]{2,1,0:T(8,128)(2,1)} %pad_maximum_fusion.1.mix.mix_in, f32[14,128]{1,0:T(8,128)} %copy-done.7, ...), custom_call_target="tpu_custom_call" | custom-call | flops 30000000 | bytes 40000000 | tf_op jit(solution)/shard_map/first_sum/pallas_call | solution.py:244
  54.1 27.1 %all-to-all-done.1.message_in = f32[128,56,128]{2,1,0:T(8,128)} async-done(((f32[128,56,128]{2,1,0:T(8,128)}), f32[128,56,128]{2,1,0:T(8,128)}, u32[]{:S(2)}, u32[]{:S(2)}) %all-to-all-start.1) | async-done | bytes 3670048 | tf_op jit(solution)/shard_map/all_to_all | solution.py:551
  81.2 10.3 %finish_sweeps.1 = (f32[7,256,256]{2,1,0:T(8,128)}, f32[14,128]{1,0:T(8,128)}, f32[14,128]{1,0:T(8,128)}) custom-call(s32[4,128]{1,0:T(4,128)} %get-tuple-element.21.table_in, bf16[224,192]{1,0:T(8,128)(2,1)} %pad_maximum_fusion.turn_in, f32[128,56,128]{2,1,0:T(8,128)} %all-to-all-done.1.message_in, f32[8,18,32,256]{3,2,1,0:T(8,128)} %get-tuple-element.25.packed_in, ...), custom_call_target="tpu_custom_call" | custom-call | flops 45000000 | bytes 24000000 | tf_op jit(solution)/shard_map/finish_sweeps/pallas_call | solution.py:428
  91.6 0.7 broadcast_select_fusion.2
  92.3 1.1 %collective-permute-start.3 = (f32[14,128]{1,0:T(8,128)S(1)}, f32[14,128]{1,0:T(8,128)S(1)}, u32[]{:S(2)}, u32[]{:S(2)}) collective-permute-start(f32[14,128]{1,0:T(8,128)S(1)} %get-tuple-element.37), channel_id=1, source_target_pairs={{0,32},{1,2},{2,1},{3,4},{4,3},{5,6},{6,5},{7,8},{8,7},{9,10},{10,... | collective-permute-start | bytes 21512 | tf_op jit(solution)/shard_map/ppermute | solution.py:517
  93.5 1.8 %collective-permute-done.3.halo_b_in = f32[14,128]{1,0:T(8,128)S(1)} collective-permute-done((f32[14,128]{1,0:T(8,128)S(1)}, f32[14,128]{1,0:T(8,128)S(1)}, u32[]{:S(2)}, u32[]{:S(2)}) %collective-permute-start.3) | collective-permute-done | bytes 7200 | tf_op jit(solution)/shard_map/ppermute | solution.py:517
  95.4 2.5 %edge_rows.1 = f32[7,256,256]{2,1,0:T(8,128)} custom-call(s32[3]{0:T(128)S(1)} %copy-done.3, f32[7,256,256]{2,1,0:T(8,128)} %get-tuple-element.27.relaxed_in, f32[4,256,256]{2,1,0:T(8,128)S(1)} %bitcast.28, bf16[2,56,224]{2,1,0:T(8,128)(2,1)S(1)} %copy-done.2, f32[2,7,7,8,256]{4,3,2,1,0:T(8,128)S(1)} %copy-done.1, ...), custom_call_target="tpu_custom_call", output_to_operand_aliasing={{}: (1, {})} | custom-call | flops 100000 | bytes 900000 | tf_op jit(solution)/shard_map/edge_rows/pallas_call | solution.py:485
  (31 shorter events, 0.4 us)
Async XLA Ops:
  1.8 20.9 %all-to-all-start = ((s32[128,1,128]{2,1,0:T(1,128)}), s32[128,1,128]{2,1,0:T(1,128)S(1)}, u32[]{:S(2)}, u32[]{:S(2)}) async-start(s32[128,1,128]{2,1,0:T(1,128)} %get-tuple-element.19), calls=%async_computation | async-start | bytes 131072 | tf_op jit(solution)/shard_map/all_to_all | solution.py:546
  14.2 5.8 %collective-permute-start = (f32[14,128]{1,0:T(8,128)S(1)}, f32[14,128]{1,0:T(8,128)S(1)}, u32[]{:S(2)}, u32[]{:S(2)}) collective-permute-start(f32[14,128]{1,0:T(8,128)S(1)} %select_n.38), channel_id=1, source_target_pairs={{0,1},{1,0},{2,3},{3,2},{4,5},{5,4},{6,7},{7,6},{8,9},{9,8},{10,11... | collective-permute-start | bytes 21512 | tf_op jit(solution)/shard_map/ppermute | solution.py:517
  15.4 4.6 %collective-permute-start.1 = (f32[14,128]{1,0:T(8,128)S(1)}, f32[14,128]{1,0:T(8,128)S(1)}, u32[]{:S(2)}, u32[]{:S(2)}) collective-permute-start(f32[14,128]{1,0:T(8,128)S(1)} %select_n.40), channel_id=1, source_target_pairs={{0,32},{1,2},{2,1},{3,4},{4,3},{5,6},{6,5},{7,8},{8,7},{9,10},{10,... | collective-permute-start | bytes 21512 | tf_op jit(solution)/shard_map/ppermute | solution.py:517
  20.0 15.4 %copy-start.7 = (f32[14,128]{1,0:T(8,128)}, f32[14,128]{1,0:T(8,128)S(1)}, u32[]{:S(2)}) copy-start(f32[14,128]{1,0:T(8,128)S(1)} %collective-permute-done.halo_a) | copy-start | bytes 21508
  20.0 15.4 %copy-start.8 = (f32[14,128]{1,0:T(8,128)}, f32[14,128]{1,0:T(8,128)S(1)}, u32[]{:S(2)}) copy-start(f32[14,128]{1,0:T(8,128)S(1)} %collective-permute-done.1.halo_b) | copy-start | bytes 21508
  22.8 0.6 copy-start.5
  27.4 6.8 %copy-start.6 = (f32[4,7,7]{2,0,1:T(4,128)S(1)}, f32[4,7,7]{2,0,1:T(4,128)}, u32[]{:S(2)}) copy-start(f32[4,7,7]{2,0,1:T(4,128)} %param.13) | copy-start | bytes 2356
  27.4 53.8 %all-to-all-start.1 = ((f32[128,56,128]{2,1,0:T(8,128)}), f32[128,56,128]{2,1,0:T(8,128)}, u32[]{:S(2)}, u32[]{:S(2)}) async-start(f32[128,56,128]{2,1,0:T(8,128)} %get-tuple-element.22), calls=%async_computation.1 | async-start | bytes 7340032 | tf_op jit(solution)/shard_map/all_to_all | solution.py:551
  34.2 1.2 %copy-start.4 = (f32[1,256,4,256]{3,2,1,0:T(4,128)S(1)}, f32[1,256,4,256]{3,2,1,0:T(4,128)}, u32[]{:S(2)}) copy-start(f32[1,256,4,256]{3,2,1,0:T(4,128)} %param.12) | copy-start | bytes 3145732
  81.2 14.2 %copy-start = (f32[1,256,4,256]{3,1,2,0:T(8,128)S(1)}, f32[1,256,4,256]{3,1,2,0:T(8,128)}, u32[]{:S(2)}) copy-start(f32[1,256,4,256]{3,1,2,0:T(8,128)} %copy.21) | copy-start | bytes 3145732
  81.2 14.2 %copy-start.1 = (f32[2,7,7,8,256]{4,3,2,1,0:T(8,128)S(1)}, f32[2,7,7,8,256]{4,3,2,1,0:T(8,128)}, u32[]{:S(2)}) copy-start(f32[2,7,7,8,256]{4,3,2,1,0:T(8,128)} %get-tuple-element.28.inv_in) | copy-start | bytes 2408452
  81.2 14.2 %copy-start.2 = (bf16[2,56,224]{2,1,0:T(8,128)(2,1)S(1)}, bf16[2,56,224]{2,1,0:T(8,128)(2,1)}, u32[]{:S(2)}) copy-start(bf16[2,56,224]{2,1,0:T(8,128)(2,1)} %pad_maximum_fusion.1.mix.mix_in) | copy-start | bytes 150532
  81.2 14.2 %copy-start.3 = (s32[3]{0:T(128)S(1)}, s32[3]{0:T(128)}, u32[]{:S(2)}) copy-start(s32[3]{0:T(128)} %add_convert_fusion.place) | copy-start | bytes 40
  92.3 3.1 %collective-permute-start.3 = (f32[14,128]{1,0:T(8,128)S(1)}, f32[14,128]{1,0:T(8,128)S(1)}, u32[]{:S(2)}, u32[]{:S(2)}) collective-permute-start(f32[14,128]{1,0:T(8,128)S(1)} %get-tuple-element.37), channel_id=1, source_target_pairs={{0,32},{1,2},{2,1},{3,4},{4,3},{5,6},{6,5},{7,8},{8,7},{9,10},{10,... | collective-permute-start | bytes 21512 | tf_op jit(solution)/shard_map/ppermute | solution.py:517
  93.4 1.9 %collective-permute-start.2 = (f32[14,128]{1,0:T(8,128)S(1)}, f32[14,128]{1,0:T(8,128)S(1)}, u32[]{:S(2)}, u32[]{:S(2)}) collective-permute-start(f32[14,128]{1,0:T(8,128)S(1)} %get-tuple-element.38), channel_id=1, source_target_pairs={{0,1},{1,0},{2,3},{3,2},{4,5},{5,4},{6,7},{7,6},{8,9},{9,8},{10,11... | collective-permute-start | bytes 21512 | tf_op jit(solution)/shard_map/ppermute | solution.py:517

commit v5 on v4

--- a/solution.py
+++ b/solution.py
@@ -102,28 +102,32 @@
     ]
     begin(copies)
     eye = lax.broadcasted_iota(I32, (n, n), 0) == lax.broadcasted_iota(I32, (n, n), 1)
-    finish(copies[:2])
+    copies[0].wait()
     columns = asked[...].reshape(n, LANES).astype(F32)
     for k in range(2):
         tables[k : k + 1, :] = jnp.sum(jnp.where(eye, columns[:, k : k + 1], 0.0), axis=0, keepdims=True).astype(I32)
-    tables[2:4, :] = sent[...]
-    shared = [pltpu.make_async_copy(tables, table, sems.at[2]), pltpu.make_async_copy(tables, tables_out, sems.at[3])]
-    begin(shared)
-    finish(shared + copies[2:])
-
-    def step(d, carry):
-        for part in range(2):
+    to_scalar = pltpu.make_async_copy(tables, table, sems.at[2])
+    to_scalar.start()
+    finish(copies[1:])
+
+    def rows_of(source, part):
+        def step(d, carry):
             for k in range(2):
-                row = jnp.maximum(table[2 - 2 * part + k, d] - 1, 0)
+                row = jnp.maximum(source[k, d] - 1, 0)
                 for h in range(2):
                     start = 28 * part + 14 * k + NV * h
                     message[d, start : start + NV, :] = flow[row, :, LANES * h : LANES * (h + 1)]
-        return carry
-
+            return carry
+
+        return step
+
+    lax.fori_loop(0, n, rows_of(sent, 0), 0, unroll=8)
+    to_scalar.wait()
+    stores = [pltpu.make_async_copy(tables, tables_out, sems.at[3])]
+    stores[0].start()
     size = n // CHUNKS
-    stores = []
     for c in range(CHUNKS):
-        lax.fori_loop(c * size, (c + 1) * size, step, 0, unroll=4)
+        lax.fori_loop(c * size, (c + 1) * size, rows_of(table, 1), 0, unroll=8)
         part = pl.ds(c * size, size)
         stores.append(pltpu.make_async_copy(message.at[part], message_out.at[part], out_sems.at[c]))
         stores[-1].start()
@@ -137,13 +141,13 @@
         gather_kernel,
         in_specs=[whole(pltpu.HBM)] * 3,
         out_specs=[whole(pltpu.HBM)] * 2,
-        out_shape=[jax.ShapeDtypeStruct(message, F32), jax.ShapeDtypeStruct((4, devices), I32)],
+        out_shape=[jax.ShapeDtypeStruct(message, F32), jax.ShapeDtypeStruct((2, devices), I32)],
         scratch_shapes=[
             VMEM(flow.shape, F32),
+            pltpu.SMEM((2, devices), I32),
+            VMEM(asked.shape, I32),
             VMEM((2, devices), I32),
-            VMEM(asked.shape, I32),
-            VMEM((4, devices), I32),
-            pltpu.SMEM((4, devices), I32),
+            pltpu.SMEM((2, devices), I32),
             VMEM(message, F32),
             pltpu.SemaphoreType.DMA((5,)),
             pltpu.SemaphoreType.DMA((CHUNKS,)),
@@ -191,11 +195,11 @@
 
 
 def first_kernel(
-    place, flow, mix, halo_a, halo_b, right, coef, inv, packed_out, inv_out, inv_edges, state, packed, blocks, sems
+    place, jac, flow, mix, halo_a, halo_b, right, coef, inv, packed_out, inv_out, operators, state, packed, blocks, sems
 ):
     rows = 8 * TILES
     steps = flow.shape[1] // rows
-    even, ahead, behind = (place[i] == 1 for i in range(3))
+    even, ahead, behind = (place[0, i] == 1 for i in range(3))
     reads, writes = [], []
     for c in range(steps):
         part = pl.ds(rows * c, rows)
@@ -231,21 +235,28 @@
             pltpu.make_async_copy(blocks.at[c], inv_out.at[c], sems.at[4, c]),
         ]
         begin(writes[-2:])
-    inv_edges[0] = blocks[0, :, :, 0:8, :]
-    inv_edges[1] = blocks[steps - 1, :, :, rows - 8 : rows, :]
+    for g, (there, c, row) in enumerate(((ahead, 0, 0), (behind, steps - 1, rows - 1))):
+        factor = jnp.where(there, packed[c, 2 * NV + g, row : row + 1, :], 0.0)
+        for i in range(NV):
+            weights = [factor * blocks[c, i, k, row : row + 1, :] for k in range(NV)]
+            for j in range(NV):
+                total = jac[NV * NV * g + j] * weights[0]
+                for k in range(1, NV):
+                    total = total + jac[NV * (NV * g + k) + j] * weights[k]
+                operators[g, j, i : i + 1, :] = total
     finish(writes)
 
 
-def first_sum(place, flow, right, coef, mix, halo_a, halo_b, inv):
+def first_sum(place, jac, flow, right, coef, mix, halo_a, halo_b, inv):
     rows = flow.shape[1]
     steps = rows // (8 * TILES)
     packed = (steps, PACKED, 8 * TILES, COLS)
     blocks = (steps, NV, NV, 8 * TILES, COLS)
     return pl.pallas_call(
         first_kernel,
-        in_specs=[SMEM] + [whole()] * 4 + [whole(pltpu.HBM)] * 3,
+        in_specs=[SMEM] * 2 + [whole()] * 4 + [whole(pltpu.HBM)] * 3,
         out_specs=[whole(pltpu.HBM)] * 2 + [whole()],
-        out_shape=[jax.ShapeDtypeStruct(s, F32) for s in (packed, blocks, (2, NV, NV, 8, COLS))],
+        out_shape=[jax.ShapeDtypeStruct(s, F32) for s in (packed, blocks, (2, NV, 8, COLS))],
         scratch_shapes=[
             VMEM((2 * NV, rows + 16, LANES), F32),
             VMEM(packed, F32),
@@ -255,19 +266,23 @@
         compiler_params=params(61),
         cost_estimate=cost(30_000_000, 40_000_000),
         name="first_sum",
-    )(place, flow, mix, halo_a, halo_b, right, coef, inv)
+    )(place, jac, flow, mix, halo_a, halo_b, right, coef, inv)
 
 
 def finish_kernel(
-    table_in,
+    asked_in,
+    sent_in,
+    place_in,
     turn_in,
     message_in,
     packed_in,
     inv_in,
     out,
-    top_out,
-    bottom_out,
-    table,
+    edge_a_out,
+    edge_b_out,
+    asked,
+    sent,
+    place,
     turn,
     message,
     add_left,
@@ -280,8 +295,8 @@
     below,
     ends,
     done,
-    top,
-    bottom,
+    edge_a,
+    edge_b,
     message_sems,
     sems,
     out_sems,
@@ -306,7 +321,8 @@
         part = pl.ds(pl.multiple_of(rows * c, rows), rows)
         return pltpu.make_async_copy(done.at[c + 1], out.at[:, part, :], out_sems.at[c])
 
-    small = [pltpu.make_async_copy(table_in, table, small_sems.at[0]), pltpu.make_async_copy(turn_in, turn, small_sems.at[1])]
+    pairs = ((asked_in, asked), (sent_in, sent), (place_in, place), (turn_in, turn))
+    small = [pltpu.make_async_copy(src, dst, small_sems.at[i]) for i, (src, dst) in enumerate(pairs)]
     begin(small)
     begin([load(c) for c in range(CHUNKS)])
     begin(fetch(0))
@@ -323,8 +339,8 @@
 
     def scatter(d, carry):
         for k in range(2):
-            for part, refs in enumerate((plus, minus)):
-                row = pl.multiple_of(8 * table[2 * part + k, d], 8)
+            for part, (table, refs) in enumerate(((asked, plus), (sent, minus))):
+                row = pl.multiple_of(8 * table[k, d], 8)
                 for h, ref in enumerate(refs):
                     first = 28 * part + 14 * k + NV * h
                     ref[pl.ds(row, NV), :] += message[d, first : first + NV, :]
@@ -404,14 +420,17 @@
     lax.fori_loop(0, steps, step, 0)
     sweep_two(steps, 0)
     store(steps - 1).start()
+    even = place[0, 0] == 1
     for v in range(NV):
+        top, bottom = ends[0, v, 0:1, :], ends[2, v, 7:8, :]
+        out_a, out_b = jnp.where(even, bottom, top), jnp.where(even, top, bottom)
         for h in range(2):
             n = 2 * v + h
-            top[n : n + 1, :] = ends[0, v, 0:1, LANES * h : LANES * (h + 1)]
-            bottom[n : n + 1, :] = ends[2, v, 7:8, LANES * h : LANES * (h + 1)]
+            edge_a[n : n + 1, :] = out_a[:, LANES * h : LANES * (h + 1)]
+            edge_b[n : n + 1, :] = out_b[:, LANES * h : LANES * (h + 1)]
     edges = [
-        pltpu.make_async_copy(top, top_out, small_sems.at[2]),
-        pltpu.make_async_copy(bottom, bottom_out, small_sems.at[3]),
+        pltpu.make_async_copy(edge_a, edge_a_out, small_sems.at[4]),
+        pltpu.make_async_copy(edge_b, edge_b_out, small_sems.at[5]),
     ]
     begin(edges)
     for c in range(steps):
@@ -419,7 +438,7 @@
     finish(edges)
 
 
-def finish_sweeps(tables, turn, message, packed, inv):
+def finish_sweeps(asked, sent, place, turn, message, packed, inv):
     steps = packed.shape[0]
     rows = 8 * TILES * steps
     sums = VMEM((8 * (rows + 8), LANES), F32)
@@ -427,83 +446,61 @@
     slab = (NV, rows, COLS)
     return pl.pallas_call(
         finish_kernel,
-        in_specs=[whole(pltpu.HBM)] * 5,
+        in_specs=[whole(pltpu.HBM)] * 7,
         out_specs=[whole(pltpu.HBM)] * 3,
         out_shape=[jax.ShapeDtypeStruct(s, F32) for s in (slab, (2 * NV, LANES), (2 * NV, LANES))],
-        scratch_shapes=[pltpu.SMEM(tables.shape, I32), VMEM(turn.shape, BF16), VMEM(message.shape, F32)]
+        scratch_shapes=[pltpu.SMEM(a.shape, I32) for a in (asked, sent, place)]
+        + [VMEM(turn.shape, BF16), VMEM(message.shape, F32)]
         + [sums] * 4
         + [VMEM((steps + 1,) + a.shape[1:], F32) for a in (packed, inv)]
         + [padded] * 2
         + [VMEM((3, NV, 8, COLS), F32), VMEM((steps + 1, NV, 8 * TILES, COLS), F32)]
         + [VMEM((2 * NV, LANES), F32)] * 2
-        + [pltpu.SemaphoreType.DMA(s) for s in ((CHUNKS,), (2, steps), (steps,), (4,))],
+        + [pltpu.SemaphoreType.DMA(s) for s in ((CHUNKS,), (2, steps), (steps,), (6,))],
         compiler_params=params(61),
         cost_estimate=cost(45_000_000, 24_000_000),
         name="finish_sweeps",
-    )(tables, turn, message, packed, inv)
-
-
-def edge_kernel(
-    place, relaxed_in, coef_in, mix_in, inv_in, halo_a_in, halo_b_in, out, ends, coef, mix, inv, halo_a, halo_b, sems
-):
-    even = place[0] == 1
+    )(asked, sent, place, turn, message, packed, inv)
+
+
+def edge_kernel(place, relaxed, operators, halo_a, halo_b, out, ends, sems):
+    even = place[0, 0] == 1
     tiles = (pl.ds(0, 8), pl.ds(out.shape[1] - 8, 8))
-    copies = [
-        pltpu.make_async_copy(src, dst, sems.at[i])
-        for i, (src, dst) in enumerate(
-            [(mix_in, mix), (inv_in, inv), (halo_a_in, halo_a), (halo_b_in, halo_b)]
-            + [(relaxed_in.at[:, tile, :], ends.at[g]) for g, tile in enumerate(tiles)]
-            + [(coef_in.at[:, tile, :], coef.at[g]) for g, tile in enumerate(tiles)]
-        )
-    ]
-    begin(copies)
-    finish(copies)
-    sub = lax.broadcasted_iota(I32, (8, COLS), 0)
-    zero = jnp.zeros((8 * NV, COLS), F32)
-    dot = lambda a, b: jnp.dot(a, b, preferred_element_type=F32)
+    reads = [pltpu.make_async_copy(relaxed.at[:, tile, :], ends.at[g], sems.at[g]) for g, tile in enumerate(tiles)]
+    begin(reads)
+    changes = []
     for g in range(2):
         use_a = even if g else jnp.logical_not(even)
-        mine = (sub == (7 if g else 0)) & (place[1 + g] == 1)
-        parts = []
+        total = None
+        for j in range(NV):
+            halves = [jnp.where(use_a, halo_a[n : n + 1, :], halo_b[n : n + 1, :]) for n in (2 * j, 2 * j + 1)]
+            term = operators[g, j] * jnp.concatenate(halves, axis=1)
+            total = term if j == 0 else total + term
+        changes.append(total)
+    finish(reads)
+    for g, row in enumerate((0, 7)):
         for v in range(NV):
-            rows = [jnp.where(use_a, halo_a[n : n + 1, :], halo_b[n : n + 1, :]) for n in (2 * v, 2 * v + 1)]
-            row = jnp.broadcast_to(jnp.concatenate(rows, axis=1), (8, COLS))
-            parts.append(jnp.where(mine, coef[g, g] * row, 0.0))
-        cells = jnp.concatenate([zero] * g + parts + [zero] * (3 - g), axis=0)
-        high = cells.astype(BF16)
-        low = (cells - high.astype(F32)).astype(BF16)
-        sums = dot(mix[0], high) + dot(mix[1], high) + dot(mix[0], low)
-        change = apply_inv(lambda i, j, g=g: inv[g, i, j], [sums[8 * v : 8 * v + 8, :] for v in range(NV)])
-        for v in range(NV):
-            ends[g, v] = ends[g, v] - change[v]
+            ends[g, v, row : row + 1, :] = ends[g, v, row : row + 1, :] - changes[g][v : v + 1, :]
     writes = [pltpu.make_async_copy(ends.at[g], out.at[:, tile, :], sems.at[g]) for g, tile in enumerate(tiles)]
     begin(writes)
     finish(writes)
 
 
-def edge_rows(place, relaxed, coef, mix, inv, halo_a, halo_b):
+def edge_rows(place, relaxed, operators, halo_a, halo_b):
     return pl.pallas_call(
         edge_kernel,
-        in_specs=[SMEM] + [whole(pltpu.HBM)] * 6,
+        in_specs=[SMEM, whole(pltpu.HBM)] + [whole()] * 3,
         out_specs=whole(pltpu.HBM),
         out_shape=jax.ShapeDtypeStruct(relaxed.shape, F32),
-        scratch_shapes=[
-            VMEM((2, NV, 8, COLS), F32),
-            VMEM((2, 4, 8, COLS), F32),
-            VMEM(mix.shape, BF16),
-            VMEM(inv.shape, F32),
-            VMEM(halo_a.shape, F32),
-            VMEM(halo_b.shape, F32),
-            pltpu.SemaphoreType.DMA((8,)),
-        ],
+        scratch_shapes=[VMEM((2, NV, 8, COLS), F32), pltpu.SemaphoreType.DMA((2,))],
         input_output_aliases={1: 0},
-        compiler_params=params(40),
-        cost_estimate=cost(100_000, 900_000),
+        compiler_params=params(24),
+        cost_estimate=cost(100_000, 400_000),
         name="edge_rows",
-    )(place, relaxed, coef, mix, inv, halo_a, halo_b)
-
-
-def exchange(top, bottom, even):
+    )(place, relaxed, operators, halo_a, halo_b)
+
+
+def exchange(edge_a, edge_b):
     zones, size = lax.axis_size("zone"), lax.axis_size("blk")
     pairs_a = [(i, i ^ 1) for i in range(size)]
     pairs_b = []
@@ -513,7 +510,6 @@
             if not 0 <= j < size:
                 other, j = z ^ 1, i
             pairs_b.append((z * size + i, other * size + j))
-    edge_a, edge_b = jnp.where(even, bottom, top), jnp.where(even, top, bottom)
     return lax.ppermute(edge_a, "blk", pairs_a), lax.ppermute(edge_b, AXES, pairs_b)
 
 
@@ -540,24 +536,26 @@
     rows = flow.shape[1]
     slab = lax.axis_index("blk")
     even = slab % 2 == 0
-    place = jnp.stack([even, slab > 0, slab < lax.axis_size("blk") - 1]).astype(I32)
+    flags = jnp.stack([even, slab > 0, slab < lax.axis_size("blk") - 1]).astype(I32)
+    place = jnp.pad(flags, (0, LANES - 3)).reshape(1, LANES)
     as_row = lambda a: a.reshape(1, -1)
     sent, asking = slot_tables(as_row(hole_owner), as_row(block_device), as_row(source_row), as_row(target_row))
     asked = lax.all_to_all(asking, AXES, split_axis=0, concat_axis=0, tiled=True)
     top, bottom = flow[:, 0].reshape(2 * NV, LANES), flow[:, rows - 1].reshape(2 * NV, LANES)
-    halo_a, halo_b = exchange(top, bottom, even)
+    halo_a, halo_b = exchange(jnp.where(even, bottom, top), jnp.where(even, top, bottom))
     asked, halo_a, halo_b = lax.optimization_barrier((asked, halo_a, halo_b))
-    message, tables = gather(sent, asked, flow_state[0])
+    message, asked = gather(sent, asked, flow_state[0])
     message = lax.all_to_all(message, AXES, split_axis=0, concat_axis=0, tiled=True)
 
     coef = jnp.transpose(face_coef[0], (1, 0, 2))
     mix = mixing(face_jacobian)
-    packed, blocks, inv_edges = first_sum(place, flow, right, coef, mix, halo_a, halo_b, inv)
-    relaxed, top, bottom = finish_sweeps(
-        tables, turning(face_jacobian), message, packed, blocks
+    jac = face_jacobian.reshape(-1)
+    packed, blocks, operators = first_sum(place, jac, flow, right, coef, mix, halo_a, halo_b, inv)
+    relaxed, edge_a, edge_b = finish_sweeps(
+        asked, sent, place, turning(face_jacobian), message, packed, blocks
     )
-    halo_a, halo_b = exchange(top, bottom, even)
-    relaxed = edge_rows(place, relaxed, coef, mix, inv_edges, halo_a, halo_b)
+    halo_a, halo_b = exchange(edge_a, edge_b)
+    relaxed = edge_rows(place, relaxed, operators, halo_a, halo_b)
     return jnp.transpose(relaxed, (1, 0, 2))[None]
 
 

time: 98.6 us -> 98.7 us (level)
  waiting for transfers between devices: 31.7 us -> 32.8 us
  transfers between devices with their start and end apart: 6 -> 6, of which waited for: 3 -> 4; matrix products, arithmetic and copies ran while one was open for 9% -> 10% of each run, Pallas kernels for 16% -> 15%
where the time goes in v5:
time: 98.7 us; the launch traced here: 98.3 us
  Pallas kernels  33.5 us (34%)
  waiting for transfers between devices  32.8 us (33%)
  starting transfers between devices  21.4 us (22%)
  local copies, waits for them, and re-layouts  7.21 us (7%)
  other arithmetic  3.18 us (3%)
    all_to_all x1, waiting for transfers between devices, body(): lax.all_to_all(message, AXES, split_axis=0, concat_axis=0, tiled=True)  26.8 us
    pallas_call x1, Pallas kernels, first_sum(): pl.pallas_call(first_kernel, in_specs=[SMEM] * 2 + [whole()] * 4 + [whole...  15.2 us
    all_to_all x1, starting transfers between devices, body(): lax.all_to_all(asking, AXES, split_axis=0, concat_axis=0, tiled=True)  11.5 us
    pallas_call x1, Pallas kernels, finish_sweeps(): pl.pallas_call(finish_kernel, in_specs=[whole(pltpu.HBM)] * 7, out_specs=...  10.1 us
    all_to_all x1, starting transfers between devices, body(): lax.all_to_all(message, AXES, split_axis=0, concat_axis=0, tiled=True)  6.75 us
    pallas_call x1, Pallas kernels, gather(): pl.pallas_call(gather_kernel, in_specs=[whole(pltpu.HBM)] * 3, out_specs=...  4.3 us
    squeeze x1, local copies, waits for them, and re-layouts, body(): flow = jnp.transpose(flow_state[0], (1, 0, 2))  3.91 us
    all_to_all x1, waiting for transfers between devices, body(): lax.all_to_all(asking, AXES, split_axis=0, concat_axis=0, tiled=True)  2.77 us
  transfers between devices with their start and end apart: 6, of which 4 were waited for; matrix products, arithmetic and copies ran while one was open for 10% of the time, Pallas kernels for 15%

profile of v5, /device:TPU:1, one launch (start us, length us, event | category | flops | bytes accessed | tf_op | source)
XLA Modules:
  0.0 98.3 jit_solution(13210192753801345728)
XLA Ops:
  0.0 1.8 %slot_tables.1 = (s32[2,128]{1,0:T(2,128)}, s32[128,1,128]{2,1,0:T(1,128)}) custom-call(s32[1,128]{1,0:T(1,128)} %bitcast.36, s32[1,128]{1,0:T(1,128)} %bitcast.37, s32[1,128]{1,0:T(1,128)} %bitcast.38, s32[1,128]{1,0:T(1,128)} %bitcast.39), custom_call_target="tpu_custom_call" | custom-call | flops 4000000 | bytes 100000 | tf_op jit(solution)/shard_map/slot_tables/pallas_call | solution.py:72
  1.8 11.5 %all-to-all-start = ((s32[128,1,128]{2,1,0:T(1,128)}), s32[128,1,128]{2,1,0:T(1,128)S(1)}, u32[]{:S(2)}, u32[]{:S(2)}) async-start(s32[128,1,128]{2,1,0:T(1,128)} %get-tuple-element.19), calls=%async_computation | async-start | bytes 131072 | tf_op jit(solution)/shard_map/all_to_all | solution.py:543
  13.3 0.9 fusion.3
  14.2 1.1 %collective-permute-start = (f32[14,128]{1,0:T(8,128)S(1)}, f32[14,128]{1,0:T(8,128)S(1)}, u32[]{:S(2)}, u32[]{:S(2)}) collective-permute-start(f32[14,128]{1,0:T(8,128)S(1)} %select_n.28), channel_id=1, source_target_pairs={{0,1},{1,0},{2,3},{3,2},{4,5},{5,4},{6,7},{7,6},{8,9},{9,8},{10,11... | collective-permute-start | bytes 21512 | tf_op jit(solution)/shard_map/ppermute | solution.py:513
  15.4 0.7 collective-permute-start.1
  16.1 3.9 %copy.13.flow_in = f32[256,7,256]{2,1,0:T(8,128)} copy(f32[256,7,256]{2,0,1:T(8,128)} %bitcast.31) | data formatting | bytes 3670016 | tf_op jit(solution)/shard_map/squeeze | solution.py:533
  20.0 2.8 %all-to-all-done.asked_in = s32[128,1,128]{2,1,0:T(1,128)S(1)} async-done(((s32[128,1,128]{2,1,0:T(1,128)}), s32[128,1,128]{2,1,0:T(1,128)S(1)}, u32[]{:S(2)}, u32[]{:S(2)}) %all-to-all-start) | async-done | bytes 65568 | tf_op jit(solution)/shard_map/all_to_all | solution.py:543
  22.8 0.6 copy-done.3
  23.4 4.3 %gather.1 = (f32[128,56,128]{2,1,0:T(8,128)}, s32[2,128]{1,0:T(2,128)}) custom-call(s32[2,128]{1,0:T(2,128)} %get-tuple-element.18.sent_in, s32[128,1,128]{2,1,0:T(1,128)} %copy-done.3, f32[256,7,256]{2,1,0:T(8,128)} %copy.13.flow_in), custom_call_target="tpu_custom_call" | custom-call | flops 1000000 | bytes 6000000 | tf_op jit(solution)/shard_map/gather/pallas_call | solution.py:140
  27.7 6.8 %all-to-all-start.1 = ((f32[128,56,128]{2,1,0:T(8,128)}), f32[128,56,128]{2,1,0:T(8,128)}, u32[]{:S(2)}, u32[]{:S(2)}) async-start(f32[128,56,128]{2,1,0:T(8,128)} %get-tuple-element.22), calls=%async_computation.1 | async-start | bytes 7340032 | tf_op jit(solution)/shard_map/all_to_all | solution.py:548
  34.5 0.7 reshape.89.jac
  35.9 0.4 mul.55
  36.3 1.2 %copy.22 = f32[1,256,4,256]{3,1,2,0:T(8,128)} copy(f32[1,256,4,256]{3,2,1,0:T(4,128)S(1)} %copy-done.2) | data formatting | bytes 2097152 | tf_op args[3]
  37.6 0.5 fusion.5.place.place_in
  38.1 0.6 pad_maximum_fusion.1.mix
  38.8 0.7 pad_maximum_fusion.turn_in
  39.5 15.2 %first_sum.1 = (f32[8,18,32,256]{3,2,1,0:T(8,128)}, f32[8,7,7,32,256]{4,3,2,1,0:T(8,128)}, f32[2,7,8,256]{3,2,1,0:T(8,128)}) custom-call(s32[1,128]{1,0:T(1,128)} %fusion.5.place.place_in, f32[196]{0:T(256)} %reshape.89.jac, f32[7,256,256]{2,1,0:T(8,128)} %bitcast.32, bf16[2,56,224]{2,1,0:T(8,128)(2,1)} %pad_maximum_fusion.1.mix, f32[14,128]{1,0:T(8,128)} %copy-done.5, ...), custom_call_target="tpu_custom_call" | custom-call | flops 30000000 | bytes 40000000 | tf_op jit(solution)/shard_map/first_sum/pallas_call | solution.py:255
  54.7 26.8 %all-to-all-done.1.message_in = f32[128,56,128]{2,1,0:T(8,128)} async-done(((f32[128,56,128]{2,1,0:T(8,128)}), f32[128,56,128]{2,1,0:T(8,128)}, u32[]{:S(2)}, u32[]{:S(2)}) %all-to-all-start.1) | async-done | bytes 3670048 | tf_op jit(solution)/shard_map/all_to_all | solution.py:548
  81.5 10.1 %finish_sweeps.1 = (f32[7,256,256]{2,1,0:T(8,128)}, f32[14,128]{1,0:T(8,128)}, f32[14,128]{1,0:T(8,128)}) custom-call(s32[2,128]{1,0:T(2,128)} %get-tuple-element.21.asked_in, s32[2,128]{1,0:T(2,128)} %get-tuple-element.18.sent_in, s32[1,128]{1,0:T(1,128)} %fusion.5.place.place_in, bf16[224,192]{1,0:T(8,128)(2,1)} %pad_maximum_fusion.turn_in, ...), custom_call_target="tpu_custom_call" | custom-call | flops 45000000 | bytes 24000000 | tf_op jit(solution)/shard_map/finish_sweeps/pallas_call | solution.py:447
  91.6 1.1 %collective-permute-start.2 = (f32[14,128]{1,0:T(8,128)}, f32[14,128]{1,0:T(8,128)S(1)}, u32[]{:S(2)}, u32[]{:S(2)}) collective-permute-start(f32[14,128]{1,0:T(8,128)} %get-tuple-element.29), channel_id=1, source_target_pairs={{0,1},{1,0},{2,3},{3,2},{4,5},{5,4},{6,7},{7,6},{8,9},{9,8},{10,11... | collective-permute-start | bytes 21512 | tf_op jit(solution)/shard_map/ppermute | solution.py:513
  92.7 0.3 collective-permute-start.3
  92.9 0.7 collective-permute-done.2.halo_a
  93.7 2.5 %collective-permute-done.3.halo_b = f32[14,128]{1,0:T(8,128)S(1)} collective-permute-done((f32[14,128]{1,0:T(8,128)}, f32[14,128]{1,0:T(8,128)S(1)}, u32[]{:S(2)}, u32[]{:S(2)}) %collective-permute-start.3) | collective-permute-done | bytes 7200 | tf_op jit(solution)/shard_map/ppermute | solution.py:513
  96.2 2.1 %edge_rows.1 = f32[7,256,256]{2,1,0:T(8,128)} custom-call(s32[1,128]{1,0:T(1,128)S(1)} %copy-done.1, f32[7,256,256]{2,1,0:T(8,128)} %get-tuple-element.27.relaxed, f32[2,7,8,256]{3,2,1,0:T(8,128)S(1)} %copy-done, f32[14,128]{1,0:T(8,128)S(1)} %collective-permute-done.2.halo_a, ...), custom_call_target="tpu_custom_call", output_to_operand_aliasing={{}: (1, {})} | custom-call | flops 100000 | bytes 400000 | tf_op jit(solution)/shard_map/edge_rows/pallas_call | solution.py:490
  (28 shorter events, 0.8 us)
Async XLA Ops:
  1.8 20.9 %all-to-all-start = ((s32[128,1,128]{2,1,0:T(1,128)}), s32[128,1,128]{2,1,0:T(1,128)S(1)}, u32[]{:S(2)}, u32[]{:S(2)}) async-start(s32[128,1,128]{2,1,0:T(1,128)} %get-tuple-element.19), calls=%async_computation | async-start | bytes 131072 | tf_op jit(solution)/shard_map/all_to_all | solution.py:543
  14.2 5.7 %collective-permute-start = (f32[14,128]{1,0:T(8,128)S(1)}, f32[14,128]{1,0:T(8,128)S(1)}, u32[]{:S(2)}, u32[]{:S(2)}) collective-permute-start(f32[14,128]{1,0:T(8,128)S(1)} %select_n.28), channel_id=1, source_target_pairs={{0,1},{1,0},{2,3},{3,2},{4,5},{5,4},{6,7},{7,6},{8,9},{9,8},{10,11... | collective-permute-start | bytes 21512 | tf_op jit(solution)/shard_map/ppermute | solution.py:513
  15.4 4.6 %collective-permute-start.1 = (f32[14,128]{1,0:T(8,128)S(1)}, f32[14,128]{1,0:T(8,128)S(1)}, u32[]{:S(2)}, u32[]{:S(2)}) collective-permute-start(f32[14,128]{1,0:T(8,128)S(1)} %select_n.30), channel_id=1, source_target_pairs={{0,32},{1,2},{2,1},{3,4},{4,3},{5,6},{6,5},{7,8},{8,7},{9,10},{10,... | collective-permute-start | bytes 21512 | tf_op jit(solution)/shard_map/ppermute | solution.py:513
  20.0 16.3 %copy-start.5 = (f32[14,128]{1,0:T(8,128)}, f32[14,128]{1,0:T(8,128)S(1)}, u32[]{:S(2)}) copy-start(f32[14,128]{1,0:T(8,128)S(1)} %collective-permute-done.halo_a) | copy-start | bytes 21508
  20.0 16.3 %copy-start.6 = (f32[14,128]{1,0:T(8,128)}, f32[14,128]{1,0:T(8,128)S(1)}, u32[]{:S(2)}) copy-start(f32[14,128]{1,0:T(8,128)S(1)} %collective-permute-done.1.halo_b) | copy-start | bytes 21508
  22.8 0.6 copy-start.3
  27.7 6.8 %copy-start.4 = (f32[4,7,7]{2,0,1:T(4,128)S(1)}, f32[4,7,7]{2,0,1:T(4,128)}, u32[]{:S(2)}) copy-start(f32[4,7,7]{2,0,1:T(4,128)} %param.13) | copy-start | bytes 2356
  27.7 53.8 %all-to-all-start.1 = ((f32[128,56,128]{2,1,0:T(8,128)}), f32[128,56,128]{2,1,0:T(8,128)}, u32[]{:S(2)}, u32[]{:S(2)}) async-start(f32[128,56,128]{2,1,0:T(8,128)} %get-tuple-element.22), calls=%async_computation.1 | async-start | bytes 7340032 | tf_op jit(solution)/shard_map/all_to_all | solution.py:548
  34.5 1.8 %copy-start.2 = (f32[1,256,4,256]{3,2,1,0:T(4,128)S(1)}, f32[1,256,4,256]{3,2,1,0:T(4,128)}, u32[]{:S(2)}) copy-start(f32[1,256,4,256]{3,2,1,0:T(4,128)} %param.12) | copy-start | bytes 3145732
  81.5 14.7 %copy-start = (f32[2,7,8,256]{3,2,1,0:T(8,128)S(1)}, f32[2,7,8,256]{3,2,1,0:T(8,128)}, u32[]{:S(2)}) copy-start(f32[2,7,8,256]{3,2,1,0:T(8,128)} %get-tuple-element.28.operators) | copy-start | bytes 344068
  81.5 14.7 %copy-start.1 = (s32[1,128]{1,0:T(1,128)S(1)}, s32[1,128]{1,0:T(1,128)}, u32[]{:S(2)}) copy-start(s32[1,128]{1,0:T(1,128)} %fusion.5.place.place_in) | copy-start | bytes 1540
  91.6 2.1 %collective-permute-start.2 = (f32[14,128]{1,0:T(8,128)}, f32[14,128]{1,0:T(8,128)S(1)}, u32[]{:S(2)}, u32[]{:S(2)}) collective-permute-start(f32[14,128]{1,0:T(8,128)} %get-tuple-element.29), channel_id=1, source_target_pairs={{0,1},{1,0},{2,3},{3,2},{4,5},{5,4},{6,7},{7,6},{8,9},{9,8},{10,11... | collective-permute-start | bytes 21512 | tf_op jit(solution)/shard_map/ppermute | solution.py:513
  92.7 3.6 %collective-permute-start.3 = (f32[14,128]{1,0:T(8,128)}, f32[14,128]{1,0:T(8,128)S(1)}, u32[]{:S(2)}, u32[]{:S(2)}) collective-permute-start(f32[14,128]{1,0:T(8,128)} %get-tuple-element.30), channel_id=1, source_target_pairs={{0,32},{1,2},{2,1},{3,4},{4,3},{5,6},{6,5},{7,8},{8,7},{9,10},{10,... | collective-permute-start | bytes 21512 | tf_op jit(solution)/shard_map/ppermute | solution.py:513

commit v6 on v5

--- a/solution.py
+++ b/solution.py
@@ -110,24 +110,22 @@
     to_scalar.start()
     finish(copies[1:])
 
-    def rows_of(source, part):
-        def step(d, carry):
+    stores = [pltpu.make_async_copy(tables, tables_out, sems.at[3])]
+    stores[0].start()
+    to_scalar.wait()
+
+    def step(d, carry):
+        for part, source in enumerate((sent, table)):
             for k in range(2):
                 row = jnp.maximum(source[k, d] - 1, 0)
                 for h in range(2):
                     start = 28 * part + 14 * k + NV * h
                     message[d, start : start + NV, :] = flow[row, :, LANES * h : LANES * (h + 1)]
-            return carry
-
-        return step
-
-    lax.fori_loop(0, n, rows_of(sent, 0), 0, unroll=8)
-    to_scalar.wait()
-    stores = [pltpu.make_async_copy(tables, tables_out, sems.at[3])]
-    stores[0].start()
+        return carry
+
     size = n // CHUNKS
     for c in range(CHUNKS):
-        lax.fori_loop(c * size, (c + 1) * size, rows_of(table, 1), 0, unroll=8)
+        lax.fori_loop(c * size, (c + 1) * size, step, 0, unroll=4)
         part = pl.ds(c * size, size)
         stores.append(pltpu.make_async_copy(message.at[part], message_out.at[part], out_sems.at[c]))
         stores[-1].start()
@@ -280,6 +278,7 @@
     out,
     edge_a_out,
     edge_b_out,
+    rims_out,
     asked,
     sent,
     place,
@@ -431,6 +430,8 @@
     edges = [
         pltpu.make_async_copy(edge_a, edge_a_out, small_sems.at[4]),
         pltpu.make_async_copy(edge_b, edge_b_out, small_sems.at[5]),
+        pltpu.make_async_copy(done.at[1, :, 0:8, :], rims_out.at[0], small_sems.at[6]),
+        pltpu.make_async_copy(done.at[steps, :, rows - 8 : rows, :], rims_out.at[1], small_sems.at[7]),
     ]
     begin(edges)
     for c in range(steps):
@@ -444,11 +445,12 @@
     sums = VMEM((8 * (rows + 8), LANES), F32)
     padded = VMEM((2 * NV, rows + 8 * TILES + 16, LANES), F32)
     slab = (NV, rows, COLS)
+    edge = (2 * NV, LANES)
     return pl.pallas_call(
         finish_kernel,
         in_specs=[whole(pltpu.HBM)] * 7,
-        out_specs=[whole(pltpu.HBM)] * 3,
-        out_shape=[jax.ShapeDtypeStruct(s, F32) for s in (slab, (2 * NV, LANES), (2 * NV, LANES))],
+        out_specs=[whole(pltpu.HBM)] * 4,
+        out_shape=[jax.ShapeDtypeStruct(s, F32) for s in (slab, edge, edge, (2, NV, 8, COLS))],
         scratch_shapes=[pltpu.SMEM(a.shape, I32) for a in (asked, sent, place)]
         + [VMEM(turn.shape, BF16), VMEM(message.shape, F32)]
         + [sums] * 4
@@ -456,40 +458,35 @@
         + [padded] * 2
         + [VMEM((3, NV, 8, COLS), F32), VMEM((steps + 1, NV, 8 * TILES, COLS), F32)]
         + [VMEM((2 * NV, LANES), F32)] * 2
-        + [pltpu.SemaphoreType.DMA(s) for s in ((CHUNKS,), (2, steps), (steps,), (6,))],
+        + [pltpu.SemaphoreType.DMA(s) for s in ((CHUNKS,), (2, steps), (steps,), (8,))],
         compiler_params=params(61),
         cost_estimate=cost(45_000_000, 24_000_000),
         name="finish_sweeps",
     )(asked, sent, place, turn, message, packed, inv)
 
 
-def edge_kernel(place, relaxed, operators, halo_a, halo_b, out, ends, sems):
+def edge_kernel(place, relaxed, rims, operators, halo_a, halo_b, out, ends, sems):
     even = place[0, 0] == 1
-    tiles = (pl.ds(0, 8), pl.ds(out.shape[1] - 8, 8))
-    reads = [pltpu.make_async_copy(relaxed.at[:, tile, :], ends.at[g], sems.at[g]) for g, tile in enumerate(tiles)]
-    begin(reads)
-    changes = []
-    for g in range(2):
+    writes = []
+    for g, (first, row) in enumerate(((0, 0), (out.shape[1] - 8, 7))):
         use_a = even if g else jnp.logical_not(even)
-        total = None
+        change = None
         for j in range(NV):
             halves = [jnp.where(use_a, halo_a[n : n + 1, :], halo_b[n : n + 1, :]) for n in (2 * j, 2 * j + 1)]
             term = operators[g, j] * jnp.concatenate(halves, axis=1)
-            total = term if j == 0 else total + term
-        changes.append(total)
-    finish(reads)
-    for g, row in enumerate((0, 7)):
+            change = term if j == 0 else change + term
+        ends[g] = rims[g]
         for v in range(NV):
-            ends[g, v, row : row + 1, :] = ends[g, v, row : row + 1, :] - changes[g][v : v + 1, :]
-    writes = [pltpu.make_async_copy(ends.at[g], out.at[:, tile, :], sems.at[g]) for g, tile in enumerate(tiles)]
-    begin(writes)
+            ends[g, v, row : row + 1, :] = rims[g, v, row : row + 1, :] - change[v : v + 1, :]
+        writes.append(pltpu.make_async_copy(ends.at[g], out.at[:, pl.ds(first, 8), :], sems.at[g]))
+        writes[g].start()
     finish(writes)
 
 
-def edge_rows(place, relaxed, operators, halo_a, halo_b):
+def edge_rows(place, relaxed, rims, operators, halo_a, halo_b):
     return pl.pallas_call(
         edge_kernel,
-        in_specs=[SMEM, whole(pltpu.HBM)] + [whole()] * 3,
+        in_specs=[SMEM, whole(pltpu.HBM)] + [whole()] * 4,
         out_specs=whole(pltpu.HBM),
         out_shape=jax.ShapeDtypeStruct(relaxed.shape, F32),
         scratch_shapes=[VMEM((2, NV, 8, COLS), F32), pltpu.SemaphoreType.DMA((2,))],
@@ -497,7 +494,23 @@
         compiler_params=params(24),
         cost_estimate=cost(100_000, 400_000),
         name="edge_rows",
-    )(place, relaxed, operators, halo_a, halo_b)
+    )(place, relaxed, rims, operators, halo_a, halo_b)
+
+
+def hold_kernel(rims_in, rims):
+    rims[...] = rims_in[...]
+
+
+def hold(rims):
+    return pl.pallas_call(
+        hold_kernel,
+        in_specs=[whole()],
+        out_specs=whole(),
+        out_shape=jax.ShapeDtypeStruct(rims.shape, F32),
+        compiler_params=params(24),
+        cost_estimate=cost(100_000, 8_000_000),
+        name="hold",
+    )(rims)
 
 
 def exchange(edge_a, edge_b):
@@ -551,11 +564,11 @@
     mix = mixing(face_jacobian)
     jac = face_jacobian.reshape(-1)
     packed, blocks, operators = first_sum(place, jac, flow, right, coef, mix, halo_a, halo_b, inv)
-    relaxed, edge_a, edge_b = finish_sweeps(
+    relaxed, edge_a, edge_b, rims = finish_sweeps(
         asked, sent, place, turning(face_jacobian), message, packed, blocks
     )
     halo_a, halo_b = exchange(edge_a, edge_b)
-    relaxed = edge_rows(place, relaxed, operators, halo_a, halo_b)
+    relaxed = edge_rows(place, relaxed, hold(rims), operators, halo_a, halo_b)
     return jnp.transpose(relaxed, (1, 0, 2))[None]
 
 

time: 98.7 us -> 97.5 us (0.988)
  Pallas kernels: 33.5 us -> 32.3 us
    unnamed x17 -> x19, local copies, waits for them, and re-layouts: 1.82 us -> 2.72 us
  transfers between devices with their start and end apart: 6 -> 6, of which waited for: 4 -> 3; matrix products, arithmetic and copies ran while one was open for 10% -> 10% of each run, Pallas kernels for 15% -> 16%
where the time goes in v6:
time: 97.5 us; the launch traced here: 97.1 us
  Pallas kernels  32.3 us (33%)
  waiting for transfers between devices  31.9 us (33%)
  starting transfers between devices  21.4 us (22%)
  local copies, waits for them, and re-layouts  8.05 us (8%)
  other arithmetic  3.2 us (3%)
    all_to_all x1, waiting for transfers between devices, body(): lax.all_to_all(message, AXES, split_axis=0, concat_axis=0, tiled=True)  26.8 us
    pallas_call x1, Pallas kernels, first_sum(): pl.pallas_call(first_kernel, in_specs=[SMEM] * 2 + [whole()] * 4 + [whole...  15.2 us
    all_to_all x1, starting transfers between devices, body(): lax.all_to_all(asking, AXES, split_axis=0, concat_axis=0, tiled=True)  11.5 us
    pallas_call x1, Pallas kernels, finish_sweeps(): pl.pallas_call(finish_kernel, in_specs=[whole(pltpu.HBM)] * 7, out_specs=...  10.2 us
    all_to_all x1, starting transfers between devices, body(): lax.all_to_all(message, AXES, split_axis=0, concat_axis=0, tiled=True)  6.76 us
    squeeze x1, local copies, waits for them, and re-layouts, body(): flow = jnp.transpose(flow_state[0], (1, 0, 2))  3.92 us
    pallas_call x1, Pallas kernels, gather(): pl.pallas_call(gather_kernel, in_specs=[whole(pltpu.HBM)] * 3, out_specs=...  3.87 us
    all_to_all x1, waiting for transfers between devices, body(): lax.all_to_all(asking, AXES, split_axis=0, concat_axis=0, tiled=True)  2.75 us
  transfers between devices with their start and end apart: 6, of which 3 were waited for; matrix products, arithmetic and copies ran while one was open for 10% of the time, Pallas kernels for 16%

profile of v6, /device:TPU:1, one launch (start us, length us, event | category | flops | bytes accessed | tf_op | source)
XLA Modules:
  0.0 97.1 jit_solution(9284709103304066961)
XLA Ops:
  0.0 1.8 %slot_tables.1 = (s32[2,128]{1,0:T(2,128)}, s32[128,1,128]{2,1,0:T(1,128)}) custom-call(s32[1,128]{1,0:T(1,128)} %bitcast.36, s32[1,128]{1,0:T(1,128)} %bitcast.37, s32[1,128]{1,0:T(1,128)} %bitcast.38, s32[1,128]{1,0:T(1,128)} %bitcast.39), custom_call_target="tpu_custom_call" | custom-call | flops 4000000 | bytes 100000 | tf_op jit(solution)/shard_map/slot_tables/pallas_call | solution.py:72
  1.8 11.5 %all-to-all-start = ((s32[128,1,128]{2,1,0:T(1,128)}), s32[128,1,128]{2,1,0:T(1,128)S(1)}, u32[]{:S(2)}, u32[]{:S(2)}) async-start(s32[128,1,128]{2,1,0:T(1,128)} %get-tuple-element.20), calls=%async_computation | async-start | bytes 131072 | tf_op jit(solution)/shard_map/all_to_all | solution.py:556
  13.3 0.9 fusion.3
  14.2 1.1 %collective-permute-start = (f32[14,128]{1,0:T(8,128)S(1)}, f32[14,128]{1,0:T(8,128)S(1)}, u32[]{:S(2)}, u32[]{:S(2)}) collective-permute-start(f32[14,128]{1,0:T(8,128)S(1)} %select_n.28), channel_id=1, source_target_pairs={{0,1},{1,0},{2,3},{3,2},{4,5},{5,4},{6,7},{7,6},{8,9},{9,8},{10,11... | collective-permute-start | bytes 21512 | tf_op jit(solution)/shard_map/ppermute | solution.py:526
  15.4 0.7 collective-permute-start.1
  16.1 3.9 %copy.13.flow_in = f32[256,7,256]{2,1,0:T(8,128)} copy(f32[256,7,256]{2,0,1:T(8,128)} %bitcast.31) | data formatting | bytes 3670016 | tf_op jit(solution)/shard_map/squeeze | solution.py:546
  20.0 2.8 %all-to-all-done.asked_in = s32[128,1,128]{2,1,0:T(1,128)S(1)} async-done(((s32[128,1,128]{2,1,0:T(1,128)}), s32[128,1,128]{2,1,0:T(1,128)S(1)}, u32[]{:S(2)}, u32[]{:S(2)}) %all-to-all-start) | async-done | bytes 65568 | tf_op jit(solution)/shard_map/all_to_all | solution.py:556
  22.8 0.6 copy-done.4
  23.4 3.9 %gather.1 = (f32[128,56,128]{2,1,0:T(8,128)}, s32[2,128]{1,0:T(2,128)}) custom-call(s32[2,128]{1,0:T(2,128)} %get-tuple-element.19.sent_in, s32[128,1,128]{2,1,0:T(1,128)} %copy-done.4, f32[256,7,256]{2,1,0:T(8,128)} %copy.13.flow_in), custom_call_target="tpu_custom_call" | custom-call | flops 1000000 | bytes 6000000 | tf_op jit(solution)/shard_map/gather/pallas_call | solution.py:138
  27.3 6.8 %all-to-all-start.1 = ((f32[128,56,128]{2,1,0:T(8,128)}), f32[128,56,128]{2,1,0:T(8,128)}, u32[]{:S(2)}, u32[]{:S(2)}) async-start(f32[128,56,128]{2,1,0:T(8,128)} %get-tuple-element.23), calls=%async_computation.1 | async-start | bytes 7340032 | tf_op jit(solution)/shard_map/all_to_all | solution.py:561
  34.1 0.6 reshape.89.jac
  35.4 0.4 mul.55
  35.9 1.2 %copy.22 = f32[1,256,4,256]{3,1,2,0:T(8,128)} copy(f32[1,256,4,256]{3,2,1,0:T(4,128)S(1)} %copy-done.3) | data formatting | bytes 2097152 | tf_op args[3]
  37.1 0.5 fusion.5.place.place_in
  37.6 0.6 pad_maximum_fusion.1.mix
  38.3 0.7 pad_maximum_fusion.turn_in
  39.0 15.2 %first_sum.1 = (f32[8,18,32,256]{3,2,1,0:T(8,128)}, f32[8,7,7,32,256]{4,3,2,1,0:T(8,128)}, f32[2,7,8,256]{3,2,1,0:T(8,128)}) custom-call(s32[1,128]{1,0:T(1,128)} %fusion.5.place.place_in, f32[196]{0:T(256)} %reshape.89.jac, f32[7,256,256]{2,1,0:T(8,128)} %bitcast.32, bf16[2,56,224]{2,1,0:T(8,128)(2,1)} %pad_maximum_fusion.1.mix, f32[14,128]{1,0:T(8,128)} %copy-done.6, ...), custom_call_target="tpu_custom_call" | custom-call | flops 30000000 | bytes 40000000 | tf_op jit(solution)/shard_map/first_sum/pallas_call | solution.py:253
  54.3 26.8 %all-to-all-done.1.message_in = f32[128,56,128]{2,1,0:T(8,128)} async-done(((f32[128,56,128]{2,1,0:T(8,128)}), f32[128,56,128]{2,1,0:T(8,128)}, u32[]{:S(2)}, u32[]{:S(2)}) %all-to-all-start.1) | async-done | bytes 3670048 | tf_op jit(solution)/shard_map/all_to_all | solution.py:561
  81.1 10.2 %finish_sweeps.1 = (f32[7,256,256]{2,1,0:T(8,128)}, f32[14,128]{1,0:T(8,128)}, f32[14,128]{1,0:T(8,128)}, f32[2,7,8,256]{3,2,1,0:T(8,128)}) custom-call(s32[2,128]{1,0:T(2,128)} %get-tuple-element.22.asked_in, s32[2,128]{1,0:T(2,128)} %get-tuple-element.19.sent_in, s32[1,128]{1,0:T(1,128)} %fusion.5.place.place_in, ...), custom_call_target="tpu_custom_call" | custom-call | flops 45000000 | bytes 24000000 | tf_op jit(solution)/shard_map/finish_sweeps/pallas_call | solution.py:449
  91.3 1.0 %collective-permute-start.2 = (f32[14,128]{1,0:T(8,128)}, f32[14,128]{1,0:T(8,128)S(1)}, u32[]{:S(2)}, u32[]{:S(2)}) collective-permute-start(f32[14,128]{1,0:T(8,128)} %get-tuple-element.31), channel_id=1, source_target_pairs={{0,1},{1,0},{2,3},{3,2},{4,5},{5,4},{6,7},{7,6},{8,9},{9,8},{10,11... | collective-permute-start | bytes 21512 | tf_op jit(solution)/shard_map/ppermute | solution.py:526
  92.3 0.3 collective-permute-start.3
  92.6 0.9 copy-done
  93.5 2.3 %collective-permute-done.3.halo_b = f32[14,128]{1,0:T(8,128)S(1)} collective-permute-done((f32[14,128]{1,0:T(8,128)}, f32[14,128]{1,0:T(8,128)S(1)}, u32[]{:S(2)}, u32[]{:S(2)}) %collective-permute-start.3) | collective-permute-done | bytes 7200 | tf_op jit(solution)/shard_map/ppermute | solution.py:526
  95.8 1.2 %edge_rows.1 = f32[7,256,256]{2,1,0:T(8,128)} custom-call(s32[1,128]{1,0:T(1,128)S(1)} %copy-done.2, f32[7,256,256]{2,1,0:T(8,128)} %get-tuple-element.28.relaxed, f32[2,7,8,256]{3,2,1,0:T(8,128)S(1)} %hold.1.rims, f32[2,7,8,256]{3,2,1,0:T(8,128)S(1)} %copy-done.1, f32[14,128]{1,0:T(8,128)S(1)} %collective-permute-done.2.halo_a, ...), custom_call_target="tpu_custom_call", output_to_operand_aliasing={{}: (1, {})} | custom-call | flops 100000 | bytes 400000 | tf_op jit(solution)/shard_map/edge_rows/pallas_call | solution.py:487
  (31 shorter events, 0.8 us)
Async XLA Ops:
  1.8 20.9 %all-to-all-start = ((s32[128,1,128]{2,1,0:T(1,128)}), s32[128,1,128]{2,1,0:T(1,128)S(1)}, u32[]{:S(2)}, u32[]{:S(2)}) async-start(s32[128,1,128]{2,1,0:T(1,128)} %get-tuple-element.20), calls=%async_computation | async-start | bytes 131072 | tf_op jit(solution)/shard_map/all_to_all | solution.py:556
  14.2 5.8 %collective-permute-start = (f32[14,128]{1,0:T(8,128)S(1)}, f32[14,128]{1,0:T(8,128)S(1)}, u32[]{:S(2)}, u32[]{:S(2)}) collective-permute-start(f32[14,128]{1,0:T(8,128)S(1)} %select_n.28), channel_id=1, source_target_pairs={{0,1},{1,0},{2,3},{3,2},{4,5},{5,4},{6,7},{7,6},{8,9},{9,8},{10,11... | collective-permute-start | bytes 21512 | tf_op jit(solution)/shard_map/ppermute | solution.py:526
  15.4 4.6 %collective-permute-start.1 = (f32[14,128]{1,0:T(8,128)S(1)}, f32[14,128]{1,0:T(8,128)S(1)}, u32[]{:S(2)}, u32[]{:S(2)}) collective-permute-start(f32[14,128]{1,0:T(8,128)S(1)} %select_n.30), channel_id=1, source_target_pairs={{0,32},{1,2},{2,1},{3,4},{4,3},{5,6},{6,5},{7,8},{8,7},{9,10},{10,... | collective-permute-start | bytes 21512 | tf_op jit(solution)/shard_map/ppermute | solution.py:526
  20.0 15.8 %copy-start.6 = (f32[14,128]{1,0:T(8,128)}, f32[14,128]{1,0:T(8,128)S(1)}, u32[]{:S(2)}) copy-start(f32[14,128]{1,0:T(8,128)S(1)} %collective-permute-done.halo_a) | copy-start | bytes 21508
  20.0 15.8 %copy-start.7 = (f32[14,128]{1,0:T(8,128)}, f32[14,128]{1,0:T(8,128)S(1)}, u32[]{:S(2)}) copy-start(f32[14,128]{1,0:T(8,128)S(1)} %collective-permute-done.1.halo_b) | copy-start | bytes 21508
  22.8 0.6 copy-start.4
  27.3 6.8 %copy-start.5 = (f32[4,7,7]{2,0,1:T(4,128)S(1)}, f32[4,7,7]{2,0,1:T(4,128)}, u32[]{:S(2)}) copy-start(f32[4,7,7]{2,0,1:T(4,128)} %param.13) | copy-start | bytes 2356
  27.3 53.8 %all-to-all-start.1 = ((f32[128,56,128]{2,1,0:T(8,128)}), f32[128,56,128]{2,1,0:T(8,128)}, u32[]{:S(2)}, u32[]{:S(2)}) async-start(f32[128,56,128]{2,1,0:T(8,128)} %get-tuple-element.23), calls=%async_computation.1 | async-start | bytes 7340032 | tf_op jit(solution)/shard_map/all_to_all | solution.py:561
  34.1 1.8 %copy-start.3 = (f32[1,256,4,256]{3,2,1,0:T(4,128)S(1)}, f32[1,256,4,256]{3,2,1,0:T(4,128)}, u32[]{:S(2)}) copy-start(f32[1,256,4,256]{3,2,1,0:T(4,128)} %param.12) | copy-start | bytes 3145732
  81.1 14.7 %copy-start.1 = (f32[2,7,8,256]{3,2,1,0:T(8,128)S(1)}, f32[2,7,8,256]{3,2,1,0:T(8,128)}, u32[]{:S(2)}) copy-start(f32[2,7,8,256]{3,2,1,0:T(8,128)} %get-tuple-element.30.operators) | copy-start | bytes 344068
  81.1 14.7 %copy-start.2 = (s32[1,128]{1,0:T(1,128)S(1)}, s32[1,128]{1,0:T(1,128)}, u32[]{:S(2)}) copy-start(s32[1,128]{1,0:T(1,128)} %fusion.5.place.place_in) | copy-start | bytes 1540
  91.3 2.2 %collective-permute-start.2 = (f32[14,128]{1,0:T(8,128)}, f32[14,128]{1,0:T(8,128)S(1)}, u32[]{:S(2)}, u32[]{:S(2)}) collective-permute-start(f32[14,128]{1,0:T(8,128)} %get-tuple-element.31), channel_id=1, source_target_pairs={{0,1},{1,0},{2,3},{3,2},{4,5},{5,4},{6,7},{7,6},{8,9},{9,8},{10,11... | collective-permute-start | bytes 21512 | tf_op jit(solution)/shard_map/ppermute | solution.py:526
  92.3 3.6 %collective-permute-start.3 = (f32[14,128]{1,0:T(8,128)}, f32[14,128]{1,0:T(8,128)S(1)}, u32[]{:S(2)}, u32[]{:S(2)}) collective-permute-start(f32[14,128]{1,0:T(8,128)} %get-tuple-element.32), channel_id=1, source_target_pairs={{0,32},{1,2},{2,1},{3,4},{4,3},{5,6},{6,5},{7,8},{8,7},{9,10},{10,... | collective-permute-start | bytes 21512 | tf_op jit(solution)/shard_map/ppermute | solution.py:526
  92.6 0.9 copy-start

commit v7 on v6

--- a/solution.py
+++ b/solution.py
@@ -348,8 +348,8 @@
     finish(small)
     for c in range(CHUNKS):
         load(c).wait()
-        if c in (2, 6):
-            begin(fetch(1 if c == 2 else 2))
+        if c in (0, 4):
+            begin(fetch(1 if c == 0 else 2))
         lax.fori_loop(c * count, (c + 1) * count, scatter, 0, unroll=4)
 
     lane = lax.broadcasted_iota(I32, (8, COLS), 1)

time: 97.5 us -> 97.2 us (level)
  no operation moved by 1% of the time
where the time goes in v7:
time: 97.2 us; the launch traced here: 96.8 us
  Pallas kernels  32 us (33%)
  waiting for transfers between devices  32 us (33%)
  starting transfers between devices  21.4 us (22%)
  local copies, waits for them, and re-layouts  8.05 us (8%)
  other arithmetic  3.2 us (3%)
    all_to_all x1, waiting for transfers between devices, body(): lax.all_to_all(message, AXES, split_axis=0, concat_axis=0, tiled=True)  26.8 us
    pallas_call x1, Pallas kernels, first_sum(): pl.pallas_call(first_kernel, in_specs=[SMEM] * 2 + [whole()] * 4 + [whole...  15.2 us
    all_to_all x1, starting transfers between devices, body(): lax.all_to_all(asking, AXES, split_axis=0, concat_axis=0, tiled=True)  11.5 us
    pallas_call x1, Pallas kernels, finish_sweeps(): pl.pallas_call(finish_kernel, in_specs=[whole(pltpu.HBM)] * 7, out_specs=...  9.84 us
    all_to_all x1, starting transfers between devices, body(): lax.all_to_all(message, AXES, split_axis=0, concat_axis=0, tiled=True)  6.76 us
    squeeze x1, local copies, waits for them, and re-layouts, body(): flow = jnp.transpose(flow_state[0], (1, 0, 2))  3.92 us
    pallas_call x1, Pallas kernels, gather(): pl.pallas_call(gather_kernel, in_specs=[whole(pltpu.HBM)] * 3, out_specs=...  3.87 us
    all_to_all x1, waiting for transfers between devices, body(): lax.all_to_all(asking, AXES, split_axis=0, concat_axis=0, tiled=True)  2.75 us
  transfers between devices with their start and end apart: 6, of which 3 were waited for; matrix products, arithmetic and copies ran while one was open for 10% of the time, Pallas kernels for 16%

profile of v7, /device:TPU:1, one launch (start us, length us, event | category | flops | bytes accessed | tf_op | source)
XLA Modules:
  0.0 96.8 jit_solution(5100855800901191983)
XLA Ops:
  0.0 1.8 %slot_tables.1 = (s32[2,128]{1,0:T(2,128)}, s32[128,1,128]{2,1,0:T(1,128)}) custom-call(s32[1,128]{1,0:T(1,128)} %bitcast.36, s32[1,128]{1,0:T(1,128)} %bitcast.37, s32[1,128]{1,0:T(1,128)} %bitcast.38, s32[1,128]{1,0:T(1,128)} %bitcast.39), custom_call_target="tpu_custom_call" | custom-call | flops 4000000 | bytes 100000 | tf_op jit(solution)/shard_map/slot_tables/pallas_call | solution.py:72
  1.8 11.5 %all-to-all-start = ((s32[128,1,128]{2,1,0:T(1,128)}), s32[128,1,128]{2,1,0:T(1,128)S(1)}, u32[]{:S(2)}, u32[]{:S(2)}) async-start(s32[128,1,128]{2,1,0:T(1,128)} %get-tuple-element.20), calls=%async_computation | async-start | bytes 131072 | tf_op jit(solution)/shard_map/all_to_all | solution.py:556
  13.3 0.9 fusion.3
  14.2 1.1 %collective-permute-start = (f32[14,128]{1,0:T(8,128)S(1)}, f32[14,128]{1,0:T(8,128)S(1)}, u32[]{:S(2)}, u32[]{:S(2)}) collective-permute-start(f32[14,128]{1,0:T(8,128)S(1)} %select_n.28), channel_id=1, source_target_pairs={{0,1},{1,0},{2,3},{3,2},{4,5},{5,4},{6,7},{7,6},{8,9},{9,8},{10,11... | collective-permute-start | bytes 21512 | tf_op jit(solution)/shard_map/ppermute | solution.py:526
  15.4 0.7 collective-permute-start.1
  16.1 3.9 %copy.13.flow_in = f32[256,7,256]{2,1,0:T(8,128)} copy(f32[256,7,256]{2,0,1:T(8,128)} %bitcast.31) | data formatting | bytes 3670016 | tf_op jit(solution)/shard_map/squeeze | solution.py:546
  20.0 2.8 %all-to-all-done.asked_in = s32[128,1,128]{2,1,0:T(1,128)S(1)} async-done(((s32[128,1,128]{2,1,0:T(1,128)}), s32[128,1,128]{2,1,0:T(1,128)S(1)}, u32[]{:S(2)}, u32[]{:S(2)}) %all-to-all-start) | async-done | bytes 65568 | tf_op jit(solution)/shard_map/all_to_all | solution.py:556
  22.8 0.6 copy-done.4
  23.4 3.9 %gather.1 = (f32[128,56,128]{2,1,0:T(8,128)}, s32[2,128]{1,0:T(2,128)}) custom-call(s32[2,128]{1,0:T(2,128)} %get-tuple-element.19.sent_in, s32[128,1,128]{2,1,0:T(1,128)} %copy-done.4, f32[256,7,256]{2,1,0:T(8,128)} %copy.13.flow_in), custom_call_target="tpu_custom_call" | custom-call | flops 1000000 | bytes 6000000 | tf_op jit(solution)/shard_map/gather/pallas_call | solution.py:138
  27.3 6.8 %all-to-all-start.1 = ((f32[128,56,128]{2,1,0:T(8,128)}), f32[128,56,128]{2,1,0:T(8,128)}, u32[]{:S(2)}, u32[]{:S(2)}) async-start(f32[128,56,128]{2,1,0:T(8,128)} %get-tuple-element.23), calls=%async_computation.1 | async-start | bytes 7340032 | tf_op jit(solution)/shard_map/all_to_all | solution.py:561
  34.1 0.6 reshape.89.jac
  35.0 0.3 mul.50
  35.4 0.4 mul.55
  35.9 1.2 %copy.22 = f32[1,256,4,256]{3,1,2,0:T(8,128)} copy(f32[1,256,4,256]{3,2,1,0:T(4,128)S(1)} %copy-done.3) | data formatting | bytes 2097152 | tf_op args[3]
  37.1 0.5 fusion.5.place.place_in
  37.6 0.6 pad_maximum_fusion.1.mix
  38.3 0.7 pad_maximum_fusion.turn_in
  39.0 15.2 %first_sum.1 = (f32[8,18,32,256]{3,2,1,0:T(8,128)}, f32[8,7,7,32,256]{4,3,2,1,0:T(8,128)}, f32[2,7,8,256]{3,2,1,0:T(8,128)}) custom-call(s32[1,128]{1,0:T(1,128)} %fusion.5.place.place_in, f32[196]{0:T(256)} %reshape.89.jac, f32[7,256,256]{2,1,0:T(8,128)} %bitcast.32, bf16[2,56,224]{2,1,0:T(8,128)(2,1)} %pad_maximum_fusion.1.mix, f32[14,128]{1,0:T(8,128)} %copy-done.6, ...), custom_call_target="tpu_custom_call" | custom-call | flops 30000000 | bytes 40000000 | tf_op jit(solution)/shard_map/first_sum/pallas_call | solution.py:253
  54.3 26.8 %all-to-all-done.1.message_in = f32[128,56,128]{2,1,0:T(8,128)} async-done(((f32[128,56,128]{2,1,0:T(8,128)}), f32[128,56,128]{2,1,0:T(8,128)}, u32[]{:S(2)}, u32[]{:S(2)}) %all-to-all-start.1) | async-done | bytes 3670048 | tf_op jit(solution)/shard_map/all_to_all | solution.py:561
  81.1 9.8 %finish_sweeps.1 = (f32[7,256,256]{2,1,0:T(8,128)}, f32[14,128]{1,0:T(8,128)}, f32[14,128]{1,0:T(8,128)}, f32[2,7,8,256]{3,2,1,0:T(8,128)}) custom-call(s32[2,128]{1,0:T(2,128)} %get-tuple-element.22.asked_in, s32[2,128]{1,0:T(2,128)} %get-tuple-element.19.sent_in, s32[1,128]{1,0:T(1,128)} %fusion.5.place.place_in, ...), custom_call_target="tpu_custom_call" | custom-call | flops 45000000 | bytes 24000000 | tf_op jit(solution)/shard_map/finish_sweeps/pallas_call | solution.py:449
  90.9 1.0 %collective-permute-start.2 = (f32[14,128]{1,0:T(8,128)}, f32[14,128]{1,0:T(8,128)S(1)}, u32[]{:S(2)}, u32[]{:S(2)}) collective-permute-start(f32[14,128]{1,0:T(8,128)} %get-tuple-element.31), channel_id=1, source_target_pairs={{0,1},{1,0},{2,3},{3,2},{4,5},{5,4},{6,7},{7,6},{8,9},{9,8},{10,11... | collective-permute-start | bytes 21512 | tf_op jit(solution)/shard_map/ppermute | solution.py:526
  92.2 0.9 copy-done
  93.2 2.4 %collective-permute-done.3.halo_b = f32[14,128]{1,0:T(8,128)S(1)} collective-permute-done((f32[14,128]{1,0:T(8,128)}, f32[14,128]{1,0:T(8,128)S(1)}, u32[]{:S(2)}, u32[]{:S(2)}) %collective-permute-start.3) | collective-permute-done | bytes 7200 | tf_op jit(solution)/shard_map/ppermute | solution.py:526
  95.6 1.2 %edge_rows.1 = f32[7,256,256]{2,1,0:T(8,128)} custom-call(s32[1,128]{1,0:T(1,128)S(1)} %copy-done.2, f32[7,256,256]{2,1,0:T(8,128)} %get-tuple-element.28.relaxed, f32[2,7,8,256]{3,2,1,0:T(8,128)S(1)} %hold.1.rims, f32[2,7,8,256]{3,2,1,0:T(8,128)S(1)} %copy-done.1, f32[14,128]{1,0:T(8,128)S(1)} %collective-permute-done.2.halo_a, ...), custom_call_target="tpu_custom_call", output_to_operand_aliasing={{}: (1, {})} | custom-call | flops 100000 | bytes 400000 | tf_op jit(solution)/shard_map/edge_rows/pallas_call | solution.py:487
  (31 shorter events, 0.8 us)
Async XLA Ops:
  1.8 20.9 %all-to-all-start = ((s32[128,1,128]{2,1,0:T(1,128)}), s32[128,1,128]{2,1,0:T(1,128)S(1)}, u32[]{:S(2)}, u32[]{:S(2)}) async-start(s32[128,1,128]{2,1,0:T(1,128)} %get-tuple-element.20), calls=%async_computation | async-start | bytes 131072 | tf_op jit(solution)/shard_map/all_to_all | solution.py:556
  14.2 5.8 %collective-permute-start = (f32[14,128]{1,0:T(8,128)S(1)}, f32[14,128]{1,0:T(8,128)S(1)}, u32[]{:S(2)}, u32[]{:S(2)}) collective-permute-start(f32[14,128]{1,0:T(8,128)S(1)} %select_n.28), channel_id=1, source_target_pairs={{0,1},{1,0},{2,3},{3,2},{4,5},{5,4},{6,7},{7,6},{8,9},{9,8},{10,11... | collective-permute-start | bytes 21512 | tf_op jit(solution)/shard_map/ppermute | solution.py:526
  15.4 4.6 %collective-permute-start.1 = (f32[14,128]{1,0:T(8,128)S(1)}, f32[14,128]{1,0:T(8,128)S(1)}, u32[]{:S(2)}, u32[]{:S(2)}) collective-permute-start(f32[14,128]{1,0:T(8,128)S(1)} %select_n.30), channel_id=1, source_target_pairs={{0,32},{1,2},{2,1},{3,4},{4,3},{5,6},{6,5},{7,8},{8,7},{9,10},{10,... | collective-permute-start | bytes 21512 | tf_op jit(solution)/shard_map/ppermute | solution.py:526
  20.0 15.8 %copy-start.6 = (f32[14,128]{1,0:T(8,128)}, f32[14,128]{1,0:T(8,128)S(1)}, u32[]{:S(2)}) copy-start(f32[14,128]{1,0:T(8,128)S(1)} %collective-permute-done.halo_a) | copy-start | bytes 21508
  20.0 15.8 %copy-start.7 = (f32[14,128]{1,0:T(8,128)}, f32[14,128]{1,0:T(8,128)S(1)}, u32[]{:S(2)}) copy-start(f32[14,128]{1,0:T(8,128)S(1)} %collective-permute-done.1.halo_b) | copy-start | bytes 21508
  22.8 0.6 copy-start.4
  27.3 6.8 %copy-start.5 = (f32[4,7,7]{2,0,1:T(4,128)S(1)}, f32[4,7,7]{2,0,1:T(4,128)}, u32[]{:S(2)}) copy-start(f32[4,7,7]{2,0,1:T(4,128)} %param.13) | copy-start | bytes 2356
  27.3 53.8 %all-to-all-start.1 = ((f32[128,56,128]{2,1,0:T(8,128)}), f32[128,56,128]{2,1,0:T(8,128)}, u32[]{:S(2)}, u32[]{:S(2)}) async-start(f32[128,56,128]{2,1,0:T(8,128)} %get-tuple-element.23), calls=%async_computation.1 | async-start | bytes 7340032 | tf_op jit(solution)/shard_map/all_to_all | solution.py:561
  34.1 1.8 %copy-start.3 = (f32[1,256,4,256]{3,2,1,0:T(4,128)S(1)}, f32[1,256,4,256]{3,2,1,0:T(4,128)}, u32[]{:S(2)}) copy-start(f32[1,256,4,256]{3,2,1,0:T(4,128)} %param.12) | copy-start | bytes 3145732
  81.1 14.5 %copy-start.1 = (f32[2,7,8,256]{3,2,1,0:T(8,128)S(1)}, f32[2,7,8,256]{3,2,1,0:T(8,128)}, u32[]{:S(2)}) copy-start(f32[2,7,8,256]{3,2,1,0:T(8,128)} %get-tuple-element.30.operators) | copy-start | bytes 344068
  81.1 14.5 %copy-start.2 = (s32[1,128]{1,0:T(1,128)S(1)}, s32[1,128]{1,0:T(1,128)}, u32[]{:S(2)}) copy-start(s32[1,128]{1,0:T(1,128)} %fusion.5.place.place_in) | copy-start | bytes 1540
  90.9 2.2 %collective-permute-start.2 = (f32[14,128]{1,0:T(8,128)}, f32[14,128]{1,0:T(8,128)S(1)}, u32[]{:S(2)}, u32[]{:S(2)}) collective-permute-start(f32[14,128]{1,0:T(8,128)} %get-tuple-element.31), channel_id=1, source_target_pairs={{0,1},{1,0},{2,3},{3,2},{4,5},{5,4},{6,7},{7,6},{8,9},{9,8},{10,11... | collective-permute-start | bytes 21512 | tf_op jit(solution)/shard_map/ppermute | solution.py:526
  92.0 3.6 %collective-permute-start.3 = (f32[14,128]{1,0:T(8,128)}, f32[14,128]{1,0:T(8,128)S(1)}, u32[]{:S(2)}, u32[]{:S(2)}) collective-permute-start(f32[14,128]{1,0:T(8,128)} %get-tuple-element.32), channel_id=1, source_target_pairs={{0,32},{1,2},{2,1},{3,4},{4,3},{5,6},{6,5},{7,8},{8,7},{9,10},{10,... | collective-permute-start | bytes 21512 | tf_op jit(solution)/shard_map/ppermute | solution.py:526
  92.2 0.9 copy-start
